TPU v7x, 32 devices: a whole 2x2x4 slice. The times are simulated.
32 devices in a mesh: lat: 4 (over y, x), lon: 8 (over z, core).
Axes of the slice: x: 2, y: 2, z: 4, core: 2. Of those that a mesh axis runs over, the one named last changes fastest.
Arguments:
- state: float32 [8, 60, 32, 1024], P(None, None, 'lat', 'lon'), may hold values from -6 to 6
- surface: bfloat16 [76, 32, 1024], P(None, 'lat', 'lon'), may hold values from -6 to 6
- layer_one: bfloat16 [556, 768], replicated, may hold values from -0.25 to 0.25
- layer_two: bfloat16 [768, 640], replicated, may hold values from -0.21875 to 0.21875
- layer_three: bfloat16 [640, 512], replicated, may hold values from -0.25 to 0.25
- layer_four: bfloat16 [512, 640], replicated, may hold values from -0.25 to 0.25
- layer_five: bfloat16 [640, 368], replicated, may hold values from -0.25 to 0.25
- lit_columns: int32 [4, 8, 1024], P('lat', 'lon'), may hold values from 0 to 1024, as said below
- row_offset: int32 [32], P('lat'), may hold values from 0 to 383
Outputs:
- new_state: float32 [8, 60, 32, 1024], P(None, None, 'lat', 'lon')
- surface_flux: bfloat16 [8, 32, 1024], P(None, 'lat', 'lon')
Inputs may be any that keep to these rules, and one draw needn't show every extreme that they name: `lit_columns`: in each tile's list the first entries are distinct column numbers in rising order and the rest equal 1024. A tile and the tile 8/2 further along the longitude cycle, in the same latitude tile, list 1024 columns together at most, and some such pair lists exactly 1024 in every draw.
All inputs are finite; a program needn't handle non-finite values.
Results may differ from a plain program's by a relative error of at most 0.015.
Values may be sent and summed in bfloat16 or wider, within the bound.
No kernel may reach another device: no remote copies, remote signals or barrier semaphores. Data moves between devices by JAX's collectives and lax.ppermute only.
A program may use at most 64 MiB of HBM per device.

v0:
```python
import jax
import jax.numpy as jnp
from jax import lax
from jax.sharding import PartitionSpec as P

SUBSTEPS = 4
REACH = 2


SOUND_COURANT = 0.6
PHYSICS_STEP = 0.5
LEAK_SLOPE = 0.15


def shifted(value, axis, steps):
    count = lax.axis_size(axis)
    pairs = [(source, (source + steps) % count) for source in range(count)]
    return lax.ppermute(value, axis, pairs)


def passed_along(block, axis, distance):
    devices = range(lax.axis_size(axis))
    route = [(i - distance, i) for i in devices if i - distance in devices]
    return lax.ppermute(block, axis, route)


def run_network(inputs, layers):
    hidden = inputs
    for weight in layers[:-1]:
        summed = jnp.dot(hidden, weight, preferred_element_type=jnp.float32)
        hidden = jnp.maximum(summed, LEAK_SLOPE * summed).astype(jnp.bfloat16)
    summed = jnp.dot(hidden, layers[-1], preferred_element_type=jnp.float32)
    return summed.astype(jnp.bfloat16)


def fetch_tracers(scalars):
    return [scalars] + [
        shifted(scalars.astype(jnp.bfloat16), "lon", distance).astype(scalars.dtype)
        for distance in range(1, REACH + 2)
    ]


def shift_rows(extended, start, tile_cols):
    moved = extended
    for bit_place in range(tile_cols.bit_length()):
        step_size = 1 << bit_place
        stepped = jnp.concatenate(
            [moved[..., step_size:], jnp.zeros(moved.shape[:-1] + (step_size,), moved.dtype)],
            axis=-1,
        )
        chosen = start >> bit_place & 1 == 1
        moved = jnp.where(chosen[None, None, :, None], stepped, moved)
    return moved[..., :tile_cols]


def upwind_pair(tiles, block_shift, cell_shift, tile_cols):
    left_tile = jnp.zeros(tiles[0].shape, jnp.float32)
    right_tile = jnp.zeros(tiles[0].shape, jnp.float32)
    for distance, piece in enumerate(tiles):
        right_tile = right_tile + jnp.where(
            (block_shift == distance)[None, None, :, None], piece, 0.0
        )
        left_tile = left_tile + jnp.where(
            (block_shift + 1 == distance)[None, None, :, None], piece, 0.0
        )
    extended = jnp.concatenate([left_tile, right_tile], axis=3)
    near_value = shift_rows(extended, tile_cols - cell_shift, tile_cols)
    far_value = shift_rows(extended, tile_cols - cell_shift - 1, tile_cols)
    return (near_value, far_value)


def on_device(
    state,
    surface,
    layer_one,
    layer_two,
    layer_three,
    layer_four,
    layer_five,
    lit_columns,
    row_offset,
):
    field_count, levels, tile_rows, tile_cols = state.shape
    columns = tile_rows * tile_cols
    block_shift = row_offset // tile_cols
    cell_shift = row_offset % tile_cols
    zonal_wind, merid_wind, pressure = (state[0], state[1], state[2])
    lat_rows = lax.axis_index("lat") * tile_rows + lax.iota(jnp.int32, tile_rows)
    north_open = (lat_rows < tile_rows * lax.axis_size("lat") - 1).astype(jnp.float32)[
        None, :, None
    ]
    for substep in range(SUBSTEPS):
        east_col = shifted(pressure[:, :, 0], "lon", -1)
        north_row = passed_along(pressure[:, 0, :], "lat", -1)
        zonal_wind = zonal_wind - SOUND_COURANT * (
            jnp.concatenate([pressure[:, :, 1:], east_col[:, :, None]], axis=2) - pressure
        )
        merid_wind = (
            merid_wind
            - SOUND_COURANT
            * (jnp.concatenate([pressure[:, 1:, :], north_row[:, None, :]], axis=1) - pressure)
        ) * north_open
        west_col = shifted(zonal_wind[:, :, -1], "lon", 1)
        south_row = passed_along(merid_wind[:, -1, :], "lat", 1)
        zonal_diff = zonal_wind - jnp.concatenate(
            [west_col[:, :, None], zonal_wind[:, :, :-1]], axis=2
        )
        merid_diff = merid_wind - jnp.concatenate(
            [south_row[:, None, :], merid_wind[:, :-1, :]], axis=1
        )
        pressure = pressure - SOUND_COURANT * (zonal_diff + merid_diff)
    dynamics = jnp.stack([zonal_wind, merid_wind, pressure]).reshape(3 * levels, columns)
    features = jnp.concatenate(
        [
            dynamics,
            state[3:].reshape(5 * levels, columns),
            surface.astype(jnp.float32).reshape(surface.shape[0], columns),
        ],
        axis=0,
    ).astype(jnp.bfloat16)
    feature_rows = features.T
    slots = lit_columns.reshape(columns)
    picked = jnp.take(feature_rows, jnp.minimum(slots, columns - 1), axis=0)
    layers = (layer_one, layer_two, layer_three, layer_four, layer_five)
    results = run_network(picked, layers)
    placed_rows = (
        jnp.zeros((columns + 1, results.shape[1]), jnp.bfloat16).at[slots].set(results)[:columns]
    )
    placed = placed_rows.T
    flux_count = results.shape[1] - 6 * levels
    surface_flux = placed[6 * levels :].reshape(flux_count, tile_rows, tile_cols)
    tendency = placed[: 6 * levels].astype(jnp.float32).reshape(6, levels, tile_rows, tile_cols)
    updated_zonal = zonal_wind + PHYSICS_STEP * tendency[0]
    updated_merid = merid_wind + PHYSICS_STEP * tendency[1]
    fraction = 0.5 + 0.45 * jnp.tanh(zonal_wind)
    fraction_west = jnp.concatenate(
        [0.5 + 0.45 * jnp.tanh(west_col[:, :, None]), fraction[:, :, :-1]], axis=2
    )
    scalars = state[3:] + PHYSICS_STEP * jnp.concatenate(
        [tendency[2:], jnp.zeros_like(tendency[:1])], axis=0
    )
    near_value, far_value = upwind_pair(fetch_tracers(scalars), block_shift, cell_shift, tile_cols)
    advected = (1.0 - fraction)[None] * near_value + fraction_west[None] * far_value
    new_state = jnp.concatenate(
        [jnp.stack([updated_zonal, updated_merid, pressure]), advected], axis=0
    )
    return (new_state, surface_flux)


def solution(mesh):
    in_specs = (
        P(None, None, "lat", "lon"),
        P(None, "lat", "lon"),
        P(),
        P(),
        P(),
        P(),
        P(),
        P("lat", "lon", None),
        P("lat"),
    )
    out_specs = (P(None, None, "lat", "lon"), P(None, "lat", "lon"))
    return jax.shard_map(
        on_device, mesh=mesh, in_specs=in_specs, out_specs=out_specs, check_vma=False
    )
```

profile of v0, /device:TPU:0, one launch (start us, length us, event | category | flops | bytes accessed | tf_op | source)
XLA Modules:
  0.0 200.1 jit_solution(13657652714473323403)
XLA Ops:
  0.7 1.1 slice_bitcast_fusion.3
  1.9 4.5 %collective-permute-start = (f32[60,8]{0,1:T(8,128)S(1)}, f32[60,8]{0,1:T(8,128)S(1)}, u32[]{:S(2)}, u32[]{:S(2)}) collective-permute-start(f32[60,8]{0,1:T(8,128)S(1)} %bitcast.191), channel_id=1, source_target_pairs={{0,7},{1,0},{2,1},{3,2},{4,3},{5,4},{6,5},{7,6},{8,15},{9,8},{10,9... | collective-permute-start | bytes 5768 | tf_op jit(solution)/shard_map/ppermute | solution.py:18
  6.5 1.3 collective-permute-start.2
  8.5 1.3 compare_select_fusion
  11.5 1.2 and_compare_fusion.15
  12.8 1.3 and_compare_fusion.7
  17.7 1.1 pad.94
  19.8 2.2 %copy.550 = bf16[300,1024]{0,1:T(8,128)(2,1)} copy(bf16[300,1024]{1,0:T(8,128)(2,1)} %bitcast.150) | data formatting | bytes 1228800 | tf_op jit(solution)/shard_map/reshape | solution.py:116
  23.8 1.3 fusion.49
  26.6 4.5 %collective-permute-start.3 = (f32[60,128]{1,0:T(8,128)}, f32[60,128]{1,0:T(8,128)S(1)}, u32[]{:S(2)}, u32[]{:S(2)}) collective-permute-start(f32[60,128]{1,0:T(8,128)} %bitcast.133), channel_id=1, source_target_pairs={{0,8},{8,16},{16,24},{1,9},{9,17},{17,25},{2,10},{10,18},{18,26},{... | collective-permute-start | bytes 92168 | tf_op jit(solution)/shard_map/ppermute | solution.py:24
  33.9 4.0 %collective-permute-done.1 = f32[60,8]{0,1:T(8,128)S(1)} collective-permute-done((f32[60,8]{0,1:T(8,128)S(1)}, f32[60,8]{0,1:T(8,128)S(1)}, u32[]{:S(2)}, u32[]{:S(2)}) %collective-permute-start.1) | collective-permute-done | bytes 1952 | tf_op jit(solution)/shard_map/ppermute | solution.py:18
  39.7 1.5 fusion.46
  43.7 1.3 collective-permute-start.6
  45.9 2.8 %fusion.51 = (f32[1,60,8,128]{3,2,1,0:T(8,128)}, f32[1,60,8,128]{3,2,1,0:T(8,128)}, f32[1,60,8,128]{3,2,1,0:T(8,128)}) fusion(f32[1,60,8,1]{3,2,1,0:T(8,128)} %copy.518, f32[1,60,8,127]{3,2,1,0:T(8,128)} %get-tuple-element.72, f32[1,60,7,128]{3,2,1,0:T(8,128)} %get-tuple-element.70, f32[1,60,1,128]{3,2,1,0:T(1,128)} %copy.521, ...), kind=kLoop, calls=%fused_computation.84 | loop fusion | flops 1228800 | bytes 2703392 | tf_op jit(solution)/shard_map/sub | solution.py:95
  48.9 1.2 collective-permute-done.6
  50.1 1.3 fusion.65
  52.2 4.7 %collective-permute-start.7 = (f32[60,128]{1,0:T(8,128)S(1)}, f32[60,128]{1,0:T(8,128)S(1)}, u32[]{:S(2)}, u32[]{:S(2)}) collective-permute-start(f32[60,128]{1,0:T(8,128)S(1)} %bitcast.171), channel_id=1, source_target_pairs={{0,8},{8,16},{16,24},{1,9},{9,17},{17,25},{2,10},{10,18},{18,26},{... | collective-permute-start | bytes 92168 | tf_op jit(solution)/shard_map/ppermute | solution.py:24
  58.5 3.5 %collective-permute-done.5 = f32[60,8]{0,1:T(8,128)S(1)} collective-permute-done((f32[60,8]{0,1:T(8,128)S(1)}, f32[60,8]{0,1:T(8,128)S(1)}, u32[]{:S(2)}, u32[]{:S(2)}) %collective-permute-start.5) | collective-permute-done | bytes 1952 | tf_op jit(solution)/shard_map/ppermute | solution.py:18
  63.6 1.3 collective-permute-start.10
  67.4 2.1 %collective-permute-done.10 = f32[60,128]{1,0:T(8,128)S(1)} collective-permute-done((f32[60,128]{1,0:T(8,128)S(1)}, f32[60,128]{1,0:T(8,128)S(1)}, u32[]{:S(2)}, u32[]{:S(2)}) %collective-permute-start.10) | collective-permute-done | bytes 30752 | tf_op jit(solution)/shard_map/ppermute | solution.py:24
  70.5 4.7 %collective-permute-start.11 = (f32[60,128]{1,0:T(8,128)S(1)}, f32[60,128]{1,0:T(8,128)S(1)}, u32[]{:S(2)}, u32[]{:S(2)}) collective-permute-start(f32[60,128]{1,0:T(8,128)S(1)} %bitcast.172), channel_id=1, source_target_pairs={{0,8},{8,16},{16,24},{1,9},{9,17},{17,25},{2,10},{10,18},{18,26},{... | collective-permute-start | bytes 92168 | tf_op jit(solution)/shard_map/ppermute | solution.py:24
  76.3 4.1 %collective-permute-done.9 = f32[60,8]{0,1:T(8,128)S(1)} collective-permute-done((f32[60,8]{0,1:T(8,128)S(1)}, f32[60,8]{0,1:T(8,128)S(1)}, u32[]{:S(2)}, u32[]{:S(2)}) %collective-permute-start.9) | collective-permute-done | bytes 1952 | tf_op jit(solution)/shard_map/ppermute | solution.py:18
  82.7 1.3 collective-permute-start.13
  85.5 3.4 %subtract_bitcast_fusion = (f32[60,8,128]{2,1,0:T(8,128)}, f32[1,60,8,128]{3,2,1,0:T(8,128)S(1)}, f32[1,60,8,128]{3,2,1,0:T(8,128)S(1)}, f32[1,60,8,128]{3,2,1,0:T(8,128)}, f32[1,60,8,128]{3,2,1,0:T(8,128)}) fusion(f32[1,60,8,1]{3,2,1,0:T(8,128)} %copy.539, f32[1,60,8,127]{3,2,1,0:T(8,128)S(1)} %get-tuple-element.49, ...), kind=kLoop, calls=%fused_computation.160 | loop fusion | flops 2150400 | bytes 3932192 | tf_op jit(solution)/shard_map/mul | solution.py:143
  91.0 4.5 %collective-permute-start.15 = (f32[60,128]{1,0:T(8,128)S(1)}, f32[60,128]{1,0:T(8,128)S(1)}, u32[]{:S(2)}, u32[]{:S(2)}) collective-permute-start(f32[60,128]{1,0:T(8,128)S(1)} %bitcast.168), channel_id=1, source_target_pairs={{0,8},{8,16},{16,24},{1,9},{9,17},{17,25},{2,10},{10,18},{18,26},{... | collective-permute-start | bytes 92168 | tf_op jit(solution)/shard_map/ppermute | solution.py:24
  96.0 1.2 fusion.111
  98.0 2.8 %collective-permute-done.14 = f32[60,8]{0,1:T(8,128)S(1)} collective-permute-done((f32[60,8]{0,1:T(8,128)S(1)}, f32[60,8]{0,1:T(8,128)S(1)}, u32[]{:S(2)}, u32[]{:S(2)}) %collective-permute-start.14) | collective-permute-done | bytes 1952 | tf_op jit(solution)/shard_map/ppermute | solution.py:18
  101.1 1.9 fusion.113
  104.2 1.8 maximum_bitcast_fusion
  106.0 5.2 %gather_fusion = bf16[1024,556]{1,0:T(8,128)(2,1)} fusion(bf16[1024,556]{1,0:T(8,128)(2,1)S(1)} %maximum_bitcast_fusion, s32[1024]{0:T(1024)S(1)} %broadcast_clamp_fusion), kind=kCustom, calls=%fused_computation | custom fusion | bytes 2281472 | tf_op jit(solution)/shard_map/jit(_take)/gather | solution.py:123
  111.2 5.5 %fusion.1 = bf16[1024,640]{1,0:T(8,128)(2,1)} fusion(bf16[768,640]{1,0:T(8,128)(2,1)S(1)} %copy-done, bf16[556,768]{1,0:T(8,128)(2,1)} %param.11, bf16[1024,556]{1,0:T(8,128)(2,1)} %gather_fusion, pred[1024]{0:T(1024)(128)(4,1)S(1)} %copy-done.35), kind=kOutput, calls=%fused_computation.10 | convolution fusion | flops 1886040064 | bytes 4287488 | tf_op jit(solution)/shard_map/dot_general | solution.py:30
  116.7 3.7 %fusion.119 = f32[1024,512]{1,0:T(8,128)} fusion(bf16[1024,640]{1,0:T(8,128)(2,1)} %fusion.1, bf16[640,512]{1,0:T(8,128)(2,1)S(1)} %copy-done.36), kind=kOutput, calls=%fused_computation.234 | convolution fusion | flops 671088640 | bytes 4063232 | tf_op jit(solution)/shard_map/dot_general | solution.py:30
  120.5 3.4 %convolution_convert_fusion = bf16[1024,368]{0,1:T(8,128)(2,1)S(1)} fusion(bf16[640,368]{0,1:T(8,128)(2,1)S(1)} %copy-done.38, bf16[512,640]{1,0:T(8,128)(2,1)S(1)} %copy-done.37, f32[1024,512]{1,0:T(8,128)} %fusion.119), kind=kOutput, calls=%fused_computation.37 | convolution fusion | flops 1157349376 | bytes 3977216 | tf_op jit(solution)/shard_map/dot_general | solution.py:32
  124.2 5.3 %scatter_custom_fusion = bf16[1025,368]{1,0:T(8,128)(2,1)S(1)} fusion(s32[1024]{0:T(1024)} %bitcast.199, bf16[1024,368]{1,0:T(8,128)(2,1)S(1)} %copy.551, bf16[]{:T(256)} %constant.30.clone.1), kind=kCustom, calls=%fused_computation.63 | custom fusion | bytes 754912 | tf_op jit(solution)/shard_map/scatter | solution.py:127
  130.7 1.1 copy-done.6
  132.2 1.3 copy.554
  133.4 1.4 copy.569
  136.7 1.9 pad_maximum_fusion.3
  138.6 1.8 slice.306
  140.4 1.7 copy.556
  142.2 2.4 %slice_multiply_fusion.1 = (f32[60,1024]{0,1:T(8,128)}, f32[60,1024]{0,1:T(8,128)}) fusion(f32[360,1024]{0,1:T(8,128)} %copy-done.6), kind=kLoop, calls=%fused_computation.62 | loop fusion | flops 122880 | bytes 983040 | tf_op jit(solution)/shard_map/mul | solution.py:133
  144.6 1.9 copy.557
  146.5 1.8 add.190
  148.3 1.9 copy.558
  151.2 26.3 %collective-permute-done.18 = bf16[5,60,8,128]{3,2,1,0:T(8,128)(2,1)} collective-permute-done((bf16[5,60,8,128]{3,2,1,0:T(8,128)(2,1)}, bf16[5,60,8,128]{3,2,1,0:T(8,128)(2,1)}, u32[]{:S(2)}, u32[]{:S(2)}) %collective-permute-start.18) | collective-permute-done | bytes 614432 | tf_op jit(solution)/shard_map/ppermute | solution.py:18
  177.6 2.3 %fusion.20 = (f32[5,60,8,128]{3,2,1,0:T(8,128)S(1)}, f32[5,60,8,128]{3,2,1,0:T(8,128)S(1)}) fusion(bf16[5,60,8,128]{3,2,1,0:T(8,128)(2,1)} %collective-permute-done.16, bf16[5,60,8,128]{3,2,1,0:T(8,128)(2,1)} %collective-permute-done.17, bf16[5,60,8,128]{3,2,1,0:T(8,128)(2,1)} %collective-permute-done.18, pred[8]{0:T(512)(128)(4,1)S(1)} %copy-done.25, ...), kind=kLoop, calls=%fused_computation.48 | loop fusion | flops 5836800 | bytes 6512704 | tf_op jit(solution)/shard_map/add | solution.py:60
  196.0 1.1 copy-done.5
  198.7 1.4 pad_maximum_fusion.1
  (227 shorter events, 57.8 us)
Async XLA Ops:
  0.6 110.5 %copy-start = (bf16[768,640]{1,0:T(8,128)(2,1)S(1)}, bf16[768,640]{1,0:T(8,128)(2,1)}, u32[]{:S(2)}) copy-start(bf16[768,640]{1,0:T(8,128)(2,1)} %param.12) | copy-start | bytes 2949124
  0.6 15.2 %copy-start.2 = (f32[8,60,8,128]{3,2,1,0:T(8,128)S(1)}, f32[8,60,8,128]{3,2,1,0:T(8,128)}, u32[]{:S(2)}) copy-start(f32[8,60,8,128]{3,2,1,0:T(8,128)} %param.9) | copy-start | bytes 5898244
  0.7 16.1 %copy-start.16 = (bf16[76,8,128]{2,1,0:T(8,128)(2,1)S(1)}, bf16[76,8,128]{2,1,0:T(8,128)(2,1)}, u32[]{:S(2)}) copy-start(bf16[76,8,128]{2,1,0:T(8,128)(2,1)} %param.10) | copy-start | bytes 466948
  1.9 20.1 %collective-permute-start = (f32[60,8]{0,1:T(8,128)S(1)}, f32[60,8]{0,1:T(8,128)S(1)}, u32[]{:S(2)}, u32[]{:S(2)}) collective-permute-start(f32[60,8]{0,1:T(8,128)S(1)} %bitcast.191), channel_id=1, source_target_pairs={{0,7},{1,0},{2,1},{3,2},{4,3},{5,4},{6,5},{7,6},{8,15},{9,8},{10,9... | collective-permute-start | bytes 5768 | tf_op jit(solution)/shard_map/ppermute | solution.py:18
  6.5 17.2 %collective-permute-start.2 = (f32[60,128]{1,0:T(8,128)S(1)}, f32[60,128]{1,0:T(8,128)S(1)}, u32[]{:S(2)}, u32[]{:S(2)}) collective-permute-start(f32[60,128]{1,0:T(8,128)S(1)} %bitcast.167), channel_id=1, source_target_pairs={{8,0},{16,8},{24,16},{9,1},{17,9},{25,17},{10,2},{18,10},{26,18},{... | collective-permute-start | bytes 92168 | tf_op jit(solution)/shard_map/ppermute | solution.py:24
  25.1 14.6 %copy-start.8 = (f32[60,8,128]{2,1,0:T(8,128)}, f32[60,8,128]{2,1,0:T(8,128)S(1)}, u32[]{:S(2)}) copy-start(f32[60,8,128]{2,1,0:T(8,128)S(1)} %get-tuple-element.39) | copy-start | bytes 737284
  26.6 13.1 %collective-permute-start.3 = (f32[60,128]{1,0:T(8,128)}, f32[60,128]{1,0:T(8,128)S(1)}, u32[]{:S(2)}, u32[]{:S(2)}) collective-permute-start(f32[60,128]{1,0:T(8,128)} %bitcast.133), channel_id=1, source_target_pairs={{0,8},{8,16},{16,24},{1,9},{9,17},{17,25},{2,10},{10,18},{18,26},{... | collective-permute-start | bytes 92168 | tf_op jit(solution)/shard_map/ppermute | solution.py:24
  33.0 4.9 %collective-permute-start.1 = (f32[60,8]{0,1:T(8,128)S(1)}, f32[60,8]{0,1:T(8,128)S(1)}, u32[]{:S(2)}, u32[]{:S(2)}) collective-permute-start(f32[60,8]{0,1:T(8,128)S(1)} %bitcast.196), channel_id=1, source_target_pairs={{0,1},{1,2},{2,3},{3,4},{4,5},{5,6},{6,7},{7,0},{8,9},{9,10},{10,1... | collective-permute-start | bytes 5768 | tf_op jit(solution)/shard_map/ppermute | solution.py:18
  42.1 2.9 %collective-permute-start.4 = (f32[60,8]{0,1:T(8,128)S(1)}, f32[60,8]{0,1:T(8,128)S(1)}, u32[]{:S(2)}, u32[]{:S(2)}) collective-permute-start(f32[60,8]{0,1:T(8,128)S(1)} %bitcast.193), channel_id=1, source_target_pairs={{0,7},{1,0},{2,1},{3,2},{4,3},{5,4},{6,5},{7,6},{8,15},{9,8},{10,9... | collective-permute-start | bytes 5768 | tf_op jit(solution)/shard_map/ppermute | solution.py:18
  43.7 6.3 %collective-permute-start.6 = (f32[60,128]{1,0:T(8,128)S(1)}, f32[60,128]{1,0:T(8,128)S(1)}, u32[]{:S(2)}, u32[]{:S(2)}) collective-permute-start(f32[60,128]{1,0:T(8,128)S(1)} %bitcast.170), channel_id=1, source_target_pairs={{8,0},{16,8},{24,16},{9,1},{17,9},{25,17},{10,2},{18,10},{26,18},{... | collective-permute-start | bytes 92168 | tf_op jit(solution)/shard_map/ppermute | solution.py:24
  52.2 10.9 %collective-permute-start.7 = (f32[60,128]{1,0:T(8,128)S(1)}, f32[60,128]{1,0:T(8,128)S(1)}, u32[]{:S(2)}, u32[]{:S(2)}) collective-permute-start(f32[60,128]{1,0:T(8,128)S(1)} %bitcast.171), channel_id=1, source_target_pairs={{0,8},{8,16},{16,24},{1,9},{9,17},{17,25},{2,10},{10,18},{18,26},{... | collective-permute-start | bytes 92168 | tf_op jit(solution)/shard_map/ppermute | solution.py:24
  57.2 4.9 %collective-permute-start.5 = (f32[60,8]{0,1:T(8,128)S(1)}, f32[60,8]{0,1:T(8,128)S(1)}, u32[]{:S(2)}, u32[]{:S(2)}) collective-permute-start(f32[60,8]{0,1:T(8,128)S(1)} %bitcast.197), channel_id=1, source_target_pairs={{0,1},{1,2},{2,3},{3,4},{4,5},{5,6},{6,7},{7,0},{8,9},{9,10},{10,1... | collective-permute-start | bytes 5768 | tf_op jit(solution)/shard_map/ppermute | solution.py:18
  63.5 2.9 %collective-permute-start.8 = (f32[60,8]{0,1:T(8,128)S(1)}, f32[60,8]{0,1:T(8,128)S(1)}, u32[]{:S(2)}, u32[]{:S(2)}) collective-permute-start(f32[60,8]{0,1:T(8,128)S(1)} %bitcast.195), channel_id=1, source_target_pairs={{0,7},{1,0},{2,1},{3,2},{4,3},{5,4},{6,5},{7,6},{8,15},{9,8},{10,9... | collective-permute-start | bytes 5768 | tf_op jit(solution)/shard_map/ppermute | solution.py:18
  63.6 5.9 %collective-permute-start.10 = (f32[60,128]{1,0:T(8,128)S(1)}, f32[60,128]{1,0:T(8,128)S(1)}, u32[]{:S(2)}, u32[]{:S(2)}) collective-permute-start(f32[60,128]{1,0:T(8,128)S(1)} %bitcast.173), channel_id=1, source_target_pairs={{8,0},{16,8},{24,16},{9,1},{17,9},{25,17},{10,2},{18,10},{26,18},{... | collective-permute-start | bytes 92168 | tf_op jit(solution)/shard_map/ppermute | solution.py:24
  70.5 10.9 %collective-permute-start.11 = (f32[60,128]{1,0:T(8,128)S(1)}, f32[60,128]{1,0:T(8,128)S(1)}, u32[]{:S(2)}, u32[]{:S(2)}) collective-permute-start(f32[60,128]{1,0:T(8,128)S(1)} %bitcast.172), channel_id=1, source_target_pairs={{0,8},{8,16},{16,24},{1,9},{9,17},{17,25},{2,10},{10,18},{18,26},{... | collective-permute-start | bytes 92168 | tf_op jit(solution)/shard_map/ppermute | solution.py:24
  75.5 4.9 %collective-permute-start.9 = (f32[60,8]{0,1:T(8,128)S(1)}, f32[60,8]{0,1:T(8,128)S(1)}, u32[]{:S(2)}, u32[]{:S(2)}) collective-permute-start(f32[60,8]{0,1:T(8,128)S(1)} %bitcast.198), channel_id=1, source_target_pairs={{0,1},{1,2},{2,3},{3,4},{4,5},{5,6},{6,7},{7,0},{8,9},{9,10},{10,1... | collective-permute-start | bytes 5768 | tf_op jit(solution)/shard_map/ppermute | solution.py:18
  81.8 2.7 %collective-permute-start.12 = (f32[60,8]{0,1:T(8,128)S(1)}, f32[60,8]{0,1:T(8,128)S(1)}, u32[]{:S(2)}, u32[]{:S(2)}) collective-permute-start(f32[60,8]{0,1:T(8,128)S(1)} %bitcast.194), channel_id=1, source_target_pairs={{0,7},{1,0},{2,1},{3,2},{4,3},{5,4},{6,5},{7,6},{8,15},{9,8},{10,9... | collective-permute-start | bytes 5768 | tf_op jit(solution)/shard_map/ppermute | solution.py:18
  82.7 7.1 %collective-permute-start.13 = (f32[60,128]{1,0:T(8,128)}, f32[60,128]{1,0:T(8,128)S(1)}, u32[]{:S(2)}, u32[]{:S(2)}) collective-permute-start(f32[60,128]{1,0:T(8,128)} %bitcast.136), channel_id=1, source_target_pairs={{8,0},{16,8},{24,16},{9,1},{17,9},{25,17},{10,2},{18,10},{26,18},{... | collective-permute-start | bytes 92168 | tf_op jit(solution)/shard_map/ppermute | solution.py:24
  88.8 8.4 %copy-start.11 = (f32[1,60,8,128]{3,2,1,0:T(8,128)}, f32[1,60,8,128]{3,2,1,0:T(8,128)S(1)}, u32[]{:S(2)}) copy-start(f32[1,60,8,128]{3,2,1,0:T(8,128)S(1)} %get-tuple-element.23) | copy-start | bytes 737284
  88.8 12.3 %copy-start.10 = (f32[1,60,8,128]{3,2,1,0:T(8,128)}, f32[1,60,8,128]{3,2,1,0:T(8,128)S(1)}, u32[]{:S(2)}) copy-start(f32[1,60,8,128]{3,2,1,0:T(8,128)S(1)} %get-tuple-element.22) | copy-start | bytes 737284
  91.0 10.1 %collective-permute-start.15 = (f32[60,128]{1,0:T(8,128)S(1)}, f32[60,128]{1,0:T(8,128)S(1)}, u32[]{:S(2)}, u32[]{:S(2)}) collective-permute-start(f32[60,128]{1,0:T(8,128)S(1)} %bitcast.168), channel_id=1, source_target_pairs={{0,8},{8,16},{16,24},{1,9},{9,17},{17,25},{2,10},{10,18},{18,26},{... | collective-permute-start | bytes 92168 | tf_op jit(solution)/shard_map/ppermute | solution.py:24
  95.8 5.0 %collective-permute-start.14 = (f32[60,8]{0,1:T(8,128)S(1)}, f32[60,8]{0,1:T(8,128)S(1)}, u32[]{:S(2)}, u32[]{:S(2)}) collective-permute-start(f32[60,8]{0,1:T(8,128)S(1)} %bitcast.192), channel_id=1, source_target_pairs={{0,1},{1,2},{2,3},{3,4},{4,5},{5,6},{6,7},{7,0},{8,9},{9,10},{10,1... | collective-permute-start | bytes 5768 | tf_op jit(solution)/shard_map/ppermute | solution.py:18
  101.1 3.1 %copy-start.9 = (bf16[300,1024]{0,1:T(8,128)(2,1)S(1)}, bf16[300,1024]{0,1:T(8,128)(2,1)}, u32[]{:S(2)}) copy-start(bf16[300,1024]{0,1:T(8,128)(2,1)} %copy.550) | copy-start | bytes 1843204
  106.0 5.2 %copy-start.35 = (pred[1024]{0:T(1024)(128)(4,1)S(1)}, pred[1024]{0:T(1024)(128)(4,1)}, u32[]{:S(2)}) copy-start(pred[1024]{0:T(1024)(128)(4,1)} %compare_and_fusion) | copy-start | bytes 3076
  111.2 5.5 %copy-start.36 = (bf16[640,512]{1,0:T(8,128)(2,1)S(1)}, bf16[640,512]{1,0:T(8,128)(2,1)}, u32[]{:S(2)}) copy-start(bf16[640,512]{1,0:T(8,128)(2,1)} %param.13) | copy-start | bytes 1966084
  116.7 3.8 %copy-start.37 = (bf16[512,640]{1,0:T(8,128)(2,1)S(1)}, bf16[512,640]{1,0:T(8,128)(2,1)}, u32[]{:S(2)}) copy-start(bf16[512,640]{1,0:T(8,128)(2,1)} %param.14) | copy-start | bytes 1966084
  116.7 3.8 %copy-start.38 = (bf16[640,368]{0,1:T(8,128)(2,1)S(1)}, bf16[640,368]{0,1:T(8,128)(2,1)}, u32[]{:S(2)}) copy-start(bf16[640,368]{0,1:T(8,128)(2,1)} %param.15) | copy-start | bytes 1413124
  132.1 2.7 %copy-start.3 = (f32[8,60,8,128]{3,2,1,0:T(8,128)S(1)}, f32[8,60,8,128]{3,2,1,0:T(8,128)}, u32[]{:S(2)}) copy-start(f32[8,60,8,128]{3,2,1,0:T(8,128)} %param.9) | copy-start | bytes 5898244
  133.4 2.4 %copy-start.29 = (s32[8]{0:T(128)S(1)}, s32[8]{0:T(128)}, u32[]{:S(2)}) copy-start(s32[8]{0:T(128)} %get-tuple-element.17) | copy-start | bytes 100
  135.8 41.7 %collective-permute-start.18 = (bf16[5,60,8,128]{3,2,1,0:T(8,128)(2,1)}, bf16[5,60,8,128]{3,2,1,0:T(8,128)(2,1)}, u32[]{:S(2)}, u32[]{:S(2)}) collective-permute-start(bf16[5,60,8,128]{3,2,1,0:T(8,128)(2,1)} %fusion.106), channel_id=1, source_target_pairs={{0,3},{1,4},{2,5},{3,6},{4,7},{5,0},{6,1},{7,2},{8,11},{9,12},{10,... | collective-permute-start | bytes 1843208 | tf_op jit(solution)/shard_map/ppermute | solution.py:18
  135.8 41.7 %collective-permute-start.17 = (bf16[5,60,8,128]{3,2,1,0:T(8,128)(2,1)}, bf16[5,60,8,128]{3,2,1,0:T(8,128)(2,1)}, u32[]{:S(2)}, u32[]{:S(2)}) collective-permute-start(bf16[5,60,8,128]{3,2,1,0:T(8,128)(2,1)} %fusion.106), channel_id=1, source_target_pairs={{0,2},{1,3},{2,4},{3,5},{4,6},{5,7},{6,0},{7,1},{8,10},{9,11},{10,... | collective-permute-start | bytes 1843208 | tf_op jit(solution)/shard_map/ppermute | solution.py:18
  135.8 41.7 %collective-permute-start.16 = (bf16[5,60,8,128]{3,2,1,0:T(8,128)(2,1)}, bf16[5,60,8,128]{3,2,1,0:T(8,128)(2,1)}, u32[]{:S(2)}, u32[]{:S(2)}) collective-permute-start(bf16[5,60,8,128]{3,2,1,0:T(8,128)(2,1)} %fusion.106), channel_id=1, source_target_pairs={{0,1},{1,2},{2,3},{3,4},{4,5},{5,6},{6,7},{7,0},{8,9},{9,10},{10,1... | collective-permute-start | bytes 1843208 | tf_op jit(solution)/shard_map/ppermute | solution.py:18
  142.1 35.4 %copy-start.19 = (pred[8]{0:T(512)(128)(4,1)S(1)}, pred[8]{0:T(512)(128)(4,1)}, u32[]{:S(2)}) copy-start(pred[8]{0:T(512)(128)(4,1)} %get-tuple-element.96) | copy-start | bytes 28
  142.1 35.5 %copy-start.22 = (pred[8]{0:T(512)(128)(4,1)S(1)}, pred[8]{0:T(512)(128)(4,1)}, u32[]{:S(2)}) copy-start(pred[8]{0:T(512)(128)(4,1)} %get-tuple-element.98) | copy-start | bytes 28
  142.1 35.5 %copy-start.23 = (pred[8]{0:T(512)(128)(4,1)S(1)}, pred[8]{0:T(512)(128)(4,1)}, u32[]{:S(2)}) copy-start(pred[8]{0:T(512)(128)(4,1)} %get-tuple-element.99) | copy-start | bytes 28
  142.1 35.5 %copy-start.24 = (pred[8]{0:T(512)(128)(4,1)S(1)}, pred[8]{0:T(512)(128)(4,1)}, u32[]{:S(2)}) copy-start(pred[8]{0:T(512)(128)(4,1)} %get-tuple-element.100) | copy-start | bytes 28
  142.1 35.5 %copy-start.25 = (pred[8]{0:T(512)(128)(4,1)S(1)}, pred[8]{0:T(512)(128)(4,1)}, u32[]{:S(2)}) copy-start(pred[8]{0:T(512)(128)(4,1)} %get-tuple-element.101) | copy-start | bytes 28
  142.1 35.5 %copy-start.26 = (pred[8]{0:T(512)(128)(4,1)S(1)}, pred[8]{0:T(512)(128)(4,1)}, u32[]{:S(2)}) copy-start(pred[8]{0:T(512)(128)(4,1)} %get-tuple-element.102) | copy-start | bytes 28
  142.1 35.5 %copy-start.27 = (pred[8]{0:T(512)(128)(4,1)S(1)}, pred[8]{0:T(512)(128)(4,1)}, u32[]{:S(2)}) copy-start(pred[8]{0:T(512)(128)(4,1)} %get-tuple-element.103) | copy-start | bytes 28
  142.1 35.5 %copy-start.28 = (pred[8]{0:T(512)(128)(4,1)S(1)}, pred[8]{0:T(512)(128)(4,1)}, u32[]{:S(2)}) copy-start(pred[8]{0:T(512)(128)(4,1)} %get-tuple-element.104) | copy-start | bytes 28
  189.2 1.5 copy-start.4
  195.4 1.7 copy-start.5
  195.8 1.7 slice-start
  195.9 1.7 copy-start.12
  195.9 1.8 copy-start.13
  195.9 1.8 copy-start.17
  195.9 1.7 copy-start.18
  197.6 2.5 %copy-start.1 = (bf16[768,640]{1,0:T(8,128)(2,1)S(1)}, bf16[768,640]{1,0:T(8,128)(2,1)}, u32[]{:S(2)}) copy-start(bf16[768,640]{1,0:T(8,128)(2,1)} %param.12) | copy-start | bytes 2949124
  (11 other events, 9.4 us)
where the time goes:
time: 201 us; the launch traced here: 200 us
  local copies, waits for them, and re-layouts  70.6 us (35%)
  waiting for transfers between devices  43.9 us (22%)
  other arithmetic  42.6 us (21%)
  starting transfers between devices  28.6 us (14%)
  matrix products  12.7 us (6%)
    ppermute x11, waiting for transfers between devices, shifted(): return lax.ppermute(value, axis, pairs)  40.7 us
    ppermute x8, starting transfers between devices, passed_along(): return lax.ppermute(block, axis, route)  23.6 us
    unnamed x93, local copies, waits for them, and re-layouts  12.3 us
    dot_general x2, matrix products, run_network(): summed = jnp.dot(hidden, weight, preferred_element_type=jnp.float32)  9.25 us
    slice x15, local copies, waits for them, and re-layouts, shift_rows(): moved[..., step_size:]  8.89 us
    concatenate x7, local copies, waits for them, and re-layouts, on_device(): jnp.concatenate([pressure[:, :, 1:], east_col[:, :, None]], axis=2)  6.21 us
    select_n x12, other arithmetic, shift_rows(): moved = jnp.where(chosen[None, None, :, None], stepped, moved)  5.57 us
    scatter x1, local copies, waits for them, and re-layouts, on_device(): jnp.zeros((columns + 1, results.shape[1]), jnp.bfloat16).at[slots]  5.31 us
  transfers between devices with their start and end apart: 19, of which 7 were waited for; matrix products, arithmetic and copies ran while one was open for 29% of the time, Pallas kernels for 0%

commit v1 on v0

v1 whole, which is shorter than its diff:
```python
import functools

import jax
import jax.numpy as jnp
from jax import lax
from jax.experimental import pallas as pl
from jax.experimental.pallas import tpu as pltpu
from jax.sharding import PartitionSpec as P

SUBSTEPS = 4
SOUND_COURANT = 0.6
PHYSICS_STEP = 0.5
LEAK_SLOPE = 0.15

STRIP = 6 * SUBSTEPS
F32 = jnp.float32
BF16 = jnp.bfloat16


def vmem():
    return pl.BlockSpec(memory_space=pltpu.VMEM)


def any_space():
    return pl.BlockSpec(memory_space=pl.ANY)


def params(mib):
    return pltpu.CompilerParams(vmem_limit_bytes=mib << 20)


def cost(flops, nbytes):
    return pl.CostEstimate(flops=flops, bytes_accessed=nbytes, transcendentals=0)


def iota(shape, dim):
    return lax.broadcasted_iota(jnp.int32, shape, dim)


def back(shift, size):
    return (size - shift) % size


def pack_rows_kernel(state_ref, south_ref, north_ref, ozone_ref):
    levels = 3 * state_ref.shape[1]
    rows, cols = state_ref.shape[2:]
    low = iota((rows, cols), 0) < rows // 2
    flat = state_ref.reshape(state_ref.shape[0] * state_ref.shape[1], rows, cols)

    def body(step, carry):
        block = flat[pl.ds(step * 20, 20)].reshape(10, 2, rows, cols)
        even = block[:, 0]
        odd = pltpu.roll(block[:, 1], rows // 2, 1)
        south = jnp.where(low, even, odd)
        north = jnp.where(low, odd, even)
        south_ref[pl.ds(step * 5, 5)] = south.reshape(5, 2 * rows, cols).astype(BF16)
        north_ref[pl.ds(step * 5, 5)] = north.reshape(5, 2 * rows, cols).astype(BF16)
        return carry

    lax.fori_loop(0, levels // 20, body, 0)
    count = state_ref.shape[1]
    last = state_ref[state_ref.shape[0] - 1]
    ozone_ref[...] = last.reshape(count // 2, 2 * rows, cols).astype(BF16)


def pack_rows(state):
    fields, levels, rows, cols = state.shape
    half = jax.ShapeDtypeStruct((3 * levels // 4, 2 * rows, cols), BF16)
    return pl.pallas_call(
        pack_rows_kernel,
        out_shape=(half, half, jax.ShapeDtypeStruct((levels // 2, 2 * rows, cols), BF16)),
        in_specs=[vmem()],
        out_specs=(vmem(), vmem(), vmem()),
        compiler_params=params(8),
        cost_estimate=cost(1 << 20, 4 << 20),
    )(state)


def halo_rows(north_pair, south_pair, low):
    even = jnp.where(low, north_pair, south_pair)
    odd = pltpu.roll(jnp.where(low, south_pair, north_pair), north_pair.shape[-2] // 2, 1)
    return even, odd


def pack_cols_kernel(state_ref, from_north_ref, from_south_ref, west_ref, east_ref):
    levels = state_ref.shape[1]
    rows, cols = state_ref.shape[2:]
    per = cols // STRIP
    low = iota((rows, cols), 0) < rows // 2
    lane = iota((2 * rows, cols), 1)
    flat = state_ref.reshape(state_ref.shape[0] * levels, rows, cols)

    def body(step, carry):
        own = flat[pl.ds(step * 20, 20)]
        north = from_north_ref[pl.ds(step * 5, 5)].astype(F32).reshape(10, rows, cols)
        south = from_south_ref[pl.ds(step * 5, 5)].astype(F32).reshape(10, rows, cols)
        even, odd = halo_rows(north, south, low)
        west_out, east_out = [], []
        for pack in range(4):
            west = jnp.zeros((2 * rows, cols), F32)
            east = jnp.zeros((2 * rows, cols), F32)
            for slot in range(per):
                level = pack * per + slot
                side = (odd if level % 2 else even)[level // 2]
                tile = jnp.concatenate([own[level], side], axis=0)
                start = slot * STRIP
                inside = (lane >= start) & (lane < start + STRIP)
                west = jnp.where(inside, pltpu.roll(tile, start + 2 * SUBSTEPS, 1), west)
                east = jnp.where(inside, pltpu.roll(tile, start + 4 * SUBSTEPS, 1), east)
            west_out.append(west)
            east_out.append(east)
        west_ref[pl.ds(step * 4, 4)] = jnp.stack(west_out).astype(BF16)
        east_ref[pl.ds(step * 4, 4)] = jnp.stack(east_out).astype(BF16)
        return carry

    lax.fori_loop(0, 3 * levels // 20, body, 0)


def pack_cols(state, from_north, from_south):
    fields, levels, rows, cols = state.shape
    packs = 3 * levels // (cols // STRIP)
    strip = jax.ShapeDtypeStruct((packs, 2 * rows, cols), BF16)
    return pl.pallas_call(
        pack_cols_kernel,
        out_shape=(strip, strip),
        in_specs=[vmem()] * 3,
        out_specs=(vmem(), vmem()),
        compiler_params=params(8),
        cost_estimate=cost(1 << 20, 4 << 20),
    )(state, from_north, from_south)


def open_rows(rows, cols):
    place = iota((2 * rows, cols), 0)
    offset = jnp.where(place < rows + rows // 2, place, place - 2 * rows)
    row = lax.axis_index("lat") * rows + offset
    last = rows * lax.axis_size("lat") - 1
    return jnp.where((row >= 0) & (row < last), 1.0, 0.0).astype(F32)


def substeps(zonal, merid, press, free):
    rows, cols = zonal.shape[-2:]
    for _ in range(SUBSTEPS):
        zonal = zonal - SOUND_COURANT * (pltpu.roll(press, cols - 1, 2) - press)
        merid = (merid - SOUND_COURANT * (pltpu.roll(press, rows - 1, 1) - press)) * free
        press = press - SOUND_COURANT * (
            zonal - pltpu.roll(zonal, 1, 2) + merid - pltpu.roll(merid, 1, 1)
        )
    return zonal, merid, press


def inner_kernel(state_ref, from_north_ref, from_south_ref, out_ref):
    levels = state_ref.shape[1]
    rows, cols = state_ref.shape[2:]
    low = iota((rows, cols), 0) < rows // 2
    free = open_rows(rows, cols)

    def body(step, carry):
        parts = []
        for field in range(3):
            own = state_ref[field, pl.ds(step * 4, 4)]
            at = field * (levels // 4) + step
            north = from_north_ref[at].astype(F32).reshape(2, rows, cols)
            south = from_south_ref[at].astype(F32).reshape(2, rows, cols)
            even, odd = halo_rows(north, south, low)
            side = jnp.stack([even[0], odd[0], even[1], odd[1]])
            parts.append(jnp.concatenate([own, side], axis=1))
        for field, value in enumerate(substeps(*parts, free)):
            out_ref[field, pl.ds(step * 4, 4)] = value[:, :rows]
        return carry

    lax.fori_loop(0, levels // 4, body, 0)


def inner(state, from_north, from_south):
    fields, levels, rows, cols = state.shape
    return pl.pallas_call(
        inner_kernel,
        out_shape=jax.ShapeDtypeStruct((3, levels, rows, cols), F32),
        in_specs=[vmem()] * 3,
        out_specs=vmem(),
        compiler_params=params(8),
        cost_estimate=cost(1 << 24, 4 << 20),
    )(state, from_north, from_south)


def rest_kernel(state_ref, surface_ref, slots_ref, rest_ref, lit_ref, buffer, wide):
    fields, levels, rows, cols = state_ref.shape
    extra = surface_ref.shape[0]
    first = 3 * levels
    wide[...] = surface_ref[...].astype(F32).reshape(extra * rows, cols)
    flat = state_ref.reshape(fields * levels * rows, cols)
    buffer[0:first] = jnp.zeros((first, cols), F32)
    for row in range(rows):
        buffer[first : fields * levels] = flat[
            pl.ds(first * rows + row, (fields - 3) * levels, stride=rows), :
        ]
        buffer[fields * levels : fields * levels + extra] = wide[pl.ds(row, extra, stride=rows), :]
        rest_ref[:, row * cols : (row + 1) * cols] = buffer[...].astype(BF16)
    slots = slots_ref[...]
    count = slots.shape[1]
    in_row = (slots // cols == iota((rows, count), 0)).astype(F32).astype(BF16)
    in_col = (slots % cols == iota((cols, count), 0)).astype(F32).astype(BF16)
    lit_ref[...] = lax.dot_general(
        in_row, in_col, (((1,), (1,)), ((), ())), preferred_element_type=F32
    )


def rest_features(state, surface, slots):
    fields, levels, rows, cols = state.shape
    count = fields * levels + surface.shape[0]
    return pl.pallas_call(
        rest_kernel,
        out_shape=(
            jax.ShapeDtypeStruct((count, rows * cols), BF16),
            jax.ShapeDtypeStruct((rows, cols), F32),
        ),
        in_specs=[vmem()] * 3,
        out_specs=(vmem(), vmem()),
        scratch_shapes=[
            pltpu.VMEM((count, cols), F32),
            pltpu.VMEM((surface.shape[0] * rows, cols), F32),
        ],
        compiler_params=params(12),
        cost_estimate=cost(1 << 24, 4 << 20),
    )(state, surface, slots)


def leaky(value):
    return jnp.maximum(value, LEAK_SLOPE * value).astype(BF16)


def tracer_update(weight, hidden, lit, state_at, out_ref, spread):
    rows, cols = lit.shape
    levels = weight.shape[0]
    result = lax.dot_general(
        weight, hidden, (((1,), (1,)), ((), ())), preferred_element_type=F32
    )
    for row in range(rows):
        spread[pl.ds(row, levels, stride=rows), :] = result[:, row * cols : (row + 1) * cols]

    def body(step, carry):
        value = spread[pl.ds(step * 10 * rows, 10 * rows), :].reshape(10, rows, cols)
        value = jnp.where(lit > 0.5, value.astype(BF16).astype(F32), 0.0)
        value = state_at(step) + PHYSICS_STEP * value
        out_ref[pl.ds(step * 5, 5)] = value.reshape(5, 2 * rows, cols).astype(BF16)
        return carry

    lax.fori_loop(0, levels // 10, body, 0)


def network_kernel(
    inner_ref,
    own_west_ref,
    own_east_ref,
    from_east_ref,
    from_west_ref,
    rest_ref,
    one_ref,
    two_ref,
    three_ref,
    four_ref,
    five_ref,
    lit_ref,
    state_ref,
    winds_ref,
    upwind_ref,
    hidden_ref,
    tracer_ref,
    strips,
    spread,
    features,
):
    fields, levels, rows, cols = inner_ref.shape
    per = cols // STRIP
    packs = levels // per
    place = iota((2 * rows, cols), 1) % STRIP
    free = open_rows(rows, cols)

    def side(step, carry):
        parts = []
        for field in range(3):
            at = pl.ds(field * packs + step * 4, 4)
            value = jnp.where(
                place < 2 * SUBSTEPS,
                own_west_ref[at].astype(F32),
                jnp.where(
                    place < 3 * SUBSTEPS,
                    from_east_ref[at].astype(F32),
                    jnp.where(
                        place < 4 * SUBSTEPS,
                        from_west_ref[at].astype(F32),
                        own_east_ref[at].astype(F32),
                    ),
                ),
            )
            parts.append(value)
        for field, value in enumerate(substeps(*parts, free)):
            strips[field, pl.ds(step * 4, 4)] = value[:, :rows]
        return carry

    lax.fori_loop(0, packs // 4, side, 0)
    lane = iota((rows, cols), 1)

    def merge(step, carry):
        for slot in range(per):
            level = step * per + slot
            for field in range(3):
                strip = strips[field, step]
                west = pltpu.roll(strip, back(slot * STRIP + 4 * SUBSTEPS, cols), 1)
                east = pltpu.roll(strip, back(slot * STRIP + 2 * SUBSTEPS, cols), 1)
                value = inner_ref[field, level]
                value = jnp.where(lane < SUBSTEPS, west, value)
                value = jnp.where(lane >= cols - SUBSTEPS, east, value)
                winds_ref[pl.ds((field * levels + level) * rows, rows), :] = value
                if field == 0:
                    upwind_ref[level] = pltpu.roll(jnp.where(lane == cols - 1, west, value), 1, 1)
        return carry

    lax.fori_loop(0, packs, merge, 0)
    count = 3 * levels
    features[...] = rest_ref[...]
    for row in range(rows):
        features[0:count, row * cols : (row + 1) * cols] = winds_ref[
            pl.ds(row, count, stride=rows), :
        ].astype(BF16)
    total = rows * cols
    chunk = total // 2

    for part in range(2):
        at = part * chunk
        hidden = leaky(
            lax.dot_general(
                features[:, at : at + chunk],
                one_ref[...],
                (((0,), (0,)), ((), ())),
                preferred_element_type=F32,
            )
        )
        for weight in (two_ref, three_ref, four_ref):
            hidden = leaky(jnp.dot(hidden, weight[...], preferred_element_type=F32))
        hidden_ref[at : at + chunk] = hidden
    size = five_ref.shape[0]
    tracer_update(
        five_ref[...],
        hidden_ref[...],
        lit_ref[...],
        lambda step: state_ref[pl.ds(step * 10, 10)],
        tracer_ref,
        spread,
    )


def network(inner_out, strips, rest, layers, five, lit, tracers):
    fields, levels, rows, cols = inner_out.shape
    count = five.shape[0]
    width = layers[3].shape[1]
    return pl.pallas_call(
        network_kernel,
        out_shape=(
            jax.ShapeDtypeStruct((3 * levels * rows, cols), F32),
            jax.ShapeDtypeStruct((levels, rows, cols), F32),
            jax.ShapeDtypeStruct((rows * cols, width), BF16),
            jax.ShapeDtypeStruct((count // 2, 2 * rows, cols), BF16),
        ),
        in_specs=[vmem()] * 13,
        out_specs=(vmem(),) * 4,
        scratch_shapes=[
            pltpu.VMEM((3, levels * STRIP // (cols - cols % STRIP), rows, cols), F32),
            pltpu.VMEM((count * rows, cols), F32),
            pltpu.VMEM(rest.shape, BF16),
        ],
        compiler_params=params(32),
        cost_estimate=cost(4 << 30, 8 << 20),
    )(inner_out, *strips, rest, *layers, five, lit, tracers)


def second_kernel(hidden_ref, five_ref, lit_ref, state_ref, tracer_ref, spread):
    tracer_update(
        five_ref[...],
        hidden_ref[...],
        lit_ref[...],
        lambda step: state_ref[pl.ds(step * 10, 10)],
        tracer_ref,
        spread,
    )


def second(hidden, five, lit, tracers):
    rows, cols = lit.shape
    count = five.shape[0]
    return pl.pallas_call(
        second_kernel,
        out_shape=jax.ShapeDtypeStruct((count // 2, 2 * rows, cols), BF16),
        in_specs=[vmem()] * 4,
        out_specs=vmem(),
        scratch_shapes=[pltpu.VMEM((count * rows, cols), F32)],
        compiler_params=params(16),
        cost_estimate=cost(1 << 28, 3 << 20),
    )(hidden, five, lit, tracers)


def winds_kernel(
    hidden_ref, five_ref, lit_ref, winds_ref, upwind_ref, out_ref, flux_ref, stay_ref, come_ref,
    spread, updated, sem
):
    rows, cols = lit_ref.shape
    levels = upwind_ref.shape[0]
    fluxes = flux_ref.shape[0]
    result = lax.dot_general(
        five_ref[...], hidden_ref[...], (((1,), (1,)), ((), ())), preferred_element_type=F32
    )
    count = five_ref.shape[0]
    for row in range(rows):
        spread[pl.ds(row, count, stride=rows), :] = result[:, row * cols : (row + 1) * cols]
    lit = lit_ref[...] > 0.5

    def body(step, carry):
        value = spread[pl.ds(step * 10 * rows, 10 * rows), :].reshape(10, rows, cols)
        value = jnp.where(lit, value.astype(BF16).astype(F32), 0.0)
        wind = winds_ref[pl.ds(step * 10 * rows, 10 * rows), :].reshape(10, rows, cols)
        updated[pl.ds(step * 10, 10)] = wind + PHYSICS_STEP * value
        return carry

    lax.fori_loop(0, 2 * levels // 10, body, 0)
    updated[2 * levels : 3 * levels] = winds_ref[2 * levels * rows :, :].reshape(
        levels, rows, cols
    )
    copy = pltpu.make_async_copy(
        updated, out_ref.at[pl.ds(0, 3 * levels)], sem
    )
    copy.start()
    value = spread[2 * levels * rows :, :].reshape(fluxes, rows, cols)
    flux_ref[...] = jnp.where(lit, value, 0.0).astype(BF16)

    def share(step, carry):
        here = winds_ref[pl.ds(step * 10 * rows, 10 * rows), :].reshape(10, rows, cols)
        stay_ref[pl.ds(step * 10, 10)] = 0.5 - 0.45 * jnp.tanh(here)
        come_ref[pl.ds(step * 10, 10)] = 0.5 + 0.45 * jnp.tanh(upwind_ref[pl.ds(step * 10, 10)])
        return carry

    lax.fori_loop(0, levels // 10, share, 0)
    copy.wait()


def winds_out(hidden, five, lit, winds, upwind, fields):
    levels, rows, cols = upwind.shape
    fluxes = five.shape[0] - 2 * levels
    share = jax.ShapeDtypeStruct((levels, rows, cols), F32)
    return pl.pallas_call(
        winds_kernel,
        out_shape=(
            jax.ShapeDtypeStruct((fields * levels, rows, cols), F32),
            jax.ShapeDtypeStruct((fluxes, rows, cols), BF16),
            share,
            share,
        ),
        in_specs=[vmem()] * 5,
        out_specs=(any_space(), vmem(), vmem(), vmem()),
        scratch_shapes=[
            pltpu.VMEM((five.shape[0] * rows, cols), F32),
            pltpu.VMEM((3 * levels, rows, cols), F32),
            pltpu.SemaphoreType.DMA,
        ],
        compiler_params=params(16),
        cost_estimate=cost(1 << 28, 4 << 20),
    )(hidden, five, lit, winds, upwind)


def spread_offsets(offset_ref, rows, cols):
    place = iota((rows, cols), 0)
    offset = jnp.zeros((rows, cols), jnp.int32)
    for row in range(rows):
        offset = jnp.where(place == row, offset_ref[row], offset)
    return offset // cols, offset % cols


def along(value, index):
    return jnp.take_along_axis(value, index, axis=1, mode="promise_in_bounds")


def relay_kernel(offset_ref, own_ref, near_ref, out_ref):
    rows = own_ref.shape[1] // 2
    cols = own_ref.shape[2]
    pairs = own_ref.shape[0]
    blocks, cells = spread_offsets(offset_ref, rows, cols)
    lane = iota((rows, cols), 1)
    take_near = (blocks >= 2) & (lane > cols - 1 - cells)
    edge = cols - 1 - cells

    def body(step, column):
        at = pl.ds(step * 5, 5)
        own = own_ref[at].astype(F32).reshape(10, rows, cols)
        near = near_ref[at].astype(F32).reshape(10, rows, cols)
        out = jnp.where(take_near, near, own)
        out_ref[at] = out.reshape(5, 2 * rows, cols).astype(BF16)
        for level in range(10):
            column = jnp.where(lane == step * 10 + level, along(near[level], edge), column)
        return column

    column = lax.fori_loop(0, pairs // 5, body, jnp.zeros((rows, cols), F32))
    out_ref[pairs] = jnp.concatenate([column, column], axis=0).astype(BF16)


def relay(offset, own, near):
    pairs, height, cols = own.shape
    return pl.pallas_call(
        relay_kernel,
        out_shape=jax.ShapeDtypeStruct((pairs + 1, height, cols), BF16),
        in_specs=[pl.BlockSpec(memory_space=pltpu.SMEM), vmem(), vmem()],
        out_specs=vmem(),
        compiler_params=params(8),
        cost_estimate=cost(1 << 20, 1 << 20),
    )(offset, own, near)


def advect_kernel(
    first, offset_ref, own_ref, near_ref, far_ref, stay_ref, come_ref, whole_ref, out_ref, result, sem
):
    levels, rows, cols = stay_ref.shape
    pairs = own_ref.shape[0]
    blocks, cells = spread_offsets(offset_ref, rows, cols)
    lane = iota((rows, cols), 1)
    from_right = lane <= cols - 1 - cells
    index = (lane - cells) & (cols - 1)
    index_less = (lane - cells - 1) & (cols - 1)
    column = far_ref[pairs].astype(F32)[:rows]
    is_zero, is_one, is_two = blocks == 0, blocks == 1, blocks >= 2
    steps = levels // 10
    copies = []
    for field in range(2 * pairs // levels):
        def body(step, carry):
            at = pl.ds(field * (levels // 2) + step * 5, 5)
            own = own_ref[at].astype(F32).reshape(10, rows, cols)
            near = near_ref[at].astype(F32).reshape(10, rows, cols)
            far = far_ref[at].astype(F32).reshape(10, rows, cols)
            stay = stay_ref[pl.ds(step * 10, 10)]
            come = come_ref[pl.ds(step * 10, 10)]
            right = jnp.where(is_zero, own, jnp.where(is_one, near, far))
            left = jnp.where(is_zero, near, far)
            merged = jnp.where(from_right, right, left)
            for level in range(10):
                which = field * levels + step * 10 + level
                lone = along(column, jnp.zeros((rows, cols), jnp.int32) + which)
                edge = jnp.where(is_two, lone, left[level])
                shifted = jnp.where(lane == cols - 1 - cells, edge, merged[level])
                here = along(merged[level], index)
                behind = along(shifted, index_less)
                result[field * levels + step * 10 + level] = (
                    stay[level] * here + come[level] * behind
                )
            return carry

        lax.fori_loop(0, steps, body, 0)
        copy = pltpu.make_async_copy(
            result.at[pl.ds(field * levels, levels)],
            out_ref.at[pl.ds((first + field) * levels, levels)],
            sem.at[field],
        )
        copy.start()
        copies.append(copy)
    for copy in copies:
        copy.wait()


def advect(first, offset, own, near, far, stay, come, whole):
    pairs, height, cols = own.shape
    levels = stay.shape[0]
    return pl.pallas_call(
        functools.partial(advect_kernel, first),
        out_shape=jax.ShapeDtypeStruct(whole.shape, F32),
        in_specs=[pl.BlockSpec(memory_space=pltpu.SMEM)] + [vmem()] * 5 + [any_space()],
        out_specs=any_space(),
        scratch_shapes=[
            pltpu.VMEM((2 * pairs, height // 2, cols), F32),
            pltpu.SemaphoreType.DMA((2 * pairs // levels,)),
        ],
        input_output_aliases={6: 0},
        compiler_params=params(12),
        cost_estimate=cost(1 << 22, 3 << 20),
    )(offset, own, near, far, stay, come, whole)


def shifted(value, axis, steps):
    count = lax.axis_size(axis)
    return lax.ppermute(value, axis, [(i, (i + steps) % count) for i in range(count)])


def passed_along(block, axis, distance):
    devices = range(lax.axis_size(axis))
    return lax.ppermute(
        block, axis, [(i, i + distance) for i in devices if i + distance in devices]
    )


def on_device(
    state,
    surface,
    layer_one,
    layer_two,
    layer_three,
    layer_four,
    layer_five,
    lit_columns,
    row_offset,
):
    fields, levels, rows, cols = state.shape
    slots = lit_columns.reshape(1, rows * cols)
    flat = state.reshape(fields * levels, rows, cols)

    to_south, to_north, ozone = pack_rows(state)
    from_north = passed_along(to_south, "lat", -1)
    from_south = passed_along(to_north, "lat", 1)
    ozone_near = shifted(ozone, "lon", 1)

    rest, lit = rest_features(state, surface, slots)
    five = layer_five.T
    five_first = five[2 * levels : 4 * levels]
    five_second = five[4 * levels : 6 * levels]
    five_winds = jnp.concatenate([five[: 2 * levels], five[6 * levels :]], axis=0)

    to_west, to_east = pack_cols(state, from_north, from_south)
    from_east = shifted(to_west, "lon", -1)
    from_west = shifted(to_east, "lon", 1)
    inner_out = inner(state, from_north, from_south)
    ozone_far = shifted(relay(row_offset, ozone, ozone_near), "lon", 2)

    winds, upwind, hidden, first = network(
        inner_out,
        (to_west, to_east, from_east, from_west),
        rest,
        (layer_one, layer_two, layer_three, layer_four),
        five_first,
        lit,
        flat[3 * levels : 5 * levels],
    )
    first_near = shifted(first, "lon", 1)
    other = second(hidden, five_second, lit, flat[5 * levels : 7 * levels])
    other_near = shifted(other, "lon", 1)
    first_far = shifted(relay(row_offset, first, first_near), "lon", 2)
    other_far = shifted(relay(row_offset, other, other_near), "lon", 2)
    whole, flux, stay, come = winds_out(hidden, five_winds, lit, winds, upwind, fields)
    whole = advect(7, row_offset, ozone, ozone_near, ozone_far, stay, come, whole)
    whole = advect(3, row_offset, first, first_near, first_far, stay, come, whole)
    whole = advect(5, row_offset, other, other_near, other_far, stay, come, whole)
    return whole.reshape(fields, levels, rows, cols), flux


def solution(mesh):
    in_specs = (
        P(None, None, "lat", "lon"),
        P(None, "lat", "lon"),
        P(),
        P(),
        P(),
        P(),
        P(),
        P("lat", "lon", None),
        P("lat"),
    )
    out_specs = (P(None, None, "lat", "lon"), P(None, "lat", "lon"))
    return jax.shard_map(
        on_device, mesh=mesh, in_specs=in_specs, out_specs=out_specs, check_vma=False
    )
```

time: 201 us -> 69.2 us (0.34)
  the two profiles are of different devices: /device:TPU:0 before, /device:TPU:6 now
where the time goes in v1:
time: 69.2 us; the launch traced here: 69 us
  Pallas kernels  35 us (51%)
  waiting for transfers between devices  22.8 us (33%)
  starting transfers between devices  7.7 us (11%)
  local copies, waits for them, and re-layouts  2.61 us (4%)
  between operations  0.9 us (1%)
    ppermute x8, waiting for transfers between devices, shifted(): lax.ppermute(value, axis, [(i, (i + steps) % count) for i in range(count)])  16.2 us
    pallas_call x3, Pallas kernels, advect(): pl.pallas_call(functools.partial(advect_kernel, first), out_shape=jax.Sha...  8.81 us
    pallas_call x1, Pallas kernels, inner(): pl.pallas_call(inner_kernel, out_shape=jax.ShapeDtypeStruct((3, levels, r...  8.69 us
    pallas_call x1, Pallas kernels, network(): pl.pallas_call(network_kernel, out_shape=(jax.ShapeDtypeStruct((3 * level...  8.57 us
    ppermute x2, waiting for transfers between devices, passed_along(): lax.ppermute(block, axis, [(i, i + distance) for i in devices if i + dist...  6.63 us
    pallas_call x3, Pallas kernels, relay(): pl.pallas_call(relay_kernel, out_shape=jax.ShapeDtypeStruct((pairs + 1, h...  4.07 us
    ppermute x2, starting transfers between devices, passed_along(): lax.ppermute(block, axis, [(i, i + distance) for i in devices if i + dist...  3.87 us
    ppermute x8, starting transfers between devices, shifted(): lax.ppermute(value, axis, [(i, (i + steps) % count) for i in range(count)])  3.82 us
  transfers between devices with their start and end apart: 10, of which 5 were waited for; matrix products, arithmetic and copies ran while one was open for 0% of the time, Pallas kernels for 32%

profile of v1, /device:TPU:6, one launch (start us, length us, event | category | flops | bytes accessed | tf_op | source)
XLA Modules:
  0.0 69.0 jit_solution(17545808571487729895)
XLA Ops:
  0.6 0.0 copy-start
  0.6 1.5 %copy-done = f32[8,60,8,128]{3,2,1,0:T(8,128)S(1)} copy-done((f32[8,60,8,128]{3,2,1,0:T(8,128)S(1)}, f32[8,60,8,128]{3,2,1,0:T(8,128)}, u32[]{:S(2)}) %copy-start) | copy-done | bytes 1966104
  2.2 0.1 shard_map.104
  2.3 2.6 %collective-permute-start = (bf16[45,16,128]{2,1,0:T(8,128)(2,1)S(1)}, bf16[45,16,128]{2,1,0:T(8,128)(2,1)S(1)}, u32[]{:S(2)}, u32[]{:S(2)}) collective-permute-start(bf16[45,16,128]{2,1,0:T(8,128)(2,1)S(1)} %get-tuple-element.17), channel_id=1, source_target_pairs={{8,0},{16,8},{24,16},{9,1},{17,9},{25,17},{10,2},{18,10},{26,18},{... | collective-permute-start | bytes 552968 | tf_op jit(solution)/shard_map/ppermute | solution.py:591
  4.9 1.3 %collective-permute-start.1 = (bf16[45,16,128]{2,1,0:T(8,128)(2,1)S(1)}, bf16[45,16,128]{2,1,0:T(8,128)(2,1)S(1)}, u32[]{:S(2)}, u32[]{:S(2)}) collective-permute-start(bf16[45,16,128]{2,1,0:T(8,128)(2,1)S(1)} %get-tuple-element.18), channel_id=1, source_target_pairs={{0,8},{8,16},{16,24},{1,9},{9,17},{17,25},{2,10},{10,18},{18,26},{... | collective-permute-start | bytes 552968 | tf_op jit(solution)/shard_map/ppermute | solution.py:591
  6.2 0.0 copy-done.1
  6.2 0.0 copy-done.4
  6.2 0.0 copy-start.2
  6.2 0.9 %copy-done.2 = bf16[76,8,128]{2,1,0:T(8,128)(2,1)S(1)} copy-done((bf16[76,8,128]{2,1,0:T(8,128)(2,1)S(1)}, bf16[76,8,128]{2,1,0:T(8,128)(2,1)}, u32[]{:S(2)}) %copy-start.2) | copy-done | bytes 155672
  7.1 0.8 %shard_map.107 = (bf16[556,1024]{1,0:T(8,128)(2,1)S(1)}, f32[8,128]{1,0:T(8,128)S(1)}) custom-call(f32[8,60,8,128]{3,2,1,0:T(8,128)S(1)} %copy-done.1, bf16[76,8,128]{2,1,0:T(8,128)(2,1)S(1)} %copy-done.2, s32[1,1024]{1,0:T(1,128)S(1)} %bitcast.7), custom_call_target="tpu_custom_call" | custom-call | flops 16777216 | bytes 4194304 | tf_op jit(solution)/shard_map/pallas_call | solution.py:212
  7.9 0.1 fusion
  8.0 0.8 %collective-permute-done.from_north_ref = bf16[45,16,128]{2,1,0:T(8,128)(2,1)S(1)} collective-permute-done((bf16[45,16,128]{2,1,0:T(8,128)(2,1)S(1)}, bf16[45,16,128]{2,1,0:T(8,128)(2,1)S(1)}, u32[]{:S(2)}, u32[]{:S(2)}) %collective-permute-start) | collective-permute-done | bytes 184352 | tf_op jit(solution)/shard_map/ppermute | solution.py:591
  8.7 5.8 %collective-permute-done.1.from_south_ref = bf16[45,16,128]{2,1,0:T(8,128)(2,1)S(1)} collective-permute-done((bf16[45,16,128]{2,1,0:T(8,128)(2,1)S(1)}, bf16[45,16,128]{2,1,0:T(8,128)(2,1)S(1)}, u32[]{:S(2)}, u32[]{:S(2)}) %collective-permute-start.1) | collective-permute-done | bytes 184352 | tf_op jit(solution)/shard_map/ppermute | solution.py:591
  14.6 1.1 %shard_map.106 = (bf16[36,16,128]{2,1,0:T(8,128)(2,1)S(1)}, bf16[36,16,128]{2,1,0:T(8,128)(2,1)S(1)}) custom-call(f32[8,60,8,128]{3,2,1,0:T(8,128)S(1)} %copy-done.1, bf16[45,16,128]{2,1,0:T(8,128)(2,1)S(1)} %collective-permute-done.from_north_ref, bf16[45,16,128]{2,1,0:T(8,128)(2,1)S(1)} %collective-permute-done.1.from_south_ref), custom_call_target="tpu_custom_call" | custom-call | flops 1048576 | bytes 4194304 | tf_op jit(solution)/shard_map/pallas_call | solution.py:123
  15.6 2.2 %collective-permute-start.2 = (bf16[36,16,128]{2,1,0:T(8,128)(2,1)S(1)}, bf16[36,16,128]{2,1,0:T(8,128)(2,1)S(1)}, u32[]{:S(2)}, u32[]{:S(2)}) collective-permute-start(bf16[36,16,128]{2,1,0:T(8,128)(2,1)S(1)} %get-tuple-element.19.own_west_ref), channel_id=1, source_target_pairs={{0,7},{1,0},{2,1},{3,2},{4,3},{5,4},{6,5},{7,6},{8,15},{9,8},{10,9... | collective-permute-start | bytes 442376 | tf_op jit(solution)/shard_map/ppermute | solution.py:586
  17.9 0.0 collective-permute-start.3
  17.9 0.0 copy-done.9
  17.9 0.0 copy-start.7
  17.9 0.0 copy-start.8
  18.0 8.7 %shard_map.105.inner_ref = f32[3,60,8,128]{3,2,1,0:T(8,128)S(1)} custom-call(f32[8,60,8,128]{3,2,1,0:T(8,128)S(1)} %copy-done.1, bf16[45,16,128]{2,1,0:T(8,128)(2,1)S(1)} %collective-permute-done.from_north_ref, bf16[45,16,128]{2,1,0:T(8,128)(2,1)S(1)} %collective-permute-done.1.from_south_ref), custom_call_target="tpu_custom_call" | custom-call | flops 16777216 | bytes 4194304 | tf_op jit(solution)/shard_map/pallas_call | solution.py:177
  26.7 0.0 collective-permute-done.2.from_east_ref
  26.7 0.0 collective-permute-done.3.from_west_ref
  26.7 0.0 copy-done.5
  26.7 0.0 copy-done.6
  26.7 0.0 copy-done.7
  26.7 0.0 copy-done.8
  26.7 8.6 %shard_map.108 = (f32[1440,128]{1,0:T(8,128)S(1)}, f32[60,8,128]{2,1,0:T(8,128)S(1)}, bf16[1024,640]{1,0:T(8,128)(2,1)S(1)}, bf16[60,16,128]{2,1,0:T(8,128)(2,1)S(1)}) custom-call(f32[3,60,8,128]{3,2,1,0:T(8,128)S(1)} %shard_map.105.inner_ref, bf16[36,16,128]{2,1,0:T(8,128)(2,1)S(1)} %get-tuple-element.19.own_west_ref, ...), custom_call_target="tpu_custom_call" | custom-call | flops 4294967296 | bytes 8388608 | tf_op jit(solution)/shard_map/pallas_call | solution.py:358
  35.3 0.0 copy-start.3
  35.3 0.1 collective-permute-start.6
  35.4 0.7 %shard_map.109.own_ref = bf16[60,16,128]{2,1,0:T(8,128)(2,1)S(1)} custom-call(bf16[1024,640]{1,0:T(8,128)(2,1)S(1)} %get-tuple-element.23.hidden_ref, bf16[120,640]{1,0:T(8,128)(2,1)S(1)} %get-tuple-element.35.five_ref, f32[8,128]{1,0:T(8,128)S(1)} %get-tuple-element.22.lit_ref, f32[120,8,128]{2,1,0:T(8,128)S(1)} %bitcast.5), custom_call_target="tpu_custom_call" | custom-call | flops 268435456 | bytes 3145728 | tf_op jit(solution)/shard_map/pallas_call | solution.py:392
  36.1 0.1 collective-permute-start.4
  36.2 1.2 %collective-permute-start.8 = (bf16[30,16,128]{2,1,0:T(8,128)(2,1)S(1)}, bf16[30,16,128]{2,1,0:T(8,128)(2,1)S(1)}, u32[]{:S(2)}, u32[]{:S(2)}) collective-permute-start(bf16[30,16,128]{2,1,0:T(8,128)(2,1)S(1)} %get-tuple-element.29.own_ref), channel_id=1, source_target_pairs={{0,1},{1,2},{2,3},{3,4},{4,5},{5,6},{6,7},{7,0},{8,9},{9,10},{10,1... | collective-permute-start | bytes 368648 | tf_op jit(solution)/shard_map/ppermute | solution.py:586
  37.4 5.4 %collective-permute-done.6.near_ref = bf16[60,16,128]{2,1,0:T(8,128)(2,1)S(1)} collective-permute-done((bf16[60,16,128]{2,1,0:T(8,128)(2,1)S(1)}, bf16[60,16,128]{2,1,0:T(8,128)(2,1)S(1)}, u32[]{:S(2)}, u32[]{:S(2)}) %collective-permute-start.6) | collective-permute-done | bytes 245792 | tf_op jit(solution)/shard_map/ppermute | solution.py:586
  42.8 1.5 %shard_map.112 = bf16[61,16,128]{2,1,0:T(8,128)(2,1)S(1)} custom-call(s32[8]{0:T(128)S(1)} %copy-done.3, bf16[60,16,128]{2,1,0:T(8,128)(2,1)S(1)} %get-tuple-element.28.own_ref, bf16[60,16,128]{2,1,0:T(8,128)(2,1)S(1)} %collective-permute-done.6.near_ref), custom_call_target="tpu_custom_call" | custom-call | flops 1048576 | bytes 1048576 | tf_op jit(solution)/shard_map/pallas_call | solution.py:507
  44.3 0.0 collective-permute-start.7
  44.4 1.1 %collective-permute-done.4.near_ref = bf16[60,16,128]{2,1,0:T(8,128)(2,1)S(1)} collective-permute-done((bf16[60,16,128]{2,1,0:T(8,128)(2,1)S(1)}, bf16[60,16,128]{2,1,0:T(8,128)(2,1)S(1)}, u32[]{:S(2)}, u32[]{:S(2)}) %collective-permute-start.4) | collective-permute-done | bytes 245792 | tf_op jit(solution)/shard_map/ppermute | solution.py:586
  45.4 1.5 %shard_map.110 = bf16[61,16,128]{2,1,0:T(8,128)(2,1)S(1)} custom-call(s32[8]{0:T(128)S(1)} %copy-done.3, bf16[60,16,128]{2,1,0:T(8,128)(2,1)S(1)} %shard_map.109.own_ref, bf16[60,16,128]{2,1,0:T(8,128)(2,1)S(1)} %collective-permute-done.4.near_ref), custom_call_target="tpu_custom_call" | custom-call | flops 1048576 | bytes 1048576 | tf_op jit(solution)/shard_map/pallas_call | solution.py:507
  46.9 0.0 collective-permute-start.5
  47.0 0.0 collective-permute-done.8.near_ref
  47.0 1.0 %shard_map.113 = bf16[31,16,128]{2,1,0:T(8,128)(2,1)S(1)} custom-call(s32[8]{0:T(128)S(1)} %copy-done.3, bf16[30,16,128]{2,1,0:T(8,128)(2,1)S(1)} %get-tuple-element.29.own_ref, bf16[30,16,128]{2,1,0:T(8,128)(2,1)S(1)} %collective-permute-done.8.near_ref), custom_call_target="tpu_custom_call" | custom-call | flops 1048576 | bytes 1048576 | tf_op jit(solution)/shard_map/pallas_call | solution.py:507
  48.0 0.2 collective-permute-start.9
  48.2 2.2 %shard_map.111 = (f32[480,8,128]{2,1,0:T(8,128)}, bf16[8,8,128]{2,1,0:T(8,128)(2,1)}, f32[60,8,128]{2,1,0:T(8,128)S(1)}, f32[60,8,128]{2,1,0:T(8,128)S(1)}) custom-call(bf16[1024,640]{1,0:T(8,128)(2,1)S(1)} %get-tuple-element.23.hidden_ref, bf16[128,640]{1,0:T(8,128)(2,1)S(1)} %pad_maximum_fusion.five_ref, f32[8,128]{1,0:T(8,128)S(1)} %get-tuple-element.22.lit_ref, ...), custom_call_target="tpu_custom_call" | custom-call | flops 268435456 | bytes 4194304 | tf_op jit(solution)/shard_map/pallas_call | solution.py:450
  50.5 9.7 %collective-permute-done.9.far_ref = bf16[31,16,128]{2,1,0:T(8,128)(2,1)S(1)} collective-permute-done((bf16[31,16,128]{2,1,0:T(8,128)(2,1)S(1)}, bf16[31,16,128]{2,1,0:T(8,128)(2,1)S(1)}, u32[]{:S(2)}, u32[]{:S(2)}) %collective-permute-start.9) | collective-permute-done | bytes 127008 | tf_op jit(solution)/shard_map/ppermute | solution.py:586
  60.2 2.3 %shard_map.114.whole_ref = f32[480,8,128]{2,1,0:T(8,128)} custom-call(s32[8]{0:T(128)S(1)} %copy-done.3, bf16[30,16,128]{2,1,0:T(8,128)(2,1)S(1)} %get-tuple-element.29.own_ref, bf16[30,16,128]{2,1,0:T(8,128)(2,1)S(1)} %collective-permute-done.8.near_ref, bf16[31,16,128]{2,1,0:T(8,128)(2,1)S(1)} %collective-permute-done.9.far_ref, ...), custom_call_target="tpu_custom_call", output_to_operand_aliasing={{}: (6, {})} | custom-call | flops 4194304 | bytes 3145728 | tf_op jit(solution)/shard_map/pallas_call | solution.py:569
  62.4 0.0 collective-permute-done.7.far_ref
  62.5 3.3 %shard_map.115.whole_ref = f32[480,8,128]{2,1,0:T(8,128)} custom-call(s32[8]{0:T(128)S(1)} %copy-done.3, bf16[60,16,128]{2,1,0:T(8,128)(2,1)S(1)} %get-tuple-element.28.own_ref, bf16[60,16,128]{2,1,0:T(8,128)(2,1)S(1)} %collective-permute-done.6.near_ref, bf16[61,16,128]{2,1,0:T(8,128)(2,1)S(1)} %collective-permute-done.7.far_ref, ...), custom_call_target="tpu_custom_call", output_to_operand_aliasing={{}: (6, {})} | custom-call | flops 4194304 | bytes 3145728 | tf_op jit(solution)/shard_map/pallas_call | solution.py:569
  65.7 0.0 collective-permute-done.5.far_ref
  65.7 3.3 %shard_map.116 = f32[480,8,128]{2,1,0:T(8,128)} custom-call(s32[8]{0:T(128)S(1)} %copy-done.3, bf16[60,16,128]{2,1,0:T(8,128)(2,1)S(1)} %shard_map.109.own_ref, bf16[60,16,128]{2,1,0:T(8,128)(2,1)S(1)} %collective-permute-done.4.near_ref, bf16[61,16,128]{2,1,0:T(8,128)(2,1)S(1)} %collective-permute-done.5.far_ref, ...), custom_call_target="tpu_custom_call", output_to_operand_aliasing={{}: (6, {})} | custom-call | flops 4194304 | bytes 3145728 | tf_op jit(solution)/shard_map/pallas_call | solution.py:569
  (9 shorter events, 0.1 us)
Async XLA Ops:
  0.6 1.5 %copy-start = (f32[8,60,8,128]{3,2,1,0:T(8,128)S(1)}, f32[8,60,8,128]{3,2,1,0:T(8,128)}, u32[]{:S(2)}) copy-start(f32[8,60,8,128]{3,2,1,0:T(8,128)} %state_ref.7) | copy-start | bytes 5898244
  2.2 4.0 %copy-start.1 = (f32[8,60,8,128]{3,2,1,0:T(8,128)S(1)}, f32[8,60,8,128]{3,2,1,0:T(8,128)}, u32[]{:S(2)}) copy-start(f32[8,60,8,128]{3,2,1,0:T(8,128)} %state_ref.7) | copy-start | bytes 5898244
  2.2 4.0 %copy-start.4 = (s32[1,1,1024]{2,1,0:T(1,128)S(1)}, s32[1,1,1024]{2,1,0:T(1,128)}, u32[]{:S(2)}) copy-start(s32[1,1,1024]{2,1,0:T(1,128)} %param.16) | copy-start | bytes 12292
  2.3 6.5 %collective-permute-start = (bf16[45,16,128]{2,1,0:T(8,128)(2,1)S(1)}, bf16[45,16,128]{2,1,0:T(8,128)(2,1)S(1)}, u32[]{:S(2)}, u32[]{:S(2)}) collective-permute-start(bf16[45,16,128]{2,1,0:T(8,128)(2,1)S(1)} %get-tuple-element.17), channel_id=1, source_target_pairs={{8,0},{16,8},{24,16},{9,1},{17,9},{25,17},{10,2},{18,10},{26,18},{... | collective-permute-start | bytes 552968 | tf_op jit(solution)/shard_map/ppermute | solution.py:591
  4.9 9.7 %collective-permute-start.1 = (bf16[45,16,128]{2,1,0:T(8,128)(2,1)S(1)}, bf16[45,16,128]{2,1,0:T(8,128)(2,1)S(1)}, u32[]{:S(2)}, u32[]{:S(2)}) collective-permute-start(bf16[45,16,128]{2,1,0:T(8,128)(2,1)S(1)} %get-tuple-element.18), channel_id=1, source_target_pairs={{0,8},{8,16},{16,24},{1,9},{9,17},{17,25},{2,10},{10,18},{18,26},{... | collective-permute-start | bytes 552968 | tf_op jit(solution)/shard_map/ppermute | solution.py:591
  6.2 0.9 %copy-start.2 = (bf16[76,8,128]{2,1,0:T(8,128)(2,1)S(1)}, bf16[76,8,128]{2,1,0:T(8,128)(2,1)}, u32[]{:S(2)}) copy-start(bf16[76,8,128]{2,1,0:T(8,128)(2,1)} %surface_ref.1) | copy-start | bytes 466948
  7.9 10.0 %copy-start.9 = (bf16[640,368]{0,1:T(8,128)(2,1)S(1)}, bf16[640,368]{0,1:T(8,128)(2,1)}, u32[]{:S(2)}) copy-start(bf16[640,368]{0,1:T(8,128)(2,1)} %param.15) | copy-start | bytes 1413124
  15.6 11.0 %collective-permute-start.2 = (bf16[36,16,128]{2,1,0:T(8,128)(2,1)S(1)}, bf16[36,16,128]{2,1,0:T(8,128)(2,1)S(1)}, u32[]{:S(2)}, u32[]{:S(2)}) collective-permute-start(bf16[36,16,128]{2,1,0:T(8,128)(2,1)S(1)} %get-tuple-element.19.own_west_ref), channel_id=1, source_target_pairs={{0,7},{1,0},{2,1},{3,2},{4,3},{5,4},{6,5},{7,6},{8,15},{9,8},{10,9... | collective-permute-start | bytes 442376 | tf_op jit(solution)/shard_map/ppermute | solution.py:586
  17.9 8.8 %collective-permute-start.3 = (bf16[36,16,128]{2,1,0:T(8,128)(2,1)S(1)}, bf16[36,16,128]{2,1,0:T(8,128)(2,1)S(1)}, u32[]{:S(2)}, u32[]{:S(2)}) collective-permute-start(bf16[36,16,128]{2,1,0:T(8,128)(2,1)S(1)} %get-tuple-element.20.own_east_ref), channel_id=1, source_target_pairs={{0,1},{1,2},{2,3},{3,4},{4,5},{5,6},{6,7},{7,0},{8,9},{9,10},{10,1... | collective-permute-start | bytes 442376 | tf_op jit(solution)/shard_map/ppermute | solution.py:586
  17.9 8.8 %copy-start.5 = (bf16[768,640]{1,0:T(8,128)(2,1)S(1)}, bf16[768,640]{1,0:T(8,128)(2,1)}, u32[]{:S(2)}) copy-start(bf16[768,640]{1,0:T(8,128)(2,1)} %two_ref.1) | copy-start | bytes 2949124
  17.9 8.8 %copy-start.6 = (bf16[556,768]{1,0:T(8,128)(2,1)S(1)}, bf16[556,768]{1,0:T(8,128)(2,1)}, u32[]{:S(2)}) copy-start(bf16[556,768]{1,0:T(8,128)(2,1)} %one_ref.1) | copy-start | bytes 2562052
  17.9 8.8 %copy-start.7 = (bf16[640,512]{1,0:T(8,128)(2,1)S(1)}, bf16[640,512]{1,0:T(8,128)(2,1)}, u32[]{:S(2)}) copy-start(bf16[640,512]{1,0:T(8,128)(2,1)} %three_ref.1) | copy-start | bytes 1966084
  17.9 8.8 %copy-start.8 = (bf16[512,640]{1,0:T(8,128)(2,1)S(1)}, bf16[512,640]{1,0:T(8,128)(2,1)}, u32[]{:S(2)}) copy-start(bf16[512,640]{1,0:T(8,128)(2,1)} %four_ref.1) | copy-start | bytes 1966084
  35.3 7.5 %copy-start.3 = (s32[8]{0:T(128)S(1)}, s32[8]{0:T(128)}, u32[]{:S(2)}) copy-start(s32[8]{0:T(128)} %offset_ref.11) | copy-start | bytes 100
  35.3 7.5 %collective-permute-start.6 = (bf16[60,16,128]{2,1,0:T(8,128)(2,1)S(1)}, bf16[60,16,128]{2,1,0:T(8,128)(2,1)S(1)}, u32[]{:S(2)}, u32[]{:S(2)}) collective-permute-start(bf16[60,16,128]{2,1,0:T(8,128)(2,1)S(1)} %get-tuple-element.28.own_ref), channel_id=1, source_target_pairs={{0,1},{1,2},{2,3},{3,4},{4,5},{5,6},{6,7},{7,0},{8,9},{9,10},{10,1... | collective-permute-start | bytes 737288 | tf_op jit(solution)/shard_map/ppermute | solution.py:586
  36.1 9.3 %collective-permute-start.4 = (bf16[60,16,128]{2,1,0:T(8,128)(2,1)S(1)}, bf16[60,16,128]{2,1,0:T(8,128)(2,1)S(1)}, u32[]{:S(2)}, u32[]{:S(2)}) collective-permute-start(bf16[60,16,128]{2,1,0:T(8,128)(2,1)S(1)} %shard_map.109.own_ref), channel_id=1, source_target_pairs={{0,1},{1,2},{2,3},{3,4},{4,5},{5,6},{6,7},{7,0},{8,9},{9,10},{10,1... | collective-permute-start | bytes 737288 | tf_op jit(solution)/shard_map/ppermute | solution.py:586
  36.2 10.8 %collective-permute-start.8 = (bf16[30,16,128]{2,1,0:T(8,128)(2,1)S(1)}, bf16[30,16,128]{2,1,0:T(8,128)(2,1)S(1)}, u32[]{:S(2)}, u32[]{:S(2)}) collective-permute-start(bf16[30,16,128]{2,1,0:T(8,128)(2,1)S(1)} %get-tuple-element.29.own_ref), channel_id=1, source_target_pairs={{0,1},{1,2},{2,3},{3,4},{4,5},{5,6},{6,7},{7,0},{8,9},{9,10},{10,1... | collective-permute-start | bytes 368648 | tf_op jit(solution)/shard_map/ppermute | solution.py:586
  44.3 18.1 %collective-permute-start.7 = (bf16[61,16,128]{2,1,0:T(8,128)(2,1)S(1)}, bf16[61,16,128]{2,1,0:T(8,128)(2,1)S(1)}, u32[]{:S(2)}, u32[]{:S(2)}) collective-permute-start(bf16[61,16,128]{2,1,0:T(8,128)(2,1)S(1)} %shard_map.112), channel_id=1, source_target_pairs={{0,2},{1,3},{2,4},{3,5},{4,6},{5,7},{6,0},{7,1},{8,10},{9,11},{10,... | collective-permute-start | bytes 749576 | tf_op jit(solution)/shard_map/ppermute | solution.py:586
  46.9 18.8 %collective-permute-start.5 = (bf16[61,16,128]{2,1,0:T(8,128)(2,1)S(1)}, bf16[61,16,128]{2,1,0:T(8,128)(2,1)S(1)}, u32[]{:S(2)}, u32[]{:S(2)}) collective-permute-start(bf16[61,16,128]{2,1,0:T(8,128)(2,1)S(1)} %shard_map.110), channel_id=1, source_target_pairs={{0,2},{1,3},{2,4},{3,5},{4,6},{5,7},{6,0},{7,1},{8,10},{9,11},{10,... | collective-permute-start | bytes 749576 | tf_op jit(solution)/shard_map/ppermute | solution.py:586
  48.0 12.1 %collective-permute-start.9 = (bf16[31,16,128]{2,1,0:T(8,128)(2,1)S(1)}, bf16[31,16,128]{2,1,0:T(8,128)(2,1)S(1)}, u32[]{:S(2)}, u32[]{:S(2)}) collective-permute-start(bf16[31,16,128]{2,1,0:T(8,128)(2,1)S(1)} %shard_map.113), channel_id=1, source_target_pairs={{0,2},{1,3},{2,4},{3,5},{4,6},{5,7},{6,0},{7,1},{8,10},{9,11},{10,... | collective-permute-start | bytes 380936 | tf_op jit(solution)/shard_map/ppermute | solution.py:586

commit v2 on v1

--- a/solution.py
+++ b/solution.py
@@ -7,6 +7,7 @@
 from jax.experimental.pallas import tpu as pltpu
 from jax.sharding import PartitionSpec as P
 
+
 SUBSTEPS = 4
 SOUND_COURANT = 0.6
 PHYSICS_STEP = 0.5
@@ -41,93 +42,128 @@
     return (size - shift) % size
 
 
-def pack_rows_kernel(state_ref, south_ref, north_ref, ozone_ref):
-    levels = 3 * state_ref.shape[1]
-    rows, cols = state_ref.shape[2:]
-    low = iota((rows, cols), 0) < rows // 2
-    flat = state_ref.reshape(state_ref.shape[0] * state_ref.shape[1], rows, cols)
-
-    def body(step, carry):
-        block = flat[pl.ds(step * 20, 20)].reshape(10, 2, rows, cols)
-        even = block[:, 0]
-        odd = pltpu.roll(block[:, 1], rows // 2, 1)
-        south = jnp.where(low, even, odd)
-        north = jnp.where(low, odd, even)
-        south_ref[pl.ds(step * 5, 5)] = south.reshape(5, 2 * rows, cols).astype(BF16)
-        north_ref[pl.ds(step * 5, 5)] = north.reshape(5, 2 * rows, cols).astype(BF16)
-        return carry
-
-    lax.fori_loop(0, levels // 20, body, 0)
-    count = state_ref.shape[1]
-    last = state_ref[state_ref.shape[0] - 1]
-    ozone_ref[...] = last.reshape(count // 2, 2 * rows, cols).astype(BF16)
-
-
-def pack_rows(state):
-    fields, levels, rows, cols = state.shape
-    half = jax.ShapeDtypeStruct((3 * levels // 4, 2 * rows, cols), BF16)
-    return pl.pallas_call(
-        pack_rows_kernel,
-        out_shape=(half, half, jax.ShapeDtypeStruct((levels // 2, 2 * rows, cols), BF16)),
-        in_specs=[vmem()],
-        out_specs=(vmem(), vmem(), vmem()),
-        compiler_params=params(8),
-        cost_estimate=cost(1 << 20, 4 << 20),
-    )(state)
+def paired(tiles, rows, low):
+    tiles = tiles.reshape((tiles.shape[0] // 2, 2) + tiles.shape[1:])
+    even = tiles[:, 0]
+    odd = pltpu.roll(tiles[:, 1], rows // 2, 1)
+    return jnp.where(low, even, odd), jnp.where(low, odd, even)
 
 
 def halo_rows(north_pair, south_pair, low):
     even = jnp.where(low, north_pair, south_pair)
     odd = pltpu.roll(jnp.where(low, south_pair, north_pair), north_pair.shape[-2] // 2, 1)
-    return even, odd
-
-
-def pack_cols_kernel(state_ref, from_north_ref, from_south_ref, west_ref, east_ref):
-    levels = state_ref.shape[1]
-    rows, cols = state_ref.shape[2:]
-    per = cols // STRIP
+    return jnp.stack([even, odd], axis=1).reshape((-1,) + even.shape[1:])
+
+
+def side_packs(tiles, lane):
+    per = tiles.shape[-1] // STRIP
+    west_packs, east_packs = [], []
+    for pack in range(tiles.shape[0] // per):
+        west = jnp.zeros(tiles.shape[1:], F32)
+        east = jnp.zeros(tiles.shape[1:], F32)
+        for slot in range(per):
+            tile = tiles[pack * per + slot]
+            start = slot * STRIP
+            inside = (lane >= start) & (lane < start + STRIP)
+            west = jnp.where(inside, pltpu.roll(tile, start + 2 * SUBSTEPS, 1), west)
+            east = jnp.where(inside, pltpu.roll(tile, start + 4 * SUBSTEPS, 1), east)
+        west_packs.append(west)
+        east_packs.append(east)
+    return jnp.stack(west_packs), jnp.stack(east_packs)
+
+
+def tall(tiles):
+    count, rows, cols = tiles.shape
+    return tiles.reshape(count // 2, 2 * rows, cols).astype(BF16)
+
+
+def messages_kernel(
+    state_ref, south_ref, north_ref, west_ref, east_ref, ozone_ref, held, sems
+):
+    fields, levels, rows, cols = state_ref.shape
     low = iota((rows, cols), 0) < rows // 2
-    lane = iota((2 * rows, cols), 1)
-    flat = state_ref.reshape(state_ref.shape[0] * levels, rows, cols)
+    lane = iota((rows, cols), 1)
+    copies = []
+    for place, field in enumerate((0, 1, 2, fields - 1)):
+        copy = pltpu.make_async_copy(
+            state_ref.at[field], held.at[pl.ds(place * levels, levels)], sems.at[place]
+        )
+        copy.start()
+        copies.append(copy)
 
     def body(step, carry):
-        own = flat[pl.ds(step * 20, 20)]
-        north = from_north_ref[pl.ds(step * 5, 5)].astype(F32).reshape(10, rows, cols)
-        south = from_south_ref[pl.ds(step * 5, 5)].astype(F32).reshape(10, rows, cols)
-        even, odd = halo_rows(north, south, low)
-        west_out, east_out = [], []
-        for pack in range(4):
-            west = jnp.zeros((2 * rows, cols), F32)
-            east = jnp.zeros((2 * rows, cols), F32)
-            for slot in range(per):
-                level = pack * per + slot
-                side = (odd if level % 2 else even)[level // 2]
-                tile = jnp.concatenate([own[level], side], axis=0)
-                start = slot * STRIP
-                inside = (lane >= start) & (lane < start + STRIP)
-                west = jnp.where(inside, pltpu.roll(tile, start + 2 * SUBSTEPS, 1), west)
-                east = jnp.where(inside, pltpu.roll(tile, start + 4 * SUBSTEPS, 1), east)
-            west_out.append(west)
-            east_out.append(east)
-        west_ref[pl.ds(step * 4, 4)] = jnp.stack(west_out).astype(BF16)
-        east_ref[pl.ds(step * 4, 4)] = jnp.stack(east_out).astype(BF16)
+        tiles = held[pl.ds(step * 20, 20)]
+        south, north = paired(tiles, rows, low)
+        south_ref[pl.ds(step * 5, 5)] = tall(south)
+        north_ref[pl.ds(step * 5, 5)] = tall(north)
+        west, east = side_packs(tiles, lane)
+        west_ref[pl.ds(step * 2, 2)] = tall(west)
+        east_ref[pl.ds(step * 2, 2)] = tall(east)
         return carry
 
-    lax.fori_loop(0, 3 * levels // 20, body, 0)
-
-
-def pack_cols(state, from_north, from_south):
-    fields, levels, rows, cols = state.shape
+    for place in range(3):
+        copies[place].wait()
+        lax.fori_loop(
+            place * levels // 20, (place + 1) * levels // 20, body, 0, unroll=levels // 20
+        )
+    copies[3].wait()
+    ozone_ref[...] = tall(held[3 * levels :])
+
+
+def messages(state):
+    _, levels, rows, cols = state.shape
+
+    def shape(count):
+        return jax.ShapeDtypeStruct((count // 2, 2 * rows, cols), BF16)
+
     packs = 3 * levels // (cols // STRIP)
-    strip = jax.ShapeDtypeStruct((packs, 2 * rows, cols), BF16)
-    return pl.pallas_call(
-        pack_cols_kernel,
-        out_shape=(strip, strip),
-        in_specs=[vmem()] * 3,
-        out_specs=(vmem(), vmem()),
-        compiler_params=params(8),
+    return pl.pallas_call(
+        messages_kernel,
+        out_shape=(shape(3 * levels // 2),) * 2
+        + (shape(packs),) * 2
+        + (shape(levels),),
+        in_specs=[pl.BlockSpec(memory_space=pltpu.HBM)],
+        out_specs=(vmem(),) * 5,
+        scratch_shapes=[
+            pltpu.VMEM((4 * levels, rows, cols), F32),
+            pltpu.SemaphoreType.DMA((4,)),
+        ],
+        compiler_params=pltpu.CompilerParams(vmem_limit_bytes=125 << 19),
         cost_estimate=cost(1 << 20, 4 << 20),
-    )(state, from_north, from_south)
+    )(state)
+
+
+def short(ref, at, size):
+    rows, cols = ref.shape[1] // 2, ref.shape[2]
+    return ref[pl.ds(at // 2, size // 2)].astype(F32).reshape(size, rows, cols)
+
+
+def strips_kernel(own_west_ref, own_east_ref, from_east_ref, from_west_ref, out_ref, south_ref, north_ref):
+    count = 2 * own_west_ref.shape[0]
+    rows, cols = own_west_ref.shape[1] // 2, own_west_ref.shape[2]
+    place = iota((rows, cols), 1) % STRIP
+    low = iota((rows, cols), 0) < rows // 2
+    value = short(own_east_ref, 0, count)
+    value = jnp.where(place < 4 * SUBSTEPS, short(from_west_ref, 0, count), value)
+    value = jnp.where(place < 3 * SUBSTEPS, short(from_east_ref, 0, count), value)
+    value = jnp.where(place < 2 * SUBSTEPS, short(own_west_ref, 0, count), value)
+    out_ref[...] = value
+    south, north = paired(value, rows, low)
+    south_ref[...] = tall(south)
+    north_ref[...] = tall(north)
+
+
+def strips_of(own_west, own_east, from_east, from_west):
+    count, height, cols = own_west.shape
+    half = jax.ShapeDtypeStruct((count // 2, height, cols), BF16)
+    return pl.pallas_call(
+        strips_kernel,
+        out_shape=(jax.ShapeDtypeStruct((2 * count, height // 2, cols), F32), half, half),
+        in_specs=[vmem()] * 4,
+        out_specs=(vmem(),) * 3,
+        compiler_params=params(4),
+        cost_estimate=cost(1 << 20, 1 << 20),
+    )(own_west, own_east, from_east, from_west)
 
 
 def open_rows(rows, cols):
@@ -154,32 +190,25 @@
     rows, cols = state_ref.shape[2:]
     low = iota((rows, cols), 0) < rows // 2
     free = open_rows(rows, cols)
-
-    def body(step, carry):
-        parts = []
-        for field in range(3):
-            own = state_ref[field, pl.ds(step * 4, 4)]
-            at = field * (levels // 4) + step
-            north = from_north_ref[at].astype(F32).reshape(2, rows, cols)
-            south = from_south_ref[at].astype(F32).reshape(2, rows, cols)
-            even, odd = halo_rows(north, south, low)
-            side = jnp.stack([even[0], odd[0], even[1], odd[1]])
-            parts.append(jnp.concatenate([own, side], axis=1))
-        for field, value in enumerate(substeps(*parts, free)):
-            out_ref[field, pl.ds(step * 4, 4)] = value[:, :rows]
-        return carry
-
-    lax.fori_loop(0, levels // 4, body, 0)
+    parts = []
+    for field in range(3):
+        at = pl.ds(field * (levels // 4), levels // 4)
+        north = from_north_ref[at].astype(F32).reshape(levels // 2, rows, cols)
+        south = from_south_ref[at].astype(F32).reshape(levels // 2, rows, cols)
+        side = halo_rows(north, south, low)
+        parts.append(jnp.concatenate([state_ref[field], side], axis=1))
+    for field, value in enumerate(substeps(*parts, free)):
+        out_ref[field] = value[:, :rows]
 
 
 def inner(state, from_north, from_south):
-    fields, levels, rows, cols = state.shape
+    _, levels, rows, cols = state.shape
     return pl.pallas_call(
         inner_kernel,
         out_shape=jax.ShapeDtypeStruct((3, levels, rows, cols), F32),
         in_specs=[vmem()] * 3,
         out_specs=vmem(),
-        compiler_params=params(8),
+        compiler_params=params(16),
         cost_estimate=cost(1 << 24, 4 << 20),
     )(state, from_north, from_south)
 
@@ -250,11 +279,11 @@
 
 
 def network_kernel(
+    parts_count,
     inner_ref,
-    own_west_ref,
-    own_east_ref,
-    from_east_ref,
-    from_west_ref,
+    here_ref,
+    north_ref,
+    south_ref,
     rest_ref,
     one_ref,
     two_ref,
@@ -271,35 +300,18 @@
     spread,
     features,
 ):
-    fields, levels, rows, cols = inner_ref.shape
+    _, levels, rows, cols = inner_ref.shape
     per = cols // STRIP
     packs = levels // per
-    place = iota((2 * rows, cols), 1) % STRIP
+    low = iota((rows, cols), 0) < rows // 2
     free = open_rows(rows, cols)
-
-    def side(step, carry):
-        parts = []
-        for field in range(3):
-            at = pl.ds(field * packs + step * 4, 4)
-            value = jnp.where(
-                place < 2 * SUBSTEPS,
-                own_west_ref[at].astype(F32),
-                jnp.where(
-                    place < 3 * SUBSTEPS,
-                    from_east_ref[at].astype(F32),
-                    jnp.where(
-                        place < 4 * SUBSTEPS,
-                        from_west_ref[at].astype(F32),
-                        own_east_ref[at].astype(F32),
-                    ),
-                ),
-            )
-            parts.append(value)
-        for field, value in enumerate(substeps(*parts, free)):
-            strips[field, pl.ds(step * 4, 4)] = value[:, :rows]
-        return carry
-
-    lax.fori_loop(0, packs // 4, side, 0)
+    parts = []
+    for field in range(3):
+        half = [short(ref, field * packs // 2, packs // 2) for ref in (north_ref, south_ref)]
+        here = here_ref[pl.ds(field * packs, packs)]
+        parts.append(jnp.concatenate([here, halo_rows(*half, low)], axis=1))
+    for field, value in enumerate(substeps(*parts, free)):
+        strips[field] = value[:, :rows]
     lane = iota((rows, cols), 1)
 
     def merge(step, carry):
@@ -317,7 +329,7 @@
                     upwind_ref[level] = pltpu.roll(jnp.where(lane == cols - 1, west, value), 1, 1)
         return carry
 
-    lax.fori_loop(0, packs, merge, 0)
+    lax.fori_loop(0, packs, merge, 0, unroll=4)
     count = 3 * levels
     features[...] = rest_ref[...]
     for row in range(rows):
@@ -325,9 +337,9 @@
             pl.ds(row, count, stride=rows), :
         ].astype(BF16)
     total = rows * cols
-    chunk = total // 2
-
-    for part in range(2):
+    chunk = total // parts_count
+
+    for part in range(parts_count):
         at = part * chunk
         hidden = leaky(
             lax.dot_general(
@@ -340,30 +352,29 @@
         for weight in (two_ref, three_ref, four_ref):
             hidden = leaky(jnp.dot(hidden, weight[...], preferred_element_type=F32))
         hidden_ref[at : at + chunk] = hidden
-    size = five_ref.shape[0]
     tracer_update(
         five_ref[...],
         hidden_ref[...],
         lit_ref[...],
-        lambda step: state_ref[pl.ds(step * 10, 10)],
+        lambda step: state_ref[pl.ds(3 * levels + step * 10, 10)],
         tracer_ref,
         spread,
     )
 
 
-def network(inner_out, strips, rest, layers, five, lit, tracers):
-    fields, levels, rows, cols = inner_out.shape
+def network(inner_out, strips, rest, layers, five, lit, tracers, parts_count=2):
+    _, levels, rows, cols = inner_out.shape
     count = five.shape[0]
     width = layers[3].shape[1]
     return pl.pallas_call(
-        network_kernel,
+        functools.partial(network_kernel, parts_count),
         out_shape=(
             jax.ShapeDtypeStruct((3 * levels * rows, cols), F32),
             jax.ShapeDtypeStruct((levels, rows, cols), F32),
             jax.ShapeDtypeStruct((rows * cols, width), BF16),
             jax.ShapeDtypeStruct((count // 2, 2 * rows, cols), BF16),
         ),
-        in_specs=[vmem()] * 13,
+        in_specs=[vmem()] * 12,
         out_specs=(vmem(),) * 4,
         scratch_shapes=[
             pltpu.VMEM((3, levels * STRIP // (cols - cols % STRIP), rows, cols), F32),
@@ -375,22 +386,22 @@
     )(inner_out, *strips, rest, *layers, five, lit, tracers)
 
 
-def second_kernel(hidden_ref, five_ref, lit_ref, state_ref, tracer_ref, spread):
+def second_kernel(start, hidden_ref, five_ref, lit_ref, state_ref, tracer_ref, spread):
     tracer_update(
         five_ref[...],
         hidden_ref[...],
         lit_ref[...],
-        lambda step: state_ref[pl.ds(step * 10, 10)],
+        lambda step: state_ref[pl.ds(start + step * 10, 10)],
         tracer_ref,
         spread,
     )
 
 
-def second(hidden, five, lit, tracers):
+def second(start, hidden, five, lit, tracers):
     rows, cols = lit.shape
     count = five.shape[0]
     return pl.pallas_call(
-        second_kernel,
+        functools.partial(second_kernel, start),
         out_shape=jax.ShapeDtypeStruct((count // 2, 2 * rows, cols), BF16),
         in_specs=[vmem()] * 4,
         out_specs=vmem(),
@@ -515,7 +526,7 @@
 
 
 def advect_kernel(
-    first, offset_ref, own_ref, near_ref, far_ref, stay_ref, come_ref, whole_ref, out_ref, result, sem
+    first, group, offset_ref, own_ref, near_ref, far_ref, stay_ref, come_ref, whole_ref, out_ref, result, sem
 ):
     levels, rows, cols = stay_ref.shape
     pairs = own_ref.shape[0]
@@ -526,27 +537,27 @@
     index_less = (lane - cells - 1) & (cols - 1)
     column = far_ref[pairs].astype(F32)[:rows]
     is_zero, is_one, is_two = blocks == 0, blocks == 1, blocks >= 2
-    steps = levels // 10
+    steps = levels // group
     copies = []
     for field in range(2 * pairs // levels):
         def body(step, carry):
-            at = pl.ds(field * (levels // 2) + step * 5, 5)
-            own = own_ref[at].astype(F32).reshape(10, rows, cols)
-            near = near_ref[at].astype(F32).reshape(10, rows, cols)
-            far = far_ref[at].astype(F32).reshape(10, rows, cols)
-            stay = stay_ref[pl.ds(step * 10, 10)]
-            come = come_ref[pl.ds(step * 10, 10)]
+            at = pl.ds(field * (levels // 2) + step * (group // 2), group // 2)
+            own = own_ref[at].astype(F32).reshape(group, rows, cols)
+            near = near_ref[at].astype(F32).reshape(group, rows, cols)
+            far = far_ref[at].astype(F32).reshape(group, rows, cols)
+            stay = stay_ref[pl.ds(step * group, group)]
+            come = come_ref[pl.ds(step * group, group)]
             right = jnp.where(is_zero, own, jnp.where(is_one, near, far))
             left = jnp.where(is_zero, near, far)
             merged = jnp.where(from_right, right, left)
-            for level in range(10):
-                which = field * levels + step * 10 + level
+            for level in range(group):
+                which = field * levels + step * group + level
                 lone = along(column, jnp.zeros((rows, cols), jnp.int32) + which)
                 edge = jnp.where(is_two, lone, left[level])
                 shifted = jnp.where(lane == cols - 1 - cells, edge, merged[level])
                 here = along(merged[level], index)
                 behind = along(shifted, index_less)
-                result[field * levels + step * 10 + level] = (
+                result[field * levels + step * group + level] = (
                     stay[level] * here + come[level] * behind
                 )
             return carry
@@ -563,11 +574,11 @@
         copy.wait()
 
 
-def advect(first, offset, own, near, far, stay, come, whole):
+def advect(first, offset, own, near, far, stay, come, whole, group=20):
     pairs, height, cols = own.shape
     levels = stay.shape[0]
     return pl.pallas_call(
-        functools.partial(advect_kernel, first),
+        functools.partial(advect_kernel, first, group),
         out_shape=jax.ShapeDtypeStruct(whole.shape, F32),
         in_specs=[pl.BlockSpec(memory_space=pltpu.SMEM)] + [vmem()] * 5 + [any_space()],
         out_specs=any_space(),
@@ -604,14 +615,30 @@
     lit_columns,
     row_offset,
 ):
+    return tile_step(
+        state,
+        surface,
+        (layer_one, layer_two, layer_three, layer_four),
+        layer_five,
+        lit_columns,
+        row_offset,
+    )
+
+
+def tile_step(state, surface, layers, layer_five, lit_columns, row_offset):
     fields, levels, rows, cols = state.shape
     slots = lit_columns.reshape(1, rows * cols)
     flat = state.reshape(fields * levels, rows, cols)
 
-    to_south, to_north, ozone = pack_rows(state)
+    to_south, to_north, to_west, to_east, ozone = messages(state)
+    from_east = shifted(to_west, "lon", -1)
+    from_west = shifted(to_east, "lon", 1)
+    from_south = shifted(to_north, "lat", 1)
     from_north = passed_along(to_south, "lat", -1)
-    from_south = passed_along(to_north, "lat", 1)
     ozone_near = shifted(ozone, "lon", 1)
+    strips, strips_south, strips_north = strips_of(to_west, to_east, from_east, from_west)
+    strips_from_south = shifted(strips_north, "lat", 1)
+    strips_from_north = passed_along(strips_south, "lat", -1)
 
     rest, lit = rest_features(state, surface, slots)
     five = layer_five.T
@@ -619,28 +646,29 @@
     five_second = five[4 * levels : 6 * levels]
     five_winds = jnp.concatenate([five[: 2 * levels], five[6 * levels :]], axis=0)
 
-    to_west, to_east = pack_cols(state, from_north, from_south)
-    from_east = shifted(to_west, "lon", -1)
-    from_west = shifted(to_east, "lon", 1)
     inner_out = inner(state, from_north, from_south)
-    ozone_far = shifted(relay(row_offset, ozone, ozone_near), "lon", 2)
-
+    ozone_relay = relay(row_offset, ozone, ozone_near)
+    ozone_far = shifted(ozone_relay, "lon", 2)
     winds, upwind, hidden, first = network(
         inner_out,
-        (to_west, to_east, from_east, from_west),
+        (strips, strips_from_north, strips_from_south),
         rest,
-        (layer_one, layer_two, layer_three, layer_four),
+        layers,
         five_first,
         lit,
-        flat[3 * levels : 5 * levels],
+        flat,
     )
     first_near = shifted(first, "lon", 1)
-    other = second(hidden, five_second, lit, flat[5 * levels : 7 * levels])
+    other = second(5 * levels, hidden, five_second, lit, flat)
     other_near = shifted(other, "lon", 1)
-    first_far = shifted(relay(row_offset, first, first_near), "lon", 2)
-    other_far = shifted(relay(row_offset, other, other_near), "lon", 2)
+    first_relay = relay(row_offset, first, first_near)
+    first_far = shifted(first_relay, "lon", 2)
+    other_relay = relay(row_offset, other, other_near)
+    other_far = shifted(other_relay, "lon", 2)
     whole, flux, stay, come = winds_out(hidden, five_winds, lit, winds, upwind, fields)
-    whole = advect(7, row_offset, ozone, ozone_near, ozone_far, stay, come, whole)
+    whole = advect(
+        fields - 1, row_offset, ozone, ozone_near, ozone_far, stay, come, whole
+    )
     whole = advect(3, row_offset, first, first_near, first_far, stay, come, whole)
     whole = advect(5, row_offset, other, other_near, other_far, stay, come, whole)
     return whole.reshape(fields, levels, rows, cols), flux

time: 69.2 us -> 62.5 us (0.903)
  the two profiles are of different devices: /device:TPU:6 before, /device:TPU:0 now
where the time goes in v2:
time: 62.5 us; the launch traced here: 62.2 us
  Pallas kernels  25 us (40%)
  waiting for transfers between devices  19.2 us (31%)
  starting transfers between devices  12.8 us (20%)
  local copies, waits for them, and re-layouts  4.15 us (7%)
  between operations  0.94 us (2%)
    ppermute x10, waiting for transfers between devices, shifted(): lax.ppermute(value, axis, [(i, (i + steps) % count) for i in range(count)])  19.2 us
    ppermute x10, starting transfers between devices, shifted(): lax.ppermute(value, axis, [(i, (i + steps) % count) for i in range(count)])  10.2 us
    pallas_call x3, Pallas kernels, advect(): pl.pallas_call(functools.partial(advect_kernel, first, group), out_shape=...  6.96 us
    pallas_call x1, Pallas kernels, network(): pl.pallas_call(functools.partial(network_kernel, parts_count), out_shape=...  6.84 us
    unnamed x26, local copies, waits for them, and re-layouts  4.1 us
    pallas_call x3, Pallas kernels, relay(): pl.pallas_call(relay_kernel, out_shape=jax.ShapeDtypeStruct((pairs + 1, h...  4.07 us
    ppermute x2, starting transfers between devices, passed_along(): lax.ppermute(block, axis, [(i, i + distance) for i in devices if i + dist...  2.57 us
    pallas_call x1, Pallas kernels, messages(): pl.pallas_call(messages_kernel, out_shape=(shape(3 * levels // 2),) * 2 +...  2.26 us
  transfers between devices with their start and end apart: 12, of which 4 were waited for; matrix products, arithmetic and copies ran while one was open for 0% of the time, Pallas kernels for 22%

profile of v2, /device:TPU:0, one launch (start us, length us, event | category | flops | bytes accessed | tf_op | source)
XLA Modules:
  0.0 62.2 jit_solution(16342621896273468836)
XLA Ops:
  0.7 2.3 %shard_map.104 = (bf16[45,16,128]{2,1,0:T(8,128)(2,1)}, bf16[45,16,128]{2,1,0:T(8,128)(2,1)}, bf16[18,16,128]{2,1,0:T(8,128)(2,1)}, bf16[18,16,128]{2,1,0:T(8,128)(2,1)}, bf16[30,16,128]{2,1,0:T(8,128)(2,1)}) custom-call(f32[8,60,8,128]{3,2,1,0:T(8,128)} %state_ref.5), custom_call_target="tpu_custom_call" | custom-call | flops 1048576 | bytes 4194304 | tf_op jit(solution)/shard_map/pallas_call | solution.py:120
  2.9 4.6 %collective-permute-start.2 = (bf16[18,16,128]{2,1,0:T(8,128)(2,1)}, bf16[18,16,128]{2,1,0:T(8,128)(2,1)S(1)}, u32[]{:S(2)}, u32[]{:S(2)}) collective-permute-start(bf16[18,16,128]{2,1,0:T(8,128)(2,1)} %get-tuple-element.22.own_west_ref), channel_id=1, source_target_pairs={{0,7},{1,0},{2,1},{3,2},{4,3},{5,4},{6,5},{7,6},{8,15},{9,8},{10,9... | collective-permute-start | bytes 221192 | tf_op jit(solution)/shard_map/ppermute | solution.py:597
  7.5 0.0 collective-permute-start.3
  7.5 1.3 %collective-permute-start = (bf16[45,16,128]{2,1,0:T(8,128)(2,1)}, bf16[45,16,128]{2,1,0:T(8,128)(2,1)S(1)}, u32[]{:S(2)}, u32[]{:S(2)}) collective-permute-start(bf16[45,16,128]{2,1,0:T(8,128)(2,1)} %get-tuple-element.20), channel_id=1, source_target_pairs={{8,0},{16,8},{24,16},{9,1},{17,9},{25,17},{10,2},{18,10},{26,18},{... | collective-permute-start | bytes 552968 | tf_op jit(solution)/shard_map/ppermute | solution.py:602
  8.8 2.7 %collective-permute-start.1 = (bf16[45,16,128]{2,1,0:T(8,128)(2,1)}, bf16[45,16,128]{2,1,0:T(8,128)(2,1)S(1)}, u32[]{:S(2)}, u32[]{:S(2)}) collective-permute-start(bf16[45,16,128]{2,1,0:T(8,128)(2,1)} %get-tuple-element.21), channel_id=1, source_target_pairs={{0,8},{8,16},{16,24},{24,0},{1,9},{9,17},{17,25},{25,1},{2,10},{10... | collective-permute-start | bytes 552968 | tf_op jit(solution)/shard_map/ppermute | solution.py:597
  11.5 0.0 collective-permute-done.2.from_east_ref
  11.5 1.8 %collective-permute-done.3.from_west_ref = bf16[18,16,128]{2,1,0:T(8,128)(2,1)S(1)} collective-permute-done((bf16[18,16,128]{2,1,0:T(8,128)(2,1)}, bf16[18,16,128]{2,1,0:T(8,128)(2,1)S(1)}, u32[]{:S(2)}, u32[]{:S(2)}) %collective-permute-start.3) | collective-permute-done | bytes 73760 | tf_op jit(solution)/shard_map/ppermute | solution.py:597
  13.3 0.9 %copy-done.4 = bf16[18,16,128]{2,1,0:T(8,128)(2,1)S(1)} copy-done((bf16[18,16,128]{2,1,0:T(8,128)(2,1)S(1)}, bf16[18,16,128]{2,1,0:T(8,128)(2,1)}, u32[]{:S(2)}) %copy-start.4) | copy-done | bytes 73752
  14.2 0.9 %copy-done.5 = bf16[18,16,128]{2,1,0:T(8,128)(2,1)S(1)} copy-done((bf16[18,16,128]{2,1,0:T(8,128)(2,1)S(1)}, bf16[18,16,128]{2,1,0:T(8,128)(2,1)}, u32[]{:S(2)}) %copy-start.5) | copy-done | bytes 73752
  15.1 0.1 shard_map.106
  15.1 1.3 %collective-permute-start.4 = (bf16[9,16,128]{2,1,0:T(8,128)(2,1)S(1)}, bf16[9,16,128]{2,1,0:T(8,128)(2,1)S(1)}, u32[]{:S(2)}, u32[]{:S(2)}) collective-permute-start(bf16[9,16,128]{2,1,0:T(8,128)(2,1)S(1)} %get-tuple-element.25), channel_id=1, source_target_pairs={{8,0},{16,8},{24,16},{9,1},{17,9},{25,17},{10,2},{18,10},{26,18},{... | collective-permute-start | bytes 110600 | tf_op jit(solution)/shard_map/ppermute | solution.py:602
  16.4 2.7 %collective-permute-start.5 = (bf16[9,16,128]{2,1,0:T(8,128)(2,1)S(1)}, bf16[9,16,128]{2,1,0:T(8,128)(2,1)S(1)}, u32[]{:S(2)}, u32[]{:S(2)}) collective-permute-start(bf16[9,16,128]{2,1,0:T(8,128)(2,1)S(1)} %get-tuple-element.26), channel_id=1, source_target_pairs={{0,8},{8,16},{16,24},{24,0},{1,9},{9,17},{17,25},{25,1},{2,10},{10... | collective-permute-start | bytes 110600 | tf_op jit(solution)/shard_map/ppermute | solution.py:597
  19.1 0.0 copy-done.12
  19.2 0.0 copy-done.7
  19.2 0.0 copy-done.3
  19.2 0.0 copy-start
  19.2 1.5 %copy-done = f32[8,60,8,128]{3,2,1,0:T(8,128)S(1)} copy-done((f32[8,60,8,128]{3,2,1,0:T(8,128)S(1)}, f32[8,60,8,128]{3,2,1,0:T(8,128)}, u32[]{:S(2)}) %copy-start) | copy-done | bytes 1966104
  20.7 0.8 %shard_map.107 = (bf16[556,1024]{1,0:T(8,128)(2,1)S(1)}, f32[8,128]{1,0:T(8,128)S(1)}) custom-call(f32[8,60,8,128]{3,2,1,0:T(8,128)S(1)} %copy-done, bf16[76,8,128]{2,1,0:T(8,128)(2,1)S(1)} %copy-done.3, s32[1,1024]{1,0:T(1,128)S(1)} %bitcast.6), custom_call_target="tpu_custom_call" | custom-call | flops 16777216 | bytes 4194304 | tf_op jit(solution)/shard_map/pallas_call | solution.py:241
  21.5 0.0 copy-start.10
  21.5 0.0 collective-permute-done.from_north_ref
  21.5 0.0 collective-permute-done.1.from_south_ref
  21.5 0.7 %copy-done.1 = f32[8,60,8,128]{3,2,1,0:T(8,128)S(1)} copy-done((f32[8,60,8,128]{3,2,1,0:T(8,128)S(1)}, f32[8,60,8,128]{3,2,1,0:T(8,128)}, u32[]{:S(2)}) %copy-start.1) | copy-done | bytes 1966104
  22.3 1.1 %shard_map.105.inner_ref = f32[3,60,8,128]{3,2,1,0:T(8,128)S(1)} custom-call(f32[8,60,8,128]{3,2,1,0:T(8,128)S(1)} %copy-done.1, bf16[45,16,128]{2,1,0:T(8,128)(2,1)S(1)} %collective-permute-done.from_north_ref, bf16[45,16,128]{2,1,0:T(8,128)(2,1)S(1)} %collective-permute-done.1.from_south_ref), custom_call_target="tpu_custom_call" | custom-call | flops 16777216 | bytes 4194304 | tf_op jit(solution)/shard_map/pallas_call | solution.py:206
  23.4 0.0 collective-permute-done.4.north_ref
  23.4 0.0 collective-permute-done.5.south_ref
  23.5 6.8 %shard_map.108 = (f32[1440,128]{1,0:T(8,128)S(1)}, f32[60,8,128]{2,1,0:T(8,128)S(1)}, bf16[1024,640]{1,0:T(8,128)(2,1)S(1)}, bf16[60,16,128]{2,1,0:T(8,128)(2,1)S(1)}) custom-call(f32[3,60,8,128]{3,2,1,0:T(8,128)S(1)} %shard_map.105.inner_ref, f32[36,8,128]{2,1,0:T(8,128)S(1)} %get-tuple-element.24.here_ref, ...), custom_call_target="tpu_custom_call" | custom-call | flops 4294967296 | bytes 8388608 | tf_op jit(solution)/shard_map/pallas_call | solution.py:369
  30.3 0.0 copy-start.6
  30.3 0.1 collective-permute-start.8
  30.4 0.7 %shard_map.109.own_ref = bf16[60,16,128]{2,1,0:T(8,128)(2,1)S(1)} custom-call(bf16[1024,640]{1,0:T(8,128)(2,1)S(1)} %get-tuple-element.29.hidden_ref, bf16[120,640]{1,0:T(8,128)(2,1)S(1)} %get-tuple-element.39.five_ref, f32[8,128]{1,0:T(8,128)S(1)} %get-tuple-element.28.lit_ref, f32[480,8,128]{2,1,0:T(8,128)S(1)} %bitcast.5), custom_call_target="tpu_custom_call" | custom-call | flops 268435456 | bytes 3145728 | tf_op jit(solution)/shard_map/pallas_call | solution.py:403
  31.1 0.1 collective-permute-start.6
  31.2 0.0 copy-done.2
  31.2 0.1 collective-permute-start.10
  31.3 6.5 %collective-permute-done.8.near_ref = bf16[60,16,128]{2,1,0:T(8,128)(2,1)S(1)} collective-permute-done((bf16[60,16,128]{2,1,0:T(8,128)(2,1)S(1)}, bf16[60,16,128]{2,1,0:T(8,128)(2,1)S(1)}, u32[]{:S(2)}, u32[]{:S(2)}) %collective-permute-start.8) | collective-permute-done | bytes 245792 | tf_op jit(solution)/shard_map/ppermute | solution.py:597
  37.8 1.5 %shard_map.112 = bf16[61,16,128]{2,1,0:T(8,128)(2,1)S(1)} custom-call(s32[8]{0:T(128)S(1)} %copy-done.6, bf16[60,16,128]{2,1,0:T(8,128)(2,1)S(1)} %get-tuple-element.34.own_ref, bf16[60,16,128]{2,1,0:T(8,128)(2,1)S(1)} %collective-permute-done.8.near_ref), custom_call_target="tpu_custom_call" | custom-call | flops 1048576 | bytes 1048576 | tf_op jit(solution)/shard_map/pallas_call | solution.py:518
  39.3 0.0 collective-permute-start.9
  39.4 1.1 %collective-permute-done.6.near_ref = bf16[60,16,128]{2,1,0:T(8,128)(2,1)S(1)} collective-permute-done((bf16[60,16,128]{2,1,0:T(8,128)(2,1)S(1)}, bf16[60,16,128]{2,1,0:T(8,128)(2,1)S(1)}, u32[]{:S(2)}, u32[]{:S(2)}) %collective-permute-start.6) | collective-permute-done | bytes 245792 | tf_op jit(solution)/shard_map/ppermute | solution.py:597
  40.4 1.5 %shard_map.110 = bf16[61,16,128]{2,1,0:T(8,128)(2,1)S(1)} custom-call(s32[8]{0:T(128)S(1)} %copy-done.6, bf16[60,16,128]{2,1,0:T(8,128)(2,1)S(1)} %shard_map.109.own_ref, bf16[60,16,128]{2,1,0:T(8,128)(2,1)S(1)} %collective-permute-done.6.near_ref), custom_call_target="tpu_custom_call" | custom-call | flops 1048576 | bytes 1048576 | tf_op jit(solution)/shard_map/pallas_call | solution.py:518
  42.0 0.0 collective-permute-start.7
  42.0 0.0 collective-permute-done.10.near_ref
  42.0 1.0 %shard_map.113 = bf16[31,16,128]{2,1,0:T(8,128)(2,1)S(1)} custom-call(s32[8]{0:T(128)S(1)} %copy-done.6, bf16[30,16,128]{2,1,0:T(8,128)(2,1)S(1)} %copy-done.2, bf16[30,16,128]{2,1,0:T(8,128)(2,1)S(1)} %collective-permute-done.10.near_ref), custom_call_target="tpu_custom_call" | custom-call | flops 1048576 | bytes 1048576 | tf_op jit(solution)/shard_map/pallas_call | solution.py:518
  43.1 0.0 collective-permute-start.11
  43.1 2.2 %shard_map.111 = (f32[480,8,128]{2,1,0:T(8,128)}, bf16[8,8,128]{2,1,0:T(8,128)(2,1)}, f32[60,8,128]{2,1,0:T(8,128)S(1)}, f32[60,8,128]{2,1,0:T(8,128)S(1)}) custom-call(bf16[1024,640]{1,0:T(8,128)(2,1)S(1)} %get-tuple-element.29.hidden_ref, bf16[128,640]{1,0:T(8,128)(2,1)S(1)} %pad_maximum_fusion.five_ref, f32[8,128]{1,0:T(8,128)S(1)} %get-tuple-element.28.lit_ref, ...), custom_call_target="tpu_custom_call" | custom-call | flops 268435456 | bytes 4194304 | tf_op jit(solution)/shard_map/pallas_call | solution.py:461
  45.4 9.8 %collective-permute-done.11.far_ref = bf16[31,16,128]{2,1,0:T(8,128)(2,1)S(1)} collective-permute-done((bf16[31,16,128]{2,1,0:T(8,128)(2,1)S(1)}, bf16[31,16,128]{2,1,0:T(8,128)(2,1)S(1)}, u32[]{:S(2)}, u32[]{:S(2)}) %collective-permute-start.11) | collective-permute-done | bytes 127008 | tf_op jit(solution)/shard_map/ppermute | solution.py:597
  55.2 1.9 %shard_map.114.whole_ref = f32[480,8,128]{2,1,0:T(8,128)} custom-call(s32[8]{0:T(128)S(1)} %copy-done.6, bf16[30,16,128]{2,1,0:T(8,128)(2,1)S(1)} %copy-done.2, bf16[30,16,128]{2,1,0:T(8,128)(2,1)S(1)} %collective-permute-done.10.near_ref, bf16[31,16,128]{2,1,0:T(8,128)(2,1)S(1)} %collective-permute-done.11.far_ref, ...), custom_call_target="tpu_custom_call", output_to_operand_aliasing={{}: (6, {})} | custom-call | flops 4194304 | bytes 3145728 | tf_op jit(solution)/shard_map/pallas_call | solution.py:580
  57.1 0.0 collective-permute-done.9.far_ref
  57.1 2.5 %shard_map.115.whole_ref = f32[480,8,128]{2,1,0:T(8,128)} custom-call(s32[8]{0:T(128)S(1)} %copy-done.6, bf16[60,16,128]{2,1,0:T(8,128)(2,1)S(1)} %get-tuple-element.34.own_ref, bf16[60,16,128]{2,1,0:T(8,128)(2,1)S(1)} %collective-permute-done.8.near_ref, bf16[61,16,128]{2,1,0:T(8,128)(2,1)S(1)} %collective-permute-done.9.far_ref, ...), custom_call_target="tpu_custom_call", output_to_operand_aliasing={{}: (6, {})} | custom-call | flops 4194304 | bytes 3145728 | tf_op jit(solution)/shard_map/pallas_call | solution.py:580
  59.6 0.0 collective-permute-done.7.far_ref
  59.6 2.5 %shard_map.116 = f32[480,8,128]{2,1,0:T(8,128)} custom-call(s32[8]{0:T(128)S(1)} %copy-done.6, bf16[60,16,128]{2,1,0:T(8,128)(2,1)S(1)} %shard_map.109.own_ref, bf16[60,16,128]{2,1,0:T(8,128)(2,1)S(1)} %collective-permute-done.6.near_ref, bf16[61,16,128]{2,1,0:T(8,128)(2,1)S(1)} %collective-permute-done.7.far_ref, ...), custom_call_target="tpu_custom_call", output_to_operand_aliasing={{}: (6, {})} | custom-call | flops 4194304 | bytes 3145728 | tf_op jit(solution)/shard_map/pallas_call | solution.py:580
  (18 shorter events, 0.1 us)
Async XLA Ops:
  0.6 18.5 %copy-start.12 = (bf16[640,368]{0,1:T(8,128)(2,1)S(1)}, bf16[640,368]{0,1:T(8,128)(2,1)}, u32[]{:S(2)}) copy-start(bf16[640,368]{0,1:T(8,128)(2,1)} %param.15) | copy-start | bytes 1413124
  0.6 18.5 %copy-start.7 = (s32[1,1,1024]{2,1,0:T(1,128)S(1)}, s32[1,1,1024]{2,1,0:T(1,128)}, u32[]{:S(2)}) copy-start(s32[1,1,1024]{2,1,0:T(1,128)} %param.16) | copy-start | bytes 12292
  0.7 18.5 %copy-start.3 = (bf16[76,8,128]{2,1,0:T(8,128)(2,1)S(1)}, bf16[76,8,128]{2,1,0:T(8,128)(2,1)}, u32[]{:S(2)}) copy-start(bf16[76,8,128]{2,1,0:T(8,128)(2,1)} %surface_ref.1) | copy-start | bytes 466948
  2.9 8.6 %collective-permute-start.2 = (bf16[18,16,128]{2,1,0:T(8,128)(2,1)}, bf16[18,16,128]{2,1,0:T(8,128)(2,1)S(1)}, u32[]{:S(2)}, u32[]{:S(2)}) collective-permute-start(bf16[18,16,128]{2,1,0:T(8,128)(2,1)} %get-tuple-element.22.own_west_ref), channel_id=1, source_target_pairs={{0,7},{1,0},{2,1},{3,2},{4,3},{5,4},{6,5},{7,6},{8,15},{9,8},{10,9... | collective-permute-start | bytes 221192 | tf_op jit(solution)/shard_map/ppermute | solution.py:597
  7.5 5.8 %collective-permute-start.3 = (bf16[18,16,128]{2,1,0:T(8,128)(2,1)}, bf16[18,16,128]{2,1,0:T(8,128)(2,1)S(1)}, u32[]{:S(2)}, u32[]{:S(2)}) collective-permute-start(bf16[18,16,128]{2,1,0:T(8,128)(2,1)} %get-tuple-element.23.own_east_ref), channel_id=1, source_target_pairs={{0,1},{1,2},{2,3},{3,4},{4,5},{5,6},{6,7},{7,0},{8,9},{9,10},{10,1... | collective-permute-start | bytes 221192 | tf_op jit(solution)/shard_map/ppermute | solution.py:597
  7.5 14.0 %collective-permute-start = (bf16[45,16,128]{2,1,0:T(8,128)(2,1)}, bf16[45,16,128]{2,1,0:T(8,128)(2,1)S(1)}, u32[]{:S(2)}, u32[]{:S(2)}) collective-permute-start(bf16[45,16,128]{2,1,0:T(8,128)(2,1)} %get-tuple-element.20), channel_id=1, source_target_pairs={{8,0},{16,8},{24,16},{9,1},{17,9},{25,17},{10,2},{18,10},{26,18},{... | collective-permute-start | bytes 552968 | tf_op jit(solution)/shard_map/ppermute | solution.py:602
  8.8 12.7 %collective-permute-start.1 = (bf16[45,16,128]{2,1,0:T(8,128)(2,1)}, bf16[45,16,128]{2,1,0:T(8,128)(2,1)S(1)}, u32[]{:S(2)}, u32[]{:S(2)}) collective-permute-start(bf16[45,16,128]{2,1,0:T(8,128)(2,1)} %get-tuple-element.21), channel_id=1, source_target_pairs={{0,8},{8,16},{16,24},{24,0},{1,9},{9,17},{17,25},{25,1},{2,10},{10... | collective-permute-start | bytes 552968 | tf_op jit(solution)/shard_map/ppermute | solution.py:597
  13.3 0.9 %copy-start.4 = (bf16[18,16,128]{2,1,0:T(8,128)(2,1)S(1)}, bf16[18,16,128]{2,1,0:T(8,128)(2,1)}, u32[]{:S(2)}) copy-start(bf16[18,16,128]{2,1,0:T(8,128)(2,1)} %get-tuple-element.22.own_west_ref) | copy-start | bytes 221188
  14.2 0.9 %copy-start.5 = (bf16[18,16,128]{2,1,0:T(8,128)(2,1)S(1)}, bf16[18,16,128]{2,1,0:T(8,128)(2,1)}, u32[]{:S(2)}) copy-start(bf16[18,16,128]{2,1,0:T(8,128)(2,1)} %get-tuple-element.23.own_east_ref) | copy-start | bytes 221188
  15.1 8.3 %collective-permute-start.4 = (bf16[9,16,128]{2,1,0:T(8,128)(2,1)S(1)}, bf16[9,16,128]{2,1,0:T(8,128)(2,1)S(1)}, u32[]{:S(2)}, u32[]{:S(2)}) collective-permute-start(bf16[9,16,128]{2,1,0:T(8,128)(2,1)S(1)} %get-tuple-element.25), channel_id=1, source_target_pairs={{8,0},{16,8},{24,16},{9,1},{17,9},{25,17},{10,2},{18,10},{26,18},{... | collective-permute-start | bytes 110600 | tf_op jit(solution)/shard_map/ppermute | solution.py:602
  16.4 7.0 %collective-permute-start.5 = (bf16[9,16,128]{2,1,0:T(8,128)(2,1)S(1)}, bf16[9,16,128]{2,1,0:T(8,128)(2,1)S(1)}, u32[]{:S(2)}, u32[]{:S(2)}) collective-permute-start(bf16[9,16,128]{2,1,0:T(8,128)(2,1)S(1)} %get-tuple-element.26), channel_id=1, source_target_pairs={{0,8},{8,16},{16,24},{24,0},{1,9},{9,17},{17,25},{25,1},{2,10},{10... | collective-permute-start | bytes 110600 | tf_op jit(solution)/shard_map/ppermute | solution.py:597
  19.2 1.5 %copy-start = (f32[8,60,8,128]{3,2,1,0:T(8,128)S(1)}, f32[8,60,8,128]{3,2,1,0:T(8,128)}, u32[]{:S(2)}) copy-start(f32[8,60,8,128]{3,2,1,0:T(8,128)} %state_ref.5) | copy-start | bytes 5898244
  20.7 1.5 %copy-start.1 = (f32[8,60,8,128]{3,2,1,0:T(8,128)S(1)}, f32[8,60,8,128]{3,2,1,0:T(8,128)}, u32[]{:S(2)}) copy-start(f32[8,60,8,128]{3,2,1,0:T(8,128)} %state_ref.5) | copy-start | bytes 5898244
  20.7 2.7 %copy-start.11 = (bf16[512,640]{1,0:T(8,128)(2,1)S(1)}, bf16[512,640]{1,0:T(8,128)(2,1)}, u32[]{:S(2)}) copy-start(bf16[512,640]{1,0:T(8,128)(2,1)} %four_ref.1) | copy-start | bytes 1966084
  21.5 1.9 %copy-start.8 = (bf16[768,640]{1,0:T(8,128)(2,1)S(1)}, bf16[768,640]{1,0:T(8,128)(2,1)}, u32[]{:S(2)}) copy-start(bf16[768,640]{1,0:T(8,128)(2,1)} %two_ref.1) | copy-start | bytes 2949124
  21.5 2.0 %copy-start.9 = (bf16[556,768]{1,0:T(8,128)(2,1)S(1)}, bf16[556,768]{1,0:T(8,128)(2,1)}, u32[]{:S(2)}) copy-start(bf16[556,768]{1,0:T(8,128)(2,1)} %one_ref.1) | copy-start | bytes 2562052
  21.5 2.0 %copy-start.10 = (bf16[640,512]{1,0:T(8,128)(2,1)S(1)}, bf16[640,512]{1,0:T(8,128)(2,1)}, u32[]{:S(2)}) copy-start(bf16[640,512]{1,0:T(8,128)(2,1)} %three_ref.1) | copy-start | bytes 1966084
  30.3 0.9 %copy-start.2 = (bf16[30,16,128]{2,1,0:T(8,128)(2,1)S(1)}, bf16[30,16,128]{2,1,0:T(8,128)(2,1)}, u32[]{:S(2)}) copy-start(bf16[30,16,128]{2,1,0:T(8,128)(2,1)} %get-tuple-element.35.own_ref) | copy-start | bytes 368644
  30.3 7.5 %copy-start.6 = (s32[8]{0:T(128)S(1)}, s32[8]{0:T(128)}, u32[]{:S(2)}) copy-start(s32[8]{0:T(128)} %offset_ref.11) | copy-start | bytes 100
  30.3 7.5 %collective-permute-start.8 = (bf16[60,16,128]{2,1,0:T(8,128)(2,1)S(1)}, bf16[60,16,128]{2,1,0:T(8,128)(2,1)S(1)}, u32[]{:S(2)}, u32[]{:S(2)}) collective-permute-start(bf16[60,16,128]{2,1,0:T(8,128)(2,1)S(1)} %get-tuple-element.34.own_ref), channel_id=1, source_target_pairs={{0,1},{1,2},{2,3},{3,4},{4,5},{5,6},{6,7},{7,0},{8,9},{9,10},{10,1... | collective-permute-start | bytes 737288 | tf_op jit(solution)/shard_map/ppermute | solution.py:597
  31.1 9.3 %collective-permute-start.6 = (bf16[60,16,128]{2,1,0:T(8,128)(2,1)S(1)}, bf16[60,16,128]{2,1,0:T(8,128)(2,1)S(1)}, u32[]{:S(2)}, u32[]{:S(2)}) collective-permute-start(bf16[60,16,128]{2,1,0:T(8,128)(2,1)S(1)} %shard_map.109.own_ref), channel_id=1, source_target_pairs={{0,1},{1,2},{2,3},{3,4},{4,5},{5,6},{6,7},{7,0},{8,9},{9,10},{10,1... | collective-permute-start | bytes 737288 | tf_op jit(solution)/shard_map/ppermute | solution.py:597
  31.2 10.8 %collective-permute-start.10 = (bf16[30,16,128]{2,1,0:T(8,128)(2,1)S(1)}, bf16[30,16,128]{2,1,0:T(8,128)(2,1)S(1)}, u32[]{:S(2)}, u32[]{:S(2)}) collective-permute-start(bf16[30,16,128]{2,1,0:T(8,128)(2,1)S(1)} %copy-done.2), channel_id=1, source_target_pairs={{0,1},{1,2},{2,3},{3,4},{4,5},{5,6},{6,7},{7,0},{8,9},{9,10},{10,1... | collective-permute-start | bytes 368648 | tf_op jit(solution)/shard_map/ppermute | solution.py:597
  39.3 17.8 %collective-permute-start.9 = (bf16[61,16,128]{2,1,0:T(8,128)(2,1)S(1)}, bf16[61,16,128]{2,1,0:T(8,128)(2,1)S(1)}, u32[]{:S(2)}, u32[]{:S(2)}) collective-permute-start(bf16[61,16,128]{2,1,0:T(8,128)(2,1)S(1)} %shard_map.112), channel_id=1, source_target_pairs={{0,2},{1,3},{2,4},{3,5},{4,6},{5,7},{6,0},{7,1},{8,10},{9,11},{10,... | collective-permute-start | bytes 749576 | tf_op jit(solution)/shard_map/ppermute | solution.py:597
  42.0 17.7 %collective-permute-start.7 = (bf16[61,16,128]{2,1,0:T(8,128)(2,1)S(1)}, bf16[61,16,128]{2,1,0:T(8,128)(2,1)S(1)}, u32[]{:S(2)}, u32[]{:S(2)}) collective-permute-start(bf16[61,16,128]{2,1,0:T(8,128)(2,1)S(1)} %shard_map.110), channel_id=1, source_target_pairs={{0,2},{1,3},{2,4},{3,5},{4,6},{5,7},{6,0},{7,1},{8,10},{9,11},{10,... | collective-permute-start | bytes 749576 | tf_op jit(solution)/shard_map/ppermute | solution.py:597
  43.1 12.1 %collective-permute-start.11 = (bf16[31,16,128]{2,1,0:T(8,128)(2,1)S(1)}, bf16[31,16,128]{2,1,0:T(8,128)(2,1)S(1)}, u32[]{:S(2)}, u32[]{:S(2)}) collective-permute-start(bf16[31,16,128]{2,1,0:T(8,128)(2,1)S(1)} %shard_map.113), channel_id=1, source_target_pairs={{0,2},{1,3},{2,4},{3,5},{4,6},{5,7},{6,0},{7,1},{8,10},{9,11},{10,... | collective-permute-start | bytes 380936 | tf_op jit(solution)/shard_map/ppermute | solution.py:597

commit v3 on v2

--- a/solution.py
+++ b/solution.py
@@ -77,19 +77,11 @@
     return tiles.reshape(count // 2, 2 * rows, cols).astype(BF16)
 
 
-def messages_kernel(
-    state_ref, south_ref, north_ref, west_ref, east_ref, ozone_ref, held, sems
-):
-    fields, levels, rows, cols = state_ref.shape
+def messages_kernel(winds_ref, south_ref, north_ref, west_ref, east_ref):
+    fields, levels, rows, cols = winds_ref.shape
     low = iota((rows, cols), 0) < rows // 2
     lane = iota((rows, cols), 1)
-    copies = []
-    for place, field in enumerate((0, 1, 2, fields - 1)):
-        copy = pltpu.make_async_copy(
-            state_ref.at[field], held.at[pl.ds(place * levels, levels)], sems.at[place]
-        )
-        copy.start()
-        copies.append(copy)
+    held = winds_ref.reshape(fields * levels, rows, cols)
 
     def body(step, carry):
         tiles = held[pl.ds(step * 20, 20)]
@@ -101,36 +93,25 @@
         east_ref[pl.ds(step * 2, 2)] = tall(east)
         return carry
 
-    for place in range(3):
-        copies[place].wait()
-        lax.fori_loop(
-            place * levels // 20, (place + 1) * levels // 20, body, 0, unroll=levels // 20
-        )
-    copies[3].wait()
-    ozone_ref[...] = tall(held[3 * levels :])
-
-
-def messages(state):
-    _, levels, rows, cols = state.shape
+    steps = fields * levels // 20
+    lax.fori_loop(0, steps, body, 0, unroll=steps)
+
+
+def messages(winds):
+    fields, levels, rows, cols = winds.shape
 
     def shape(count):
         return jax.ShapeDtypeStruct((count // 2, 2 * rows, cols), BF16)
 
-    packs = 3 * levels // (cols // STRIP)
+    packs = fields * levels // (cols // STRIP)
     return pl.pallas_call(
         messages_kernel,
-        out_shape=(shape(3 * levels // 2),) * 2
-        + (shape(packs),) * 2
-        + (shape(levels),),
-        in_specs=[pl.BlockSpec(memory_space=pltpu.HBM)],
-        out_specs=(vmem(),) * 5,
-        scratch_shapes=[
-            pltpu.VMEM((4 * levels, rows, cols), F32),
-            pltpu.SemaphoreType.DMA((4,)),
-        ],
-        compiler_params=pltpu.CompilerParams(vmem_limit_bytes=125 << 19),
-        cost_estimate=cost(1 << 20, 4 << 20),
-    )(state)
+        out_shape=(shape(fields * levels // 2),) * 2 + (shape(packs),) * 2,
+        in_specs=[vmem()],
+        out_specs=(vmem(),) * 4,
+        compiler_params=params(4),
+        cost_estimate=cost(1 << 20, 2 << 20),
+    )(winds)
 
 
 def short(ref, at, size):
@@ -213,8 +194,9 @@
     )(state, from_north, from_south)
 
 
-def rest_kernel(state_ref, surface_ref, slots_ref, rest_ref, lit_ref, buffer, wide):
+def rest_kernel(state_ref, surface_ref, slots_ref, rest_ref, lit_ref, ozone_ref, buffer, wide):
     fields, levels, rows, cols = state_ref.shape
+    ozone_ref[...] = tall(state_ref[fields - 1])
     extra = surface_ref.shape[0]
     first = 3 * levels
     wide[...] = surface_ref[...].astype(F32).reshape(extra * rows, cols)
@@ -243,9 +225,10 @@
         out_shape=(
             jax.ShapeDtypeStruct((count, rows * cols), BF16),
             jax.ShapeDtypeStruct((rows, cols), F32),
+            jax.ShapeDtypeStruct((levels // 2, 2 * rows, cols), BF16),
         ),
         in_specs=[vmem()] * 3,
-        out_specs=(vmem(), vmem()),
+        out_specs=(vmem(),) * 3,
         scratch_shapes=[
             pltpu.VMEM((count, cols), F32),
             pltpu.VMEM((surface.shape[0] * rows, cols), F32),
@@ -500,16 +483,16 @@
     edge = cols - 1 - cells
 
     def body(step, column):
-        at = pl.ds(step * 5, 5)
-        own = own_ref[at].astype(F32).reshape(10, rows, cols)
-        near = near_ref[at].astype(F32).reshape(10, rows, cols)
-        out = jnp.where(take_near, near, own)
-        out_ref[at] = out.reshape(5, 2 * rows, cols).astype(BF16)
-        for level in range(10):
-            column = jnp.where(lane == step * 10 + level, along(near[level], edge), column)
+        at = pl.ds(step * 10, 10)
+        own = own_ref[at].astype(F32).reshape(20, rows, cols)
+        near = near_ref[at].astype(F32).reshape(20, rows, cols)
+        out_ref[at] = tall(jnp.where(take_near, near, own))
+        for level in range(20):
+            column = jnp.where(lane == step * 20 + level, along(near[level], edge), column)
         return column
 
-    column = lax.fori_loop(0, pairs // 5, body, jnp.zeros((rows, cols), F32))
+    steps = pairs // 10
+    column = lax.fori_loop(0, steps, body, jnp.zeros((rows, cols), F32), unroll=3)
     out_ref[pairs] = jnp.concatenate([column, column], axis=0).astype(BF16)
 
 
@@ -534,49 +517,46 @@
     lane = iota((rows, cols), 1)
     from_right = lane <= cols - 1 - cells
     index = (lane - cells) & (cols - 1)
-    index_less = (lane - cells - 1) & (cols - 1)
     column = far_ref[pairs].astype(F32)[:rows]
     is_zero, is_one, is_two = blocks == 0, blocks == 1, blocks >= 2
     steps = levels // group
-    copies = []
-    for field in range(2 * pairs // levels):
-        def body(step, carry):
-            at = pl.ds(field * (levels // 2) + step * (group // 2), group // 2)
-            own = own_ref[at].astype(F32).reshape(group, rows, cols)
-            near = near_ref[at].astype(F32).reshape(group, rows, cols)
-            far = far_ref[at].astype(F32).reshape(group, rows, cols)
-            stay = stay_ref[pl.ds(step * group, group)]
-            come = come_ref[pl.ds(step * group, group)]
-            right = jnp.where(is_zero, own, jnp.where(is_one, near, far))
-            left = jnp.where(is_zero, near, far)
-            merged = jnp.where(from_right, right, left)
-            for level in range(group):
-                which = field * levels + step * group + level
-                lone = along(column, jnp.zeros((rows, cols), jnp.int32) + which)
-                edge = jnp.where(is_two, lone, left[level])
-                shifted = jnp.where(lane == cols - 1 - cells, edge, merged[level])
-                here = along(merged[level], index)
-                behind = along(shifted, index_less)
-                result[field * levels + step * group + level] = (
-                    stay[level] * here + come[level] * behind
-                )
-            return carry
-
-        lax.fori_loop(0, steps, body, 0)
-        copy = pltpu.make_async_copy(
-            result.at[pl.ds(field * levels, levels)],
-            out_ref.at[pl.ds((first + field) * levels, levels)],
-            sem.at[field],
+    edge_index = cols - 1 - cells
+
+    def body(step, carry):
+        at = pl.ds(step * (group // 2), group // 2)
+        share = pl.ds(lax.rem(step, steps) * group, group)
+        own = own_ref[at].astype(F32).reshape(group, rows, cols)
+        near = near_ref[at].astype(F32).reshape(group, rows, cols)
+        far = far_ref[at].astype(F32).reshape(group, rows, cols)
+        stay = stay_ref[share]
+        come = come_ref[share]
+        right = jnp.where(is_zero, own, jnp.where(is_one, near, far))
+        left = jnp.where(is_zero, near, far)
+        merged = jnp.where(from_right, right, left)
+        edges = jnp.where(is_two, column, left)
+        for level in range(group):
+            which = jnp.where(is_two, step * group + level, edge_index)
+            here = along(merged[level], index)
+            behind = jnp.where(lane == 0, along(edges[level], which), pltpu.roll(here, 1, 1))
+            result[step * group + level] = stay[level] * here + come[level] * behind
+        copy_of(step).start()
+        return carry
+
+    def copy_of(step):
+        return pltpu.make_async_copy(
+            result.at[pl.ds(step * group, group)],
+            out_ref.at[pl.ds(first * levels + step * group, group)],
+            sem.at[step],
         )
-        copy.start()
-        copies.append(copy)
-    for copy in copies:
-        copy.wait()
-
-
-def advect(first, offset, own, near, far, stay, come, whole, group=20):
+
+    count = 2 * pairs // group
+    lax.fori_loop(0, count, body, 0)
+    for step in range(count):
+        copy_of(step).wait()
+
+
+def advect(first, offset, own, near, far, stay, come, whole, group=30):
     pairs, height, cols = own.shape
-    levels = stay.shape[0]
     return pl.pallas_call(
         functools.partial(advect_kernel, first, group),
         out_shape=jax.ShapeDtypeStruct(whole.shape, F32),
@@ -584,7 +564,7 @@
         out_specs=any_space(),
         scratch_shapes=[
             pltpu.VMEM((2 * pairs, height // 2, cols), F32),
-            pltpu.SemaphoreType.DMA((2 * pairs // levels,)),
+            pltpu.SemaphoreType.DMA((2 * pairs // group,)),
         ],
         input_output_aliases={6: 0},
         compiler_params=params(12),
@@ -630,7 +610,9 @@
     slots = lit_columns.reshape(1, rows * cols)
     flat = state.reshape(fields * levels, rows, cols)
 
-    to_south, to_north, to_west, to_east, ozone = messages(state)
+    start_winds = state[:3]
+    to_south, to_north, to_west, to_east = messages(start_winds)
+    rest, lit, ozone = rest_features(state, surface, slots)
     from_east = shifted(to_west, "lon", -1)
     from_west = shifted(to_east, "lon", 1)
     from_south = shifted(to_north, "lat", 1)
@@ -640,13 +622,12 @@
     strips_from_south = shifted(strips_north, "lat", 1)
     strips_from_north = passed_along(strips_south, "lat", -1)
 
-    rest, lit = rest_features(state, surface, slots)
     five = layer_five.T
     five_first = five[2 * levels : 4 * levels]
     five_second = five[4 * levels : 6 * levels]
     five_winds = jnp.concatenate([five[: 2 * levels], five[6 * levels :]], axis=0)
 
-    inner_out = inner(state, from_north, from_south)
+    inner_out = inner(start_winds, from_north, from_south)
     ozone_relay = relay(row_offset, ozone, ozone_near)
     ozone_far = shifted(ozone_relay, "lon", 2)
     winds, upwind, hidden, first = network(

time: 62.5 us -> 58.7 us (0.939)
  Pallas kernels: 25 us -> 20.2 us
  waiting for transfers between devices: 19.2 us -> 22.3 us
  local copies, waits for them, and re-layouts: 4.15 us -> 1.42 us
  starting transfers between devices: 12.8 us -> 13.7 us
    unnamed x26 -> x18, local copies, waits for them, and re-layouts: 4.1 us -> 0.05 us
    ppermute x10, waiting for transfers between devices: 19.2 us -> 22.3 us  [shifted(): lax.ppermute(value, axis, [(i, (i + steps) % count) for i in range(count)])]
    pallas_call x1, Pallas kernels: 2.26 us -> 0.26 us  [messages(): pl.pallas_call(messages_kernel, out_shape=(shape(fields * levels // 2),)...]
    pallas_call x3, Pallas kernels: 4.07 us -> 2.23 us  [relay(): pl.pallas_call(relay_kernel, out_shape=jax.ShapeDtypeStruct((pairs + 1, h...]
    slice x0 -> x1, local copies, waits for them, and re-layouts: none -> 1.32 us  [tile_step(): start_winds = state[:3]]
    pallas_call x3, Pallas kernels: 6.96 us -> 5.97 us  [advect(): pl.pallas_call(functools.partial(advect_kernel, first, group), out_shape=...]
    ppermute x10, starting transfers between devices: 10.2 us -> 11.1 us  [shifted(): lax.ppermute(value, axis, [(i, (i + steps) % count) for i in range(count)])]
  transfers between devices with their start and end apart: 12 -> 12, of which waited for: 4 -> 6; matrix products, arithmetic and copies ran while one was open for 0% -> 0% of each run, Pallas kernels for 22% -> 19%
where the time goes in v3:
time: 58.7 us; the launch traced here: 58.6 us
  waiting for transfers between devices  22.3 us (38%)
  Pallas kernels  20.2 us (34%)
  starting transfers between devices  13.7 us (23%)
  local copies, waits for them, and re-layouts  1.42 us (2%)
  between operations  0.93 us (2%)
    ppermute x10, waiting for transfers between devices, shifted(): lax.ppermute(value, axis, [(i, (i + steps) % count) for i in range(count)])  22.3 us
    ppermute x10, starting transfers between devices, shifted(): lax.ppermute(value, axis, [(i, (i + steps) % count) for i in range(count)])  11.1 us
    pallas_call x1, Pallas kernels, network(): pl.pallas_call(functools.partial(network_kernel, parts_count), out_shape=...  6.84 us
    pallas_call x3, Pallas kernels, advect(): pl.pallas_call(functools.partial(advect_kernel, first, group), out_shape=...  5.97 us
    ppermute x2, starting transfers between devices, passed_along(): lax.ppermute(block, axis, [(i, i + distance) for i in devices if i + dist...  2.57 us
    pallas_call x1, Pallas kernels, winds_out(): pl.pallas_call(winds_kernel, out_shape=(jax.ShapeDtypeStruct((fields * le...  2.23 us
    pallas_call x3, Pallas kernels, relay(): pl.pallas_call(relay_kernel, out_shape=jax.ShapeDtypeStruct((pairs + 1, h...  2.23 us
    slice x1, local copies, waits for them, and re-layouts, tile_step(): start_winds = state[:3]  1.32 us
  transfers between devices with their start and end apart: 12, of which 6 were waited for; matrix products, arithmetic and copies ran while one was open for 0% of the time, Pallas kernels for 19%

profile of v3, /device:TPU:0, one launch (start us, length us, event | category | flops | bytes accessed | tf_op | source)
XLA Modules:
  0.0 58.6 jit_solution(2498507750019172641)
XLA Ops:
  0.6 0.0 copy-start
  0.6 0.0 copy-start.8
  0.7 0.0 copy-start.3
  0.7 0.0 copy-start.1
  0.7 1.3 %slice.15.winds_ref.state_ref = f32[3,60,8,128]{3,2,1,0:T(8,128)S(1)} slice(f32[8,60,8,128]{3,2,1,0:T(8,128)} %state_ref.1), slice={[0:3], [0:60], [0:8], [0:128]} | slice | bytes 1474560 | tf_op jit(solution)/shard_map/slice | solution.py:613
  2.0 0.3 shard_map.104
  2.3 4.6 %collective-permute-start.2 = (bf16[18,16,128]{2,1,0:T(8,128)(2,1)S(1)}, bf16[18,16,128]{2,1,0:T(8,128)(2,1)S(1)}, u32[]{:S(2)}, u32[]{:S(2)}) collective-permute-start(bf16[18,16,128]{2,1,0:T(8,128)(2,1)S(1)} %get-tuple-element.22.own_west_ref), channel_id=1, source_target_pairs={{0,7},{1,0},{2,1},{3,2},{4,3},{5,4},{6,5},{7,6},{8,15},{9,8},{10,9... | collective-permute-start | bytes 221192 | tf_op jit(solution)/shard_map/ppermute | solution.py:577
  6.8 0.0 collective-permute-start.3
  6.8 1.3 %collective-permute-start = (bf16[45,16,128]{2,1,0:T(8,128)(2,1)S(1)}, bf16[45,16,128]{2,1,0:T(8,128)(2,1)S(1)}, u32[]{:S(2)}, u32[]{:S(2)}) collective-permute-start(bf16[45,16,128]{2,1,0:T(8,128)(2,1)S(1)} %get-tuple-element.20), channel_id=1, source_target_pairs={{8,0},{16,8},{24,16},{9,1},{17,9},{25,17},{10,2},{18,10},{26,18},{... | collective-permute-start | bytes 552968 | tf_op jit(solution)/shard_map/ppermute | solution.py:582
  8.1 2.7 %collective-permute-start.1 = (bf16[45,16,128]{2,1,0:T(8,128)(2,1)S(1)}, bf16[45,16,128]{2,1,0:T(8,128)(2,1)S(1)}, u32[]{:S(2)}, u32[]{:S(2)}) collective-permute-start(bf16[45,16,128]{2,1,0:T(8,128)(2,1)S(1)} %get-tuple-element.21), channel_id=1, source_target_pairs={{0,8},{8,16},{16,24},{24,0},{1,9},{9,17},{17,25},{25,1},{2,10},{10... | collective-permute-start | bytes 552968 | tf_op jit(solution)/shard_map/ppermute | solution.py:577
  10.8 0.0 collective-permute-done.2.from_east_ref
  10.8 1.6 %collective-permute-done.3.from_west_ref = bf16[18,16,128]{2,1,0:T(8,128)(2,1)S(1)} collective-permute-done((bf16[18,16,128]{2,1,0:T(8,128)(2,1)S(1)}, bf16[18,16,128]{2,1,0:T(8,128)(2,1)S(1)}, u32[]{:S(2)}, u32[]{:S(2)}) %collective-permute-start.3) | collective-permute-done | bytes 73760 | tf_op jit(solution)/shard_map/ppermute | solution.py:577
  12.4 0.1 shard_map.106
  12.5 1.3 %collective-permute-start.4 = (bf16[9,16,128]{2,1,0:T(8,128)(2,1)S(1)}, bf16[9,16,128]{2,1,0:T(8,128)(2,1)S(1)}, u32[]{:S(2)}, u32[]{:S(2)}) collective-permute-start(bf16[9,16,128]{2,1,0:T(8,128)(2,1)S(1)} %get-tuple-element.25), channel_id=1, source_target_pairs={{8,0},{16,8},{24,16},{9,1},{17,9},{25,17},{10,2},{18,10},{26,18},{... | collective-permute-start | bytes 110600 | tf_op jit(solution)/shard_map/ppermute | solution.py:582
  13.8 2.7 %collective-permute-start.5 = (bf16[9,16,128]{2,1,0:T(8,128)(2,1)S(1)}, bf16[9,16,128]{2,1,0:T(8,128)(2,1)S(1)}, u32[]{:S(2)}, u32[]{:S(2)}) collective-permute-start(bf16[9,16,128]{2,1,0:T(8,128)(2,1)S(1)} %get-tuple-element.26), channel_id=1, source_target_pairs={{0,8},{8,16},{16,24},{24,0},{1,9},{9,17},{17,25},{25,1},{2,10},{10... | collective-permute-start | bytes 110600 | tf_op jit(solution)/shard_map/ppermute | solution.py:577
  16.5 0.0 copy-done.8
  16.5 0.0 copy-start.4
  16.6 0.0 copy-start.5
  16.6 0.0 copy-start.6
  16.6 0.0 copy-start.7
  16.6 0.8 %shard_map.107 = (bf16[556,1024]{1,0:T(8,128)(2,1)S(1)}, f32[8,128]{1,0:T(8,128)S(1)}, bf16[30,16,128]{2,1,0:T(8,128)(2,1)S(1)}) custom-call(f32[8,60,8,128]{3,2,1,0:T(8,128)S(1)} %copy-done, bf16[76,8,128]{2,1,0:T(8,128)(2,1)S(1)} %copy-done.1, s32[1,1024]{1,0:T(1,128)S(1)} %bitcast.6), custom_call_target="tpu_custom_call" | custom-call | flops 16777216 | bytes 4194304 | tf_op jit(solution)/shard_map/pallas_call | solution.py:223
  17.4 0.0 collective-permute-done.from_north_ref
  17.4 2.3 %collective-permute-done.1.from_south_ref = bf16[45,16,128]{2,1,0:T(8,128)(2,1)S(1)} collective-permute-done((bf16[45,16,128]{2,1,0:T(8,128)(2,1)S(1)}, bf16[45,16,128]{2,1,0:T(8,128)(2,1)S(1)}, u32[]{:S(2)}, u32[]{:S(2)}) %collective-permute-start.1) | collective-permute-done | bytes 184352 | tf_op jit(solution)/shard_map/ppermute | solution.py:577
  19.7 1.1 %shard_map.105.inner_ref = f32[3,60,8,128]{3,2,1,0:T(8,128)S(1)} custom-call(f32[3,60,8,128]{3,2,1,0:T(8,128)S(1)} %slice.15.winds_ref.state_ref, bf16[45,16,128]{2,1,0:T(8,128)(2,1)S(1)} %collective-permute-done.from_north_ref, bf16[45,16,128]{2,1,0:T(8,128)(2,1)S(1)} %collective-permute-done.1.from_south_ref), custom_call_target="tpu_custom_call" | custom-call | flops 16777216 | bytes 4194304 | tf_op jit(solution)/shard_map/pallas_call | solution.py:187
  20.8 0.0 collective-permute-done.4.north_ref
  20.8 0.0 collective-permute-done.5.south_ref
  20.9 6.8 %shard_map.108 = (f32[1440,128]{1,0:T(8,128)S(1)}, f32[60,8,128]{2,1,0:T(8,128)S(1)}, bf16[1024,640]{1,0:T(8,128)(2,1)S(1)}, bf16[60,16,128]{2,1,0:T(8,128)(2,1)S(1)}) custom-call(f32[3,60,8,128]{3,2,1,0:T(8,128)S(1)} %shard_map.105.inner_ref, f32[36,8,128]{2,1,0:T(8,128)S(1)} %get-tuple-element.24.here_ref, ...), custom_call_target="tpu_custom_call" | custom-call | flops 4294967296 | bytes 8388608 | tf_op jit(solution)/shard_map/pallas_call | solution.py:352
  27.7 0.0 copy-start.2
  27.7 0.1 collective-permute-start.8
  27.8 0.7 %shard_map.109.own_ref = bf16[60,16,128]{2,1,0:T(8,128)(2,1)S(1)} custom-call(bf16[1024,640]{1,0:T(8,128)(2,1)S(1)} %get-tuple-element.29.hidden_ref, bf16[120,640]{1,0:T(8,128)(2,1)S(1)} %get-tuple-element.39.five_ref, f32[8,128]{1,0:T(8,128)S(1)} %get-tuple-element.28.lit_ref, f32[480,8,128]{2,1,0:T(8,128)S(1)} %bitcast.5), custom_call_target="tpu_custom_call" | custom-call | flops 268435456 | bytes 3145728 | tf_op jit(solution)/shard_map/pallas_call | solution.py:386
  28.5 0.8 %collective-permute-start.6 = (bf16[60,16,128]{2,1,0:T(8,128)(2,1)S(1)}, bf16[60,16,128]{2,1,0:T(8,128)(2,1)S(1)}, u32[]{:S(2)}, u32[]{:S(2)}) collective-permute-start(bf16[60,16,128]{2,1,0:T(8,128)(2,1)S(1)} %shard_map.109.own_ref), channel_id=1, source_target_pairs={{0,1},{1,2},{2,3},{3,4},{4,5},{5,6},{6,7},{7,0},{8,9},{9,10},{10,1... | collective-permute-start | bytes 737288 | tf_op jit(solution)/shard_map/ppermute | solution.py:577
  29.3 0.1 collective-permute-start.10
  29.4 5.8 %collective-permute-done.8.near_ref = bf16[60,16,128]{2,1,0:T(8,128)(2,1)S(1)} collective-permute-done((bf16[60,16,128]{2,1,0:T(8,128)(2,1)S(1)}, bf16[60,16,128]{2,1,0:T(8,128)(2,1)S(1)}, u32[]{:S(2)}, u32[]{:S(2)}) %collective-permute-start.8) | collective-permute-done | bytes 245792 | tf_op jit(solution)/shard_map/ppermute | solution.py:577
  35.2 0.8 %shard_map.112 = bf16[61,16,128]{2,1,0:T(8,128)(2,1)S(1)} custom-call(s32[8]{0:T(128)S(1)} %copy-done.2, bf16[60,16,128]{2,1,0:T(8,128)(2,1)S(1)} %get-tuple-element.34.own_ref, bf16[60,16,128]{2,1,0:T(8,128)(2,1)S(1)} %collective-permute-done.8.near_ref), custom_call_target="tpu_custom_call" | custom-call | flops 1048576 | bytes 1048576 | tf_op jit(solution)/shard_map/pallas_call | solution.py:501
  36.0 0.1 collective-permute-start.9
  36.0 1.8 %collective-permute-done.6.near_ref = bf16[60,16,128]{2,1,0:T(8,128)(2,1)S(1)} collective-permute-done((bf16[60,16,128]{2,1,0:T(8,128)(2,1)S(1)}, bf16[60,16,128]{2,1,0:T(8,128)(2,1)S(1)}, u32[]{:S(2)}, u32[]{:S(2)}) %collective-permute-start.6) | collective-permute-done | bytes 245792 | tf_op jit(solution)/shard_map/ppermute | solution.py:577
  37.8 0.8 %shard_map.110 = bf16[61,16,128]{2,1,0:T(8,128)(2,1)S(1)} custom-call(s32[8]{0:T(128)S(1)} %copy-done.2, bf16[60,16,128]{2,1,0:T(8,128)(2,1)S(1)} %shard_map.109.own_ref, bf16[60,16,128]{2,1,0:T(8,128)(2,1)S(1)} %collective-permute-done.6.near_ref), custom_call_target="tpu_custom_call" | custom-call | flops 1048576 | bytes 1048576 | tf_op jit(solution)/shard_map/pallas_call | solution.py:501
  38.6 0.1 collective-permute-start.7
  38.7 0.5 collective-permute-done.10.near_ref
  39.1 0.7 %shard_map.113 = bf16[31,16,128]{2,1,0:T(8,128)(2,1)S(1)} custom-call(s32[8]{0:T(128)S(1)} %copy-done.2, bf16[30,16,128]{2,1,0:T(8,128)(2,1)S(1)} %get-tuple-element.35.own_ref, bf16[30,16,128]{2,1,0:T(8,128)(2,1)S(1)} %collective-permute-done.10.near_ref), custom_call_target="tpu_custom_call" | custom-call | flops 1048576 | bytes 1048576 | tf_op jit(solution)/shard_map/pallas_call | solution.py:501
  39.8 0.1 collective-permute-start.11
  39.9 2.2 %shard_map.111 = (f32[480,8,128]{2,1,0:T(8,128)}, bf16[8,8,128]{2,1,0:T(8,128)(2,1)}, f32[60,8,128]{2,1,0:T(8,128)S(1)}, f32[60,8,128]{2,1,0:T(8,128)S(1)}) custom-call(bf16[1024,640]{1,0:T(8,128)(2,1)S(1)} %get-tuple-element.29.hidden_ref, bf16[128,640]{1,0:T(8,128)(2,1)S(1)} %pad_maximum_fusion.five_ref, f32[8,128]{1,0:T(8,128)S(1)} %get-tuple-element.28.lit_ref, ...), custom_call_target="tpu_custom_call" | custom-call | flops 268435456 | bytes 4194304 | tf_op jit(solution)/shard_map/pallas_call | solution.py:444
  42.1 10.4 %collective-permute-done.11.far_ref = bf16[31,16,128]{2,1,0:T(8,128)(2,1)S(1)} collective-permute-done((bf16[31,16,128]{2,1,0:T(8,128)(2,1)S(1)}, bf16[31,16,128]{2,1,0:T(8,128)(2,1)S(1)}, u32[]{:S(2)}, u32[]{:S(2)}) %collective-permute-start.11) | collective-permute-done | bytes 127008 | tf_op jit(solution)/shard_map/ppermute | solution.py:577
  52.6 1.7 %shard_map.114.whole_ref = f32[480,8,128]{2,1,0:T(8,128)} custom-call(s32[8]{0:T(128)S(1)} %copy-done.2, bf16[30,16,128]{2,1,0:T(8,128)(2,1)S(1)} %get-tuple-element.35.own_ref, bf16[30,16,128]{2,1,0:T(8,128)(2,1)S(1)} %collective-permute-done.10.near_ref, bf16[31,16,128]{2,1,0:T(8,128)(2,1)S(1)} %collective-permute-done.11.far_ref, ...), custom_call_target="tpu_custom_call", output_to_operand_aliasing={{}: (6, {})} | custom-call | flops 4194304 | bytes 3145728 | tf_op jit(solution)/shard_map/pallas_call | solution.py:560
  54.2 0.0 collective-permute-done.9.far_ref
  54.3 2.2 %shard_map.115.whole_ref = f32[480,8,128]{2,1,0:T(8,128)} custom-call(s32[8]{0:T(128)S(1)} %copy-done.2, bf16[60,16,128]{2,1,0:T(8,128)(2,1)S(1)} %get-tuple-element.34.own_ref, bf16[60,16,128]{2,1,0:T(8,128)(2,1)S(1)} %collective-permute-done.8.near_ref, bf16[61,16,128]{2,1,0:T(8,128)(2,1)S(1)} %collective-permute-done.9.far_ref, ...), custom_call_target="tpu_custom_call", output_to_operand_aliasing={{}: (6, {})} | custom-call | flops 4194304 | bytes 3145728 | tf_op jit(solution)/shard_map/pallas_call | solution.py:560
  56.4 0.0 collective-permute-done.7.far_ref
  56.4 2.1 %shard_map.116 = f32[480,8,128]{2,1,0:T(8,128)} custom-call(s32[8]{0:T(128)S(1)} %copy-done.2, bf16[60,16,128]{2,1,0:T(8,128)(2,1)S(1)} %shard_map.109.own_ref, bf16[60,16,128]{2,1,0:T(8,128)(2,1)S(1)} %collective-permute-done.6.near_ref, bf16[61,16,128]{2,1,0:T(8,128)(2,1)S(1)} %collective-permute-done.7.far_ref, ...), custom_call_target="tpu_custom_call", output_to_operand_aliasing={{}: (6, {})} | custom-call | flops 4194304 | bytes 3145728 | tf_op jit(solution)/shard_map/pallas_call | solution.py:560
  (11 shorter events, 0.1 us)
Async XLA Ops:
  0.6 15.9 %copy-start = (f32[8,60,8,128]{3,2,1,0:T(8,128)S(1)}, f32[8,60,8,128]{3,2,1,0:T(8,128)}, u32[]{:S(2)}) copy-start(f32[8,60,8,128]{3,2,1,0:T(8,128)} %state_ref.1) | copy-start | bytes 5898244
  0.6 15.8 %copy-start.8 = (bf16[640,368]{0,1:T(8,128)(2,1)S(1)}, bf16[640,368]{0,1:T(8,128)(2,1)}, u32[]{:S(2)}) copy-start(bf16[640,368]{0,1:T(8,128)(2,1)} %param.15) | copy-start | bytes 1413124
  0.7 15.9 %copy-start.3 = (s32[1,1,1024]{2,1,0:T(1,128)S(1)}, s32[1,1,1024]{2,1,0:T(1,128)}, u32[]{:S(2)}) copy-start(s32[1,1,1024]{2,1,0:T(1,128)} %param.16) | copy-start | bytes 12292
  0.7 15.9 %copy-start.1 = (bf16[76,8,128]{2,1,0:T(8,128)(2,1)S(1)}, bf16[76,8,128]{2,1,0:T(8,128)(2,1)}, u32[]{:S(2)}) copy-start(bf16[76,8,128]{2,1,0:T(8,128)(2,1)} %surface_ref.1) | copy-start | bytes 466948
  2.3 8.6 %collective-permute-start.2 = (bf16[18,16,128]{2,1,0:T(8,128)(2,1)S(1)}, bf16[18,16,128]{2,1,0:T(8,128)(2,1)S(1)}, u32[]{:S(2)}, u32[]{:S(2)}) collective-permute-start(bf16[18,16,128]{2,1,0:T(8,128)(2,1)S(1)} %get-tuple-element.22.own_west_ref), channel_id=1, source_target_pairs={{0,7},{1,0},{2,1},{3,2},{4,3},{5,4},{6,5},{7,6},{8,15},{9,8},{10,9... | collective-permute-start | bytes 221192 | tf_op jit(solution)/shard_map/ppermute | solution.py:577
  6.8 5.6 %collective-permute-start.3 = (bf16[18,16,128]{2,1,0:T(8,128)(2,1)S(1)}, bf16[18,16,128]{2,1,0:T(8,128)(2,1)S(1)}, u32[]{:S(2)}, u32[]{:S(2)}) collective-permute-start(bf16[18,16,128]{2,1,0:T(8,128)(2,1)S(1)} %get-tuple-element.23.own_east_ref), channel_id=1, source_target_pairs={{0,1},{1,2},{2,3},{3,4},{4,5},{5,6},{6,7},{7,0},{8,9},{9,10},{10,1... | collective-permute-start | bytes 221192 | tf_op jit(solution)/shard_map/ppermute | solution.py:577
  6.8 10.5 %collective-permute-start = (bf16[45,16,128]{2,1,0:T(8,128)(2,1)S(1)}, bf16[45,16,128]{2,1,0:T(8,128)(2,1)S(1)}, u32[]{:S(2)}, u32[]{:S(2)}) collective-permute-start(bf16[45,16,128]{2,1,0:T(8,128)(2,1)S(1)} %get-tuple-element.20), channel_id=1, source_target_pairs={{8,0},{16,8},{24,16},{9,1},{17,9},{25,17},{10,2},{18,10},{26,18},{... | collective-permute-start | bytes 552968 | tf_op jit(solution)/shard_map/ppermute | solution.py:582
  8.1 11.5 %collective-permute-start.1 = (bf16[45,16,128]{2,1,0:T(8,128)(2,1)S(1)}, bf16[45,16,128]{2,1,0:T(8,128)(2,1)S(1)}, u32[]{:S(2)}, u32[]{:S(2)}) collective-permute-start(bf16[45,16,128]{2,1,0:T(8,128)(2,1)S(1)} %get-tuple-element.21), channel_id=1, source_target_pairs={{0,8},{8,16},{16,24},{24,0},{1,9},{9,17},{17,25},{25,1},{2,10},{10... | collective-permute-start | bytes 552968 | tf_op jit(solution)/shard_map/ppermute | solution.py:577
  12.5 8.3 %collective-permute-start.4 = (bf16[9,16,128]{2,1,0:T(8,128)(2,1)S(1)}, bf16[9,16,128]{2,1,0:T(8,128)(2,1)S(1)}, u32[]{:S(2)}, u32[]{:S(2)}) collective-permute-start(bf16[9,16,128]{2,1,0:T(8,128)(2,1)S(1)} %get-tuple-element.25), channel_id=1, source_target_pairs={{8,0},{16,8},{24,16},{9,1},{17,9},{25,17},{10,2},{18,10},{26,18},{... | collective-permute-start | bytes 110600 | tf_op jit(solution)/shard_map/ppermute | solution.py:582
  13.8 7.0 %collective-permute-start.5 = (bf16[9,16,128]{2,1,0:T(8,128)(2,1)S(1)}, bf16[9,16,128]{2,1,0:T(8,128)(2,1)S(1)}, u32[]{:S(2)}, u32[]{:S(2)}) collective-permute-start(bf16[9,16,128]{2,1,0:T(8,128)(2,1)S(1)} %get-tuple-element.26), channel_id=1, source_target_pairs={{0,8},{8,16},{16,24},{24,0},{1,9},{9,17},{17,25},{25,1},{2,10},{10... | collective-permute-start | bytes 110600 | tf_op jit(solution)/shard_map/ppermute | solution.py:577
  16.5 4.3 %copy-start.4 = (bf16[768,640]{1,0:T(8,128)(2,1)S(1)}, bf16[768,640]{1,0:T(8,128)(2,1)}, u32[]{:S(2)}) copy-start(bf16[768,640]{1,0:T(8,128)(2,1)} %two_ref.1) | copy-start | bytes 2949124
  16.6 4.3 %copy-start.5 = (bf16[556,768]{1,0:T(8,128)(2,1)S(1)}, bf16[556,768]{1,0:T(8,128)(2,1)}, u32[]{:S(2)}) copy-start(bf16[556,768]{1,0:T(8,128)(2,1)} %one_ref.1) | copy-start | bytes 2562052
  16.6 4.3 %copy-start.6 = (bf16[640,512]{1,0:T(8,128)(2,1)S(1)}, bf16[640,512]{1,0:T(8,128)(2,1)}, u32[]{:S(2)}) copy-start(bf16[640,512]{1,0:T(8,128)(2,1)} %three_ref.1) | copy-start | bytes 1966084
  16.6 4.3 %copy-start.7 = (bf16[512,640]{1,0:T(8,128)(2,1)S(1)}, bf16[512,640]{1,0:T(8,128)(2,1)}, u32[]{:S(2)}) copy-start(bf16[512,640]{1,0:T(8,128)(2,1)} %four_ref.1) | copy-start | bytes 1966084
  27.7 7.5 %copy-start.2 = (s32[8]{0:T(128)S(1)}, s32[8]{0:T(128)}, u32[]{:S(2)}) copy-start(s32[8]{0:T(128)} %offset_ref.11) | copy-start | bytes 100
  27.7 7.5 %collective-permute-start.8 = (bf16[60,16,128]{2,1,0:T(8,128)(2,1)S(1)}, bf16[60,16,128]{2,1,0:T(8,128)(2,1)S(1)}, u32[]{:S(2)}, u32[]{:S(2)}) collective-permute-start(bf16[60,16,128]{2,1,0:T(8,128)(2,1)S(1)} %get-tuple-element.34.own_ref), channel_id=1, source_target_pairs={{0,1},{1,2},{2,3},{3,4},{4,5},{5,6},{6,7},{7,0},{8,9},{9,10},{10,1... | collective-permute-start | bytes 737288 | tf_op jit(solution)/shard_map/ppermute | solution.py:577
  28.5 9.3 %collective-permute-start.6 = (bf16[60,16,128]{2,1,0:T(8,128)(2,1)S(1)}, bf16[60,16,128]{2,1,0:T(8,128)(2,1)S(1)}, u32[]{:S(2)}, u32[]{:S(2)}) collective-permute-start(bf16[60,16,128]{2,1,0:T(8,128)(2,1)S(1)} %shard_map.109.own_ref), channel_id=1, source_target_pairs={{0,1},{1,2},{2,3},{3,4},{4,5},{5,6},{6,7},{7,0},{8,9},{9,10},{10,1... | collective-permute-start | bytes 737288 | tf_op jit(solution)/shard_map/ppermute | solution.py:577
  29.3 9.8 %collective-permute-start.10 = (bf16[30,16,128]{2,1,0:T(8,128)(2,1)S(1)}, bf16[30,16,128]{2,1,0:T(8,128)(2,1)S(1)}, u32[]{:S(2)}, u32[]{:S(2)}) collective-permute-start(bf16[30,16,128]{2,1,0:T(8,128)(2,1)S(1)} %get-tuple-element.35.own_ref), channel_id=1, source_target_pairs={{0,1},{1,2},{2,3},{3,4},{4,5},{5,6},{6,7},{7,0},{8,9},{9,10},{10,1... | collective-permute-start | bytes 368648 | tf_op jit(solution)/shard_map/ppermute | solution.py:577
  36.0 18.3 %collective-permute-start.9 = (bf16[61,16,128]{2,1,0:T(8,128)(2,1)S(1)}, bf16[61,16,128]{2,1,0:T(8,128)(2,1)S(1)}, u32[]{:S(2)}, u32[]{:S(2)}) collective-permute-start(bf16[61,16,128]{2,1,0:T(8,128)(2,1)S(1)} %shard_map.112), channel_id=1, source_target_pairs={{0,2},{1,3},{2,4},{3,5},{4,6},{5,7},{6,0},{7,1},{8,10},{9,11},{10,... | collective-permute-start | bytes 749576 | tf_op jit(solution)/shard_map/ppermute | solution.py:577
  38.6 17.8 %collective-permute-start.7 = (bf16[61,16,128]{2,1,0:T(8,128)(2,1)S(1)}, bf16[61,16,128]{2,1,0:T(8,128)(2,1)S(1)}, u32[]{:S(2)}, u32[]{:S(2)}) collective-permute-start(bf16[61,16,128]{2,1,0:T(8,128)(2,1)S(1)} %shard_map.110), channel_id=1, source_target_pairs={{0,2},{1,3},{2,4},{3,5},{4,6},{5,7},{6,0},{7,1},{8,10},{9,11},{10,... | collective-permute-start | bytes 749576 | tf_op jit(solution)/shard_map/ppermute | solution.py:577
  39.8 12.8 %collective-permute-start.11 = (bf16[31,16,128]{2,1,0:T(8,128)(2,1)S(1)}, bf16[31,16,128]{2,1,0:T(8,128)(2,1)S(1)}, u32[]{:S(2)}, u32[]{:S(2)}) collective-permute-start(bf16[31,16,128]{2,1,0:T(8,128)(2,1)S(1)} %shard_map.113), channel_id=1, source_target_pairs={{0,2},{1,3},{2,4},{3,5},{4,6},{5,7},{6,0},{7,1},{8,10},{9,11},{10,... | collective-permute-start | bytes 380936 | tf_op jit(solution)/shard_map/ppermute | solution.py:577

commit v4 on v3

--- a/solution.py
+++ b/solution.py
@@ -242,27 +242,52 @@
     return jnp.maximum(value, LEAK_SLOPE * value).astype(BF16)
 
 
-def tracer_update(weight, hidden, lit, state_at, out_ref, spread):
-    rows, cols = lit.shape
-    levels = weight.shape[0]
+def half_tiles(tiles, low, north):
+    rows = tiles.shape[1]
+    tiles = tiles.reshape((tiles.shape[0] // 2, 2) + tiles.shape[1:])
+    even, odd = tiles[:, 0], tiles[:, 1]
+    if north:
+        return jnp.where(low, pltpu.roll(even, rows // 2, 1), odd)
+    return jnp.where(low, even, pltpu.roll(odd, rows // 2, 1))
+
+
+def half_step(features_ref, layers, five_ref, lit_ref, state_ref, first, north, hidden_ref, tracer_ref, spread):
+    rows, cols = lit_ref.shape
+    half = rows // 2
+    levels = five_ref.shape[0]
+    low = iota((rows, cols), 0) < half
+    at = half * cols if north else 0
+    hidden = leaky(
+        lax.dot_general(
+            features_ref[:, at : at + half * cols],
+            layers[0][...],
+            (((0,), (0,)), ((), ())),
+            preferred_element_type=F32,
+        )
+    )
+    for weight in layers[1:]:
+        hidden = leaky(jnp.dot(hidden, weight[...], preferred_element_type=F32))
+    hidden_ref[...] = hidden
     result = lax.dot_general(
-        weight, hidden, (((1,), (1,)), ((), ())), preferred_element_type=F32
-    )
-    for row in range(rows):
-        spread[pl.ds(row, levels, stride=rows), :] = result[:, row * cols : (row + 1) * cols]
+        five_ref[...], hidden, (((1,), (1,)), ((), ())), preferred_element_type=F32
+    )
+    for row in range(half):
+        spread[pl.ds(row, levels, stride=half), :] = result[:, row * cols : (row + 1) * cols]
+    lit = lit_ref[...]
+    other = pltpu.roll(lit, half, 0)
+    lit = jnp.where(low, other, lit) if north else jnp.where(low, lit, other)
 
     def body(step, carry):
         value = spread[pl.ds(step * 10 * rows, 10 * rows), :].reshape(10, rows, cols)
         value = jnp.where(lit > 0.5, value.astype(BF16).astype(F32), 0.0)
-        value = state_at(step) + PHYSICS_STEP * value
-        out_ref[pl.ds(step * 5, 5)] = value.reshape(5, 2 * rows, cols).astype(BF16)
+        held = half_tiles(state_ref[pl.ds(first + step * 20, 20)], low, north)
+        tracer_ref[pl.ds(step * 5, 5)] = tall(held + PHYSICS_STEP * value)
         return carry
 
-    lax.fori_loop(0, levels // 10, body, 0)
+    lax.fori_loop(0, levels // 20, body, 0, unroll=3)
 
 
 def network_kernel(
-    parts_count,
     inner_ref,
     here_ref,
     north_ref,
@@ -277,11 +302,11 @@
     state_ref,
     winds_ref,
     upwind_ref,
+    features,
     hidden_ref,
     tracer_ref,
     strips,
     spread,
-    features,
 ):
     _, levels, rows, cols = inner_ref.shape
     per = cols // STRIP
@@ -312,102 +337,96 @@
                     upwind_ref[level] = pltpu.roll(jnp.where(lane == cols - 1, west, value), 1, 1)
         return carry
 
-    lax.fori_loop(0, packs, merge, 0, unroll=4)
+    lax.fori_loop(0, packs, merge, 0, unroll=packs)
     count = 3 * levels
     features[...] = rest_ref[...]
     for row in range(rows):
         features[0:count, row * cols : (row + 1) * cols] = winds_ref[
             pl.ds(row, count, stride=rows), :
         ].astype(BF16)
-    total = rows * cols
-    chunk = total // parts_count
-
-    for part in range(parts_count):
-        at = part * chunk
-        hidden = leaky(
-            lax.dot_general(
-                features[:, at : at + chunk],
-                one_ref[...],
-                (((0,), (0,)), ((), ())),
-                preferred_element_type=F32,
-            )
-        )
-        for weight in (two_ref, three_ref, four_ref):
-            hidden = leaky(jnp.dot(hidden, weight[...], preferred_element_type=F32))
-        hidden_ref[at : at + chunk] = hidden
-    tracer_update(
-        five_ref[...],
-        hidden_ref[...],
-        lit_ref[...],
-        lambda step: state_ref[pl.ds(3 * levels + step * 10, 10)],
+    half_step(
+        features,
+        (one_ref, two_ref, three_ref, four_ref),
+        five_ref,
+        lit_ref,
+        state_ref,
+        3 * levels,
+        False,
+        hidden_ref,
         tracer_ref,
         spread,
     )
 
 
-def network(inner_out, strips, rest, layers, five, lit, tracers, parts_count=2):
+def network(inner_out, strips, rest, layers, five, lit, flat):
     _, levels, rows, cols = inner_out.shape
     count = five.shape[0]
-    width = layers[3].shape[1]
-    return pl.pallas_call(
-        functools.partial(network_kernel, parts_count),
+    return pl.pallas_call(
+        network_kernel,
         out_shape=(
             jax.ShapeDtypeStruct((3 * levels * rows, cols), F32),
             jax.ShapeDtypeStruct((levels, rows, cols), F32),
-            jax.ShapeDtypeStruct((rows * cols, width), BF16),
-            jax.ShapeDtypeStruct((count // 2, 2 * rows, cols), BF16),
+            jax.ShapeDtypeStruct(rest.shape, BF16),
+            jax.ShapeDtypeStruct((rows * cols // 2, layers[3].shape[1]), BF16),
+            jax.ShapeDtypeStruct((count // 4, 2 * rows, cols), BF16),
         ),
         in_specs=[vmem()] * 12,
-        out_specs=(vmem(),) * 4,
+        out_specs=(vmem(),) * 5,
         scratch_shapes=[
             pltpu.VMEM((3, levels * STRIP // (cols - cols % STRIP), rows, cols), F32),
-            pltpu.VMEM((count * rows, cols), F32),
-            pltpu.VMEM(rest.shape, BF16),
+            pltpu.VMEM((count * rows // 2, cols), F32),
         ],
         compiler_params=params(32),
-        cost_estimate=cost(4 << 30, 8 << 20),
-    )(inner_out, *strips, rest, *layers, five, lit, tracers)
-
-
-def second_kernel(start, hidden_ref, five_ref, lit_ref, state_ref, tracer_ref, spread):
-    tracer_update(
-        five_ref[...],
-        hidden_ref[...],
-        lit_ref[...],
-        lambda step: state_ref[pl.ds(start + step * 10, 10)],
-        tracer_ref,
-        spread,
-    )
-
-
-def second(start, hidden, five, lit, tracers):
+        cost_estimate=cost(3 << 30, 8 << 20),
+    )(inner_out, *strips, rest, *layers, five, lit, flat)
+
+
+def second_kernel(
+    first, features_ref, one_ref, two_ref, three_ref, four_ref, five_ref, lit_ref, state_ref,
+    hidden_ref, tracer_ref, spread,
+):
+    layers = (one_ref, two_ref, three_ref, four_ref)
+    half_step(
+        features_ref, layers, five_ref, lit_ref, state_ref, first, True, hidden_ref, tracer_ref, spread
+    )
+
+
+def second(first, features, layers, five, lit, flat):
     rows, cols = lit.shape
     count = five.shape[0]
     return pl.pallas_call(
-        functools.partial(second_kernel, start),
-        out_shape=jax.ShapeDtypeStruct((count // 2, 2 * rows, cols), BF16),
-        in_specs=[vmem()] * 4,
-        out_specs=vmem(),
-        scratch_shapes=[pltpu.VMEM((count * rows, cols), F32)],
-        compiler_params=params(16),
-        cost_estimate=cost(1 << 28, 3 << 20),
-    )(hidden, five, lit, tracers)
+        functools.partial(second_kernel, first),
+        out_shape=(
+            jax.ShapeDtypeStruct((rows * cols // 2, layers[3].shape[1]), BF16),
+            jax.ShapeDtypeStruct((count // 4, 2 * rows, cols), BF16),
+        ),
+        in_specs=[vmem()] * 8,
+        out_specs=(vmem(),) * 2,
+        scratch_shapes=[pltpu.VMEM((count * rows // 2, cols), F32)],
+        compiler_params=params(24),
+        cost_estimate=cost(2 << 30, 6 << 20),
+    )(features, *layers, five, lit, flat)
 
 
 def winds_kernel(
-    hidden_ref, five_ref, lit_ref, winds_ref, upwind_ref, out_ref, flux_ref, stay_ref, come_ref,
+    south_ref, north_ref, five_ref, lit_ref, winds_ref, upwind_ref, out_ref, flux_ref,
+    stay_ref, come_ref, stay_south_ref, come_south_ref, stay_north_ref, come_north_ref,
     spread, updated, sem
 ):
     rows, cols = lit_ref.shape
     levels = upwind_ref.shape[0]
     fluxes = flux_ref.shape[0]
-    result = lax.dot_general(
-        five_ref[...], hidden_ref[...], (((1,), (1,)), ((), ())), preferred_element_type=F32
-    )
     count = five_ref.shape[0]
-    for row in range(rows):
-        spread[pl.ds(row, count, stride=rows), :] = result[:, row * cols : (row + 1) * cols]
+    for side, hidden_ref in enumerate((south_ref, north_ref)):
+        result = lax.dot_general(
+            five_ref[...], hidden_ref[...], (((1,), (1,)), ((), ())), preferred_element_type=F32
+        )
+        for row in range(rows // 2):
+            spread[pl.ds(side * (rows // 2) + row, count, stride=rows), :] = result[
+                :, row * cols : (row + 1) * cols
+            ]
     lit = lit_ref[...] > 0.5
+    low = iota((rows, cols), 0) < rows // 2
 
     def body(step, carry):
         value = spread[pl.ds(step * 10 * rows, 10 * rows), :].reshape(10, rows, cols)
@@ -429,18 +448,25 @@
 
     def share(step, carry):
         here = winds_ref[pl.ds(step * 10 * rows, 10 * rows), :].reshape(10, rows, cols)
-        stay_ref[pl.ds(step * 10, 10)] = 0.5 - 0.45 * jnp.tanh(here)
-        come_ref[pl.ds(step * 10, 10)] = 0.5 + 0.45 * jnp.tanh(upwind_ref[pl.ds(step * 10, 10)])
+        stay = 0.5 - 0.45 * jnp.tanh(here)
+        come = 0.5 + 0.45 * jnp.tanh(upwind_ref[pl.ds(step * 10, 10)])
+        stay_ref[pl.ds(step * 10, 10)] = stay
+        come_ref[pl.ds(step * 10, 10)] = come
+        stay_south_ref[pl.ds(step * 5, 5)] = half_tiles(stay, low, False)
+        come_south_ref[pl.ds(step * 5, 5)] = half_tiles(come, low, False)
+        stay_north_ref[pl.ds(step * 5, 5)] = half_tiles(stay, low, True)
+        come_north_ref[pl.ds(step * 5, 5)] = half_tiles(come, low, True)
         return carry
 
     lax.fori_loop(0, levels // 10, share, 0)
     copy.wait()
 
 
-def winds_out(hidden, five, lit, winds, upwind, fields):
+def winds_out(hidden_south, hidden_north, five, lit, winds, upwind, fields):
     levels, rows, cols = upwind.shape
     fluxes = five.shape[0] - 2 * levels
     share = jax.ShapeDtypeStruct((levels, rows, cols), F32)
+    part = jax.ShapeDtypeStruct((levels // 2, rows, cols), F32)
     return pl.pallas_call(
         winds_kernel,
         out_shape=(
@@ -448,9 +474,13 @@
             jax.ShapeDtypeStruct((fluxes, rows, cols), BF16),
             share,
             share,
+            part,
+            part,
+            part,
+            part,
         ),
-        in_specs=[vmem()] * 5,
-        out_specs=(any_space(), vmem(), vmem(), vmem()),
+        in_specs=[vmem()] * 6,
+        out_specs=(any_space(),) + (vmem(),) * 7,
         scratch_shapes=[
             pltpu.VMEM((five.shape[0] * rows, cols), F32),
             pltpu.VMEM((3 * levels, rows, cols), F32),
@@ -458,14 +488,15 @@
         ],
         compiler_params=params(16),
         cost_estimate=cost(1 << 28, 4 << 20),
-    )(hidden, five, lit, winds, upwind)
-
-
-def spread_offsets(offset_ref, rows, cols):
-    place = iota((rows, cols), 0)
+    )(hidden_south, hidden_north, five, lit, winds, upwind)
+
+
+def spread_offsets(offset_ref, shape, base, span):
+    rows, cols = shape
+    place = iota((rows, cols), 0) % span
     offset = jnp.zeros((rows, cols), jnp.int32)
-    for row in range(rows):
-        offset = jnp.where(place == row, offset_ref[row], offset)
+    for row in range(span):
+        offset = jnp.where(place == row, offset_ref[base + row], offset)
     return offset // cols, offset % cols
 
 
@@ -473,11 +504,11 @@
     return jnp.take_along_axis(value, index, axis=1, mode="promise_in_bounds")
 
 
-def relay_kernel(offset_ref, own_ref, near_ref, out_ref):
+def relay_kernel(base, span, offset_ref, own_ref, near_ref, out_ref):
     rows = own_ref.shape[1] // 2
     cols = own_ref.shape[2]
     pairs = own_ref.shape[0]
-    blocks, cells = spread_offsets(offset_ref, rows, cols)
+    blocks, cells = spread_offsets(offset_ref, (rows, cols), base, span)
     lane = iota((rows, cols), 1)
     take_near = (blocks >= 2) & (lane > cols - 1 - cells)
     edge = cols - 1 - cells
@@ -496,10 +527,10 @@
     out_ref[pairs] = jnp.concatenate([column, column], axis=0).astype(BF16)
 
 
-def relay(offset, own, near):
+def relay(offset, own, near, base, span):
     pairs, height, cols = own.shape
     return pl.pallas_call(
-        relay_kernel,
+        functools.partial(relay_kernel, base, span),
         out_shape=jax.ShapeDtypeStruct((pairs + 1, height, cols), BF16),
         in_specs=[pl.BlockSpec(memory_space=pltpu.SMEM), vmem(), vmem()],
         out_specs=vmem(),
@@ -508,68 +539,171 @@
     )(offset, own, near)
 
 
-def advect_kernel(
-    first, group, offset_ref, own_ref, near_ref, far_ref, stay_ref, come_ref, whole_ref, out_ref, result, sem
-):
-    levels, rows, cols = stay_ref.shape
-    pairs = own_ref.shape[0]
-    blocks, cells = spread_offsets(offset_ref, rows, cols)
+def blend(offset_ref, shape, base, span):
+    rows, cols = shape
+    blocks, cells = spread_offsets(offset_ref, shape, base, span)
     lane = iota((rows, cols), 1)
     from_right = lane <= cols - 1 - cells
     index = (lane - cells) & (cols - 1)
-    column = far_ref[pairs].astype(F32)[:rows]
+    edge_index = cols - 1 - cells
     is_zero, is_one, is_two = blocks == 0, blocks == 1, blocks >= 2
-    steps = levels // group
-    edge_index = cols - 1 - cells
-
-    def body(step, carry):
-        at = pl.ds(step * (group // 2), group // 2)
-        share = pl.ds(lax.rem(step, steps) * group, group)
-        own = own_ref[at].astype(F32).reshape(group, rows, cols)
-        near = near_ref[at].astype(F32).reshape(group, rows, cols)
-        far = far_ref[at].astype(F32).reshape(group, rows, cols)
-        stay = stay_ref[share]
-        come = come_ref[share]
+
+    def tiles(own, near, far, column, stay, come, first):
         right = jnp.where(is_zero, own, jnp.where(is_one, near, far))
         left = jnp.where(is_zero, near, far)
         merged = jnp.where(from_right, right, left)
         edges = jnp.where(is_two, column, left)
-        for level in range(group):
-            which = jnp.where(is_two, step * group + level, edge_index)
-            here = along(merged[level], index)
-            behind = jnp.where(lane == 0, along(edges[level], which), pltpu.roll(here, 1, 1))
-            result[step * group + level] = stay[level] * here + come[level] * behind
+        values = []
+        for tile in range(own.shape[0]):
+            which = jnp.where(is_two, first + tile, edge_index)
+            here = along(merged[tile], index)
+            behind = jnp.where(lane == 0, along(edges[tile], which), pltpu.roll(here, 1, 1))
+            values.append(stay[tile] * here + come[tile] * behind)
+        return values
+
+    return tiles
+
+
+def read_tiles(refs, step, group, shape):
+    at = pl.ds(step * (group // 2), group // 2)
+    return [ref[at].astype(F32).reshape((group,) + shape) for ref in refs]
+
+
+def last_column(far_ref, pairs, rows):
+    return far_ref[pairs].astype(F32)[:rows]
+
+
+def advect_ozone_kernel(
+    first, offset_ref, own_ref, near_ref, far_ref, stay_ref, come_ref, whole_ref, out_ref, result, sem
+):
+    levels, rows, cols = stay_ref.shape
+    group = levels // 2
+    tiles = blend(offset_ref, (rows, cols), 0, rows)
+    column = last_column(far_ref, own_ref.shape[0], rows)
+    copies = []
+    for step in range(2):
+        share = pl.ds(step * group, group)
+        values = tiles(
+            *read_tiles((own_ref, near_ref, far_ref), step, group, (rows, cols)),
+            column,
+            stay_ref[share],
+            come_ref[share],
+            step * group,
+        )
+        for tile, value in enumerate(values):
+            result[step * group + tile] = value
+        copy = pltpu.make_async_copy(
+            result.at[share], out_ref.at[pl.ds(first * levels + step * group, group)], sem.at[step]
+        )
+        copy.start()
+        copies.append(copy)
+    for copy in copies:
+        copy.wait()
+
+
+def advect_ozone(first, offset, own, near, far, stay, come, whole):
+    levels, rows, cols = stay.shape
+    return pl.pallas_call(
+        functools.partial(advect_ozone_kernel, first),
+        out_shape=jax.ShapeDtypeStruct(whole.shape, F32),
+        in_specs=[pl.BlockSpec(memory_space=pltpu.SMEM)] + [vmem()] * 5 + [any_space()],
+        out_specs=any_space(),
+        scratch_shapes=[pltpu.VMEM((levels, rows, cols), F32), pltpu.SemaphoreType.DMA((2,))],
+        input_output_aliases={6: 0},
+        compiler_params=params(8),
+        cost_estimate=cost(1 << 22, 2 << 20),
+    )(offset, own, near, far, stay, come, whole)
+
+
+def advect_south_kernel(offset_ref, own_ref, near_ref, far_ref, stay_ref, come_ref, out_ref):
+    group, rows, cols = stay_ref.shape
+    pairs = own_ref.shape[0]
+    tiles = blend(offset_ref, (rows, cols), 0, rows // 2)
+    column = last_column(far_ref, pairs, rows)
+
+    def body(step, carry):
+        values = tiles(
+            *read_tiles((own_ref, near_ref, far_ref), step, group, (rows, cols)),
+            column,
+            stay_ref[...],
+            come_ref[...],
+            step * group,
+        )
+        for tile, value in enumerate(values):
+            out_ref[step * group + tile] = value
+        return carry
+
+    lax.fori_loop(0, 2 * pairs // group, body, 0)
+
+
+def advect_south(offset, own, near, far, stay, come):
+    pairs, height, cols = own.shape
+    return pl.pallas_call(
+        advect_south_kernel,
+        out_shape=jax.ShapeDtypeStruct((2 * pairs, height // 2, cols), F32),
+        in_specs=[pl.BlockSpec(memory_space=pltpu.SMEM)] + [vmem()] * 5,
+        out_specs=vmem(),
+        compiler_params=params(8),
+        cost_estimate=cost(1 << 22, 2 << 20),
+    )(offset, own, near, far, stay, come)
+
+
+def advect_north_kernel(
+    first, offset_ref, own_ref, near_ref, far_ref, stay_ref, come_ref, south_ref, whole_ref, out_ref,
+    result, sem,
+):
+    group, rows, cols = stay_ref.shape
+    pairs = own_ref.shape[0]
+    tiles = blend(offset_ref, (rows, cols), rows // 2, rows // 2)
+    column = last_column(far_ref, pairs, rows)
+    low = iota((rows, cols), 0) < rows // 2
+    count = 2 * pairs // group
+
+    def copy_of(step):
+        span = pl.ds(step * 2 * group, 2 * group)
+        return pltpu.make_async_copy(
+            result.at[span],
+            out_ref.at[pl.ds((first + step) * 2 * group, 2 * group)],
+            sem.at[step],
+        )
+
+    def body(step, carry):
+        values = tiles(
+            *read_tiles((own_ref, near_ref, far_ref), step, group, (rows, cols)),
+            column,
+            stay_ref[...],
+            come_ref[...],
+            step * group,
+        )
+        for tile, north in enumerate(values):
+            at = step * group + tile
+            south = south_ref[at]
+            result[2 * at] = jnp.where(low, south, pltpu.roll(north, rows // 2, 0))
+            result[2 * at + 1] = jnp.where(low, pltpu.roll(south, rows // 2, 0), north)
         copy_of(step).start()
         return carry
 
-    def copy_of(step):
-        return pltpu.make_async_copy(
-            result.at[pl.ds(step * group, group)],
-            out_ref.at[pl.ds(first * levels + step * group, group)],
-            sem.at[step],
-        )
-
-    count = 2 * pairs // group
     lax.fori_loop(0, count, body, 0)
     for step in range(count):
         copy_of(step).wait()
 
 
-def advect(first, offset, own, near, far, stay, come, whole, group=30):
+def advect_north(first, offset, own, near, far, stay, come, south, whole):
     pairs, height, cols = own.shape
-    return pl.pallas_call(
-        functools.partial(advect_kernel, first, group),
+    count = 2 * pairs // stay.shape[0]
+    return pl.pallas_call(
+        functools.partial(advect_north_kernel, first),
         out_shape=jax.ShapeDtypeStruct(whole.shape, F32),
-        in_specs=[pl.BlockSpec(memory_space=pltpu.SMEM)] + [vmem()] * 5 + [any_space()],
+        in_specs=[pl.BlockSpec(memory_space=pltpu.SMEM)] + [vmem()] * 6 + [any_space()],
         out_specs=any_space(),
         scratch_shapes=[
-            pltpu.VMEM((2 * pairs, height // 2, cols), F32),
-            pltpu.SemaphoreType.DMA((2 * pairs // group,)),
+            pltpu.VMEM((4 * pairs, height // 2, cols), F32),
+            pltpu.SemaphoreType.DMA((count,)),
         ],
-        input_output_aliases={6: 0},
-        compiler_params=params(12),
-        cost_estimate=cost(1 << 22, 3 << 20),
-    )(offset, own, near, far, stay, come, whole)
+        input_output_aliases={7: 0},
+        compiler_params=params(16),
+        cost_estimate=cost(1 << 22, 4 << 20),
+    )(offset, own, near, far, stay, come, south, whole)
 
 
 def shifted(value, axis, steps):
@@ -623,35 +757,36 @@
     strips_from_north = passed_along(strips_south, "lat", -1)
 
     five = layer_five.T
-    five_first = five[2 * levels : 4 * levels]
-    five_second = five[4 * levels : 6 * levels]
+    five_tracers = five[2 * levels : 6 * levels]
     five_winds = jnp.concatenate([five[: 2 * levels], five[6 * levels :]], axis=0)
 
     inner_out = inner(start_winds, from_north, from_south)
-    ozone_relay = relay(row_offset, ozone, ozone_near)
+    ozone_relay = relay(row_offset, ozone, ozone_near, 0, rows)
     ozone_far = shifted(ozone_relay, "lon", 2)
-    winds, upwind, hidden, first = network(
+    winds, upwind, features, hidden_south, first = network(
         inner_out,
         (strips, strips_from_north, strips_from_south),
         rest,
         layers,
-        five_first,
+        five_tracers,
         lit,
         flat,
     )
     first_near = shifted(first, "lon", 1)
-    other = second(5 * levels, hidden, five_second, lit, flat)
+    hidden_north, other = second(3 * levels, features, layers, five_tracers, lit, flat)
     other_near = shifted(other, "lon", 1)
-    first_relay = relay(row_offset, first, first_near)
+    first_relay = relay(row_offset, first, first_near, 0, rows // 2)
     first_far = shifted(first_relay, "lon", 2)
-    other_relay = relay(row_offset, other, other_near)
+    other_relay = relay(row_offset, other, other_near, rows // 2, rows // 2)
     other_far = shifted(other_relay, "lon", 2)
-    whole, flux, stay, come = winds_out(hidden, five_winds, lit, winds, upwind, fields)
-    whole = advect(
-        fields - 1, row_offset, ozone, ozone_near, ozone_far, stay, come, whole
-    )
-    whole = advect(3, row_offset, first, first_near, first_far, stay, come, whole)
-    whole = advect(5, row_offset, other, other_near, other_far, stay, come, whole)
+    whole, flux, stay, come, stay_south, come_south, stay_north, come_north = winds_out(
+        hidden_south, hidden_north, five_winds, lit, winds, upwind, fields
+    )
+    whole = advect_ozone(fields - 1, row_offset, ozone, ozone_near, ozone_far, stay, come, whole)
+    south = advect_south(row_offset, first, first_near, first_far, stay_south, come_south)
+    whole = advect_north(
+        3, row_offset, other, other_near, other_far, stay_north, come_north, south, whole
+    )
     return whole.reshape(fields, levels, rows, cols), flux
 
 

time: 58.7 us -> 58.7 us (level)
  waiting for transfers between devices: 22.3 us -> 23.7 us
  starting transfers between devices: 13.7 us -> 12.7 us
  Pallas kernels: 20.2 us -> 19.3 us
    ppermute x10, waiting for transfers between devices: 22.3 us -> 23.7 us  [shifted(): lax.ppermute(value, axis, [(i, (i + steps) % count) for i in range(count)])]
    ppermute x10, starting transfers between devices: 11.1 us -> 10.1 us  [shifted(): lax.ppermute(value, axis, [(i, (i + steps) % count) for i in range(count)])]
    pallas_call x8, Pallas kernels: 15.8 us -> 14.8 us  [the longest x1 3.94 us: network(): pl.pallas_call(network_kernel, out_shape=(jax.ShapeDtypeStruct((3 * level...]
  transfers between devices with their start and end apart: 12 -> 12, of which waited for: 6 -> 7; matrix products, arithmetic and copies ran while one was open for 0% -> 0% of each run, Pallas kernels for 19% -> 22%
where the time goes in v4:
time: 58.7 us; the launch traced here: 58 us
  waiting for transfers between devices  23.7 us (40%)
  Pallas kernels  19.3 us (33%)
  starting transfers between devices  12.7 us (22%)
  local copies, waits for them, and re-layouts  1.42 us (2%)
  between operations  0.93 us (2%)
    ppermute x10, waiting for transfers between devices, shifted(): lax.ppermute(value, axis, [(i, (i + steps) % count) for i in range(count)])  23.7 us
    ppermute x10, starting transfers between devices, shifted(): lax.ppermute(value, axis, [(i, (i + steps) % count) for i in range(count)])  10.1 us
    pallas_call x1, Pallas kernels, network(): pl.pallas_call(network_kernel, out_shape=(jax.ShapeDtypeStruct((3 * level...  3.94 us
    pallas_call x1, Pallas kernels, second(): pl.pallas_call(functools.partial(second_kernel, first), out_shape=(jax.Sh...  2.93 us
    ppermute x2, starting transfers between devices, passed_along(): lax.ppermute(block, axis, [(i, i + distance) for i in devices if i + dist...  2.58 us
    pallas_call x1, Pallas kernels, winds_out(): pl.pallas_call(winds_kernel, out_shape=(jax.ShapeDtypeStruct((fields * le...  2.22 us
    pallas_call x3, Pallas kernels, relay(): pl.pallas_call(functools.partial(relay_kernel, base, span), out_shape=jax...  2.21 us
    pallas_call x1, Pallas kernels, advect_north(): pl.pallas_call(functools.partial(advect_north_kernel, first), out_shape=j...  2.2 us
  transfers between devices with their start and end apart: 12, of which 7 were waited for; matrix products, arithmetic and copies ran while one was open for 0% of the time, Pallas kernels for 22%

profile of v4, /device:TPU:0, one launch (start us, length us, event | category | flops | bytes accessed | tf_op | source)
XLA Modules:
  0.0 58.0 jit_solution(11713530812153440717)
XLA Ops:
  0.6 0.0 copy-start
  0.7 1.3 %slice.12.winds_ref.state_ref = f32[3,60,8,128]{3,2,1,0:T(8,128)S(1)} slice(f32[8,60,8,128]{3,2,1,0:T(8,128)} %state_ref.1), slice={[0:3], [0:60], [0:8], [0:128]} | slice | bytes 1474560 | tf_op jit(solution)/shard_map/slice | solution.py:747
  2.0 0.3 shard_map.104
  2.3 1.3 %collective-permute-start = (bf16[45,16,128]{2,1,0:T(8,128)(2,1)S(1)}, bf16[45,16,128]{2,1,0:T(8,128)(2,1)S(1)}, u32[]{:S(2)}, u32[]{:S(2)}) collective-permute-start(bf16[45,16,128]{2,1,0:T(8,128)(2,1)S(1)} %get-tuple-element.27), channel_id=1, source_target_pairs={{8,0},{16,8},{24,16},{9,1},{17,9},{25,17},{10,2},{18,10},{26,18},{... | collective-permute-start | bytes 552968 | tf_op jit(solution)/shard_map/ppermute | solution.py:716
  3.6 3.6 %collective-permute-start.1 = (bf16[45,16,128]{2,1,0:T(8,128)(2,1)S(1)}, bf16[45,16,128]{2,1,0:T(8,128)(2,1)S(1)}, u32[]{:S(2)}, u32[]{:S(2)}) collective-permute-start(bf16[45,16,128]{2,1,0:T(8,128)(2,1)S(1)} %get-tuple-element.28), channel_id=1, source_target_pairs={{0,8},{8,16},{16,24},{24,0},{1,9},{9,17},{17,25},{25,1},{2,10},{10... | collective-permute-start | bytes 552968 | tf_op jit(solution)/shard_map/ppermute | solution.py:711
  7.2 3.0 %collective-permute-start.2 = (bf16[18,16,128]{2,1,0:T(8,128)(2,1)S(1)}, bf16[18,16,128]{2,1,0:T(8,128)(2,1)S(1)}, u32[]{:S(2)}, u32[]{:S(2)}) collective-permute-start(bf16[18,16,128]{2,1,0:T(8,128)(2,1)S(1)} %get-tuple-element.29.own_west_ref), channel_id=1, source_target_pairs={{0,7},{1,0},{2,1},{3,2},{4,3},{5,4},{6,5},{7,6},{8,15},{9,8},{10,9... | collective-permute-start | bytes 221192 | tf_op jit(solution)/shard_map/ppermute | solution.py:711
  10.2 0.0 collective-permute-start.3
  10.2 2.0 %collective-permute-done.2.from_east_ref = bf16[18,16,128]{2,1,0:T(8,128)(2,1)S(1)} collective-permute-done((bf16[18,16,128]{2,1,0:T(8,128)(2,1)S(1)}, bf16[18,16,128]{2,1,0:T(8,128)(2,1)S(1)}, u32[]{:S(2)}, u32[]{:S(2)}) %collective-permute-start.2) | collective-permute-done | bytes 73760 | tf_op jit(solution)/shard_map/ppermute | solution.py:711
  12.2 3.6 %collective-permute-done.3.from_west_ref = bf16[18,16,128]{2,1,0:T(8,128)(2,1)S(1)} collective-permute-done((bf16[18,16,128]{2,1,0:T(8,128)(2,1)S(1)}, bf16[18,16,128]{2,1,0:T(8,128)(2,1)S(1)}, u32[]{:S(2)}, u32[]{:S(2)}) %collective-permute-start.3) | collective-permute-done | bytes 73760 | tf_op jit(solution)/shard_map/ppermute | solution.py:711
  15.8 0.1 shard_map.106
  15.8 1.3 %collective-permute-start.4 = (bf16[9,16,128]{2,1,0:T(8,128)(2,1)S(1)}, bf16[9,16,128]{2,1,0:T(8,128)(2,1)S(1)}, u32[]{:S(2)}, u32[]{:S(2)}) collective-permute-start(bf16[9,16,128]{2,1,0:T(8,128)(2,1)S(1)} %get-tuple-element.32), channel_id=1, source_target_pairs={{8,0},{16,8},{24,16},{9,1},{17,9},{25,17},{10,2},{18,10},{26,18},{... | collective-permute-start | bytes 110600 | tf_op jit(solution)/shard_map/ppermute | solution.py:716
  17.1 3.1 %collective-permute-start.5 = (bf16[9,16,128]{2,1,0:T(8,128)(2,1)S(1)}, bf16[9,16,128]{2,1,0:T(8,128)(2,1)S(1)}, u32[]{:S(2)}, u32[]{:S(2)}) collective-permute-start(bf16[9,16,128]{2,1,0:T(8,128)(2,1)S(1)} %get-tuple-element.33), channel_id=1, source_target_pairs={{0,8},{8,16},{16,24},{24,0},{1,9},{9,17},{17,25},{25,1},{2,10},{10... | collective-permute-start | bytes 110600 | tf_op jit(solution)/shard_map/ppermute | solution.py:711
  20.3 0.0 copy-done
  20.3 0.0 copy-done.3
  20.3 0.0 copy-done.1
  20.3 0.0 copy-start.4
  20.3 0.0 copy-start.5
  20.3 0.0 copy-start.6
  20.3 0.0 copy-start.7
  20.3 0.8 %shard_map.107 = (bf16[556,1024]{1,0:T(8,128)(2,1)S(1)}, f32[8,128]{1,0:T(8,128)S(1)}, bf16[30,16,128]{2,1,0:T(8,128)(2,1)S(1)}) custom-call(f32[8,60,8,128]{3,2,1,0:T(8,128)S(1)} %copy-done, bf16[76,8,128]{2,1,0:T(8,128)(2,1)S(1)} %copy-done.1, s32[1,1024]{1,0:T(1,128)S(1)} %bitcast.6), custom_call_target="tpu_custom_call" | custom-call | flops 16777216 | bytes 4194304 | tf_op jit(solution)/shard_map/pallas_call | solution.py:223
  21.1 0.0 collective-permute-done.from_north_ref
  21.1 0.0 collective-permute-done.1.from_south_ref
  21.1 1.1 %shard_map.105.inner_ref = f32[3,60,8,128]{3,2,1,0:T(8,128)S(1)} custom-call(f32[3,60,8,128]{3,2,1,0:T(8,128)S(1)} %slice.12.winds_ref.state_ref, bf16[45,16,128]{2,1,0:T(8,128)(2,1)S(1)} %collective-permute-done.from_north_ref, bf16[45,16,128]{2,1,0:T(8,128)(2,1)S(1)} %collective-permute-done.1.from_south_ref), custom_call_target="tpu_custom_call" | custom-call | flops 16777216 | bytes 4194304 | tf_op jit(solution)/shard_map/pallas_call | solution.py:187
  22.3 0.0 collective-permute-done.4.north_ref
  22.3 0.8 %collective-permute-done.5.south_ref = bf16[9,16,128]{2,1,0:T(8,128)(2,1)S(1)} collective-permute-done((bf16[9,16,128]{2,1,0:T(8,128)(2,1)S(1)}, bf16[9,16,128]{2,1,0:T(8,128)(2,1)S(1)}, u32[]{:S(2)}, u32[]{:S(2)}) %collective-permute-start.5) | collective-permute-done | bytes 36896 | tf_op jit(solution)/shard_map/ppermute | solution.py:711
  23.1 3.9 %shard_map.108 = (f32[1440,128]{1,0:T(8,128)S(1)}, f32[60,8,128]{2,1,0:T(8,128)S(1)}, bf16[556,1024]{1,0:T(8,128)(2,1)S(1)}, bf16[512,640]{1,0:T(8,128)(2,1)S(1)}, bf16[60,16,128]{2,1,0:T(8,128)(2,1)S(1)}) custom-call(f32[3,60,8,128]{3,2,1,0:T(8,128)S(1)} %shard_map.105.inner_ref, f32[36,8,128]{2,1,0:T(8,128)S(1)} %get-tuple-element.31.here_ref, ...), custom_call_target="tpu_custom_call" | custom-call | flops 3221225472 | bytes 8388608 | tf_op jit(solution)/shard_map/pallas_call | solution.py:364
  27.0 0.1 collective-permute-start.8
  27.1 0.0 copy-start.2
  27.1 2.9 %shard_map.109 = (bf16[512,640]{1,0:T(8,128)(2,1)S(1)}, bf16[60,16,128]{2,1,0:T(8,128)(2,1)S(1)}) custom-call(bf16[556,1024]{1,0:T(8,128)(2,1)S(1)} %get-tuple-element.36.features_ref, bf16[556,768]{1,0:T(8,128)(2,1)S(1)} %copy-done.5, bf16[768,640]{1,0:T(8,128)(2,1)S(1)} %copy-done.4, bf16[640,512]{1,0:T(8,128)(2,1)S(1)} %copy-done.6, ...), custom_call_target="tpu_custom_call" | custom-call | flops 2147483648 | bytes 6291456 | tf_op jit(solution)/shard_map/pallas_call | solution.py:397
  30.0 0.1 collective-permute-start.6
  30.1 0.1 collective-permute-start.10
  30.2 4.3 %collective-permute-done.8.near_ref = bf16[60,16,128]{2,1,0:T(8,128)(2,1)S(1)} collective-permute-done((bf16[60,16,128]{2,1,0:T(8,128)(2,1)S(1)}, bf16[60,16,128]{2,1,0:T(8,128)(2,1)S(1)}, u32[]{:S(2)}, u32[]{:S(2)}) %collective-permute-start.8) | collective-permute-done | bytes 245792 | tf_op jit(solution)/shard_map/ppermute | solution.py:711
  34.5 0.0 copy-done.2
  34.5 0.8 %shard_map.112 = bf16[61,16,128]{2,1,0:T(8,128)(2,1)S(1)} custom-call(s32[8]{0:T(128)S(1)} %copy-done.2, bf16[60,16,128]{2,1,0:T(8,128)(2,1)S(1)} %get-tuple-element.44.own_ref, bf16[60,16,128]{2,1,0:T(8,128)(2,1)S(1)} %collective-permute-done.8.near_ref), custom_call_target="tpu_custom_call" | custom-call | flops 1048576 | bytes 1048576 | tf_op jit(solution)/shard_map/pallas_call | solution.py:532
  35.3 0.1 collective-permute-start.9
  35.3 2.2 %collective-permute-done.6.near_ref = bf16[60,16,128]{2,1,0:T(8,128)(2,1)S(1)} collective-permute-done((bf16[60,16,128]{2,1,0:T(8,128)(2,1)S(1)}, bf16[60,16,128]{2,1,0:T(8,128)(2,1)S(1)}, u32[]{:S(2)}, u32[]{:S(2)}) %collective-permute-start.6) | collective-permute-done | bytes 245792 | tf_op jit(solution)/shard_map/ppermute | solution.py:711
  37.5 0.8 %shard_map.110 = bf16[61,16,128]{2,1,0:T(8,128)(2,1)S(1)} custom-call(s32[8]{0:T(128)S(1)} %copy-done.2, bf16[60,16,128]{2,1,0:T(8,128)(2,1)S(1)} %get-tuple-element.37.own_ref, bf16[60,16,128]{2,1,0:T(8,128)(2,1)S(1)} %collective-permute-done.6.near_ref), custom_call_target="tpu_custom_call" | custom-call | flops 1048576 | bytes 1048576 | tf_op jit(solution)/shard_map/pallas_call | solution.py:532
  38.3 0.1 collective-permute-start.7
  38.4 0.4 collective-permute-done.10.near_ref
  38.8 0.7 %shard_map.114 = bf16[31,16,128]{2,1,0:T(8,128)(2,1)S(1)} custom-call(s32[8]{0:T(128)S(1)} %copy-done.2, bf16[30,16,128]{2,1,0:T(8,128)(2,1)S(1)} %get-tuple-element.47.own_ref, bf16[30,16,128]{2,1,0:T(8,128)(2,1)S(1)} %collective-permute-done.10.near_ref), custom_call_target="tpu_custom_call" | custom-call | flops 1048576 | bytes 1048576 | tf_op jit(solution)/shard_map/pallas_call | solution.py:532
  39.5 0.1 collective-permute-start.11
  39.6 2.2 %shard_map.111 = (f32[480,8,128]{2,1,0:T(8,128)}, bf16[8,8,128]{2,1,0:T(8,128)(2,1)}, f32[60,8,128]{2,1,0:T(8,128)S(1)}, f32[60,8,128]{2,1,0:T(8,128)S(1)}, f32[...) custom-call(bf16[512,640]{1,0:T(8,128)(2,1)S(1)} %get-tuple-element.38, ...), custom_call_target="tpu_custom_call" | custom-call | flops 268435456 | bytes 4194304 | tf_op jit(solution)/shard_map/pallas_call | solution.py:470
  41.8 10.4 %collective-permute-done.11.far_ref = bf16[31,16,128]{2,1,0:T(8,128)(2,1)S(1)} collective-permute-done((bf16[31,16,128]{2,1,0:T(8,128)(2,1)S(1)}, bf16[31,16,128]{2,1,0:T(8,128)(2,1)S(1)}, u32[]{:S(2)}, u32[]{:S(2)}) %collective-permute-start.11) | collective-permute-done | bytes 127008 | tf_op jit(solution)/shard_map/ppermute | solution.py:711
  52.3 2.1 %shard_map.115.whole_ref = f32[480,8,128]{2,1,0:T(8,128)} custom-call(s32[8]{0:T(128)S(1)} %copy-done.2, bf16[30,16,128]{2,1,0:T(8,128)(2,1)S(1)} %get-tuple-element.47.own_ref, bf16[30,16,128]{2,1,0:T(8,128)(2,1)S(1)} %collective-permute-done.10.near_ref, bf16[31,16,128]{2,1,0:T(8,128)(2,1)S(1)} %collective-permute-done.11.far_ref, ...), custom_call_target="tpu_custom_call", output_to_operand_aliasing={{}: (6, {})} | custom-call | flops 4194304 | bytes 2097152 | tf_op jit(solution)/shard_map/pallas_call | solution.py:606
  54.3 0.0 collective-permute-done.9.far_ref
  54.3 1.5 %shard_map.113.south_ref = f32[120,8,128]{2,1,0:T(8,128)S(1)} custom-call(s32[8]{0:T(128)S(1)} %copy-done.2, bf16[60,16,128]{2,1,0:T(8,128)(2,1)S(1)} %get-tuple-element.44.own_ref, bf16[60,16,128]{2,1,0:T(8,128)(2,1)S(1)} %collective-permute-done.8.near_ref, bf16[61,16,128]{2,1,0:T(8,128)(2,1)S(1)} %collective-permute-done.9.far_ref, ...), custom_call_target="tpu_custom_call" | custom-call | flops 4194304 | bytes 2097152 | tf_op jit(solution)/shard_map/pallas_call | solution.py:641
  55.8 0.0 collective-permute-done.7.far_ref
  55.8 2.2 %shard_map.116 = f32[480,8,128]{2,1,0:T(8,128)} custom-call(s32[8]{0:T(128)S(1)} %copy-done.2, bf16[60,16,128]{2,1,0:T(8,128)(2,1)S(1)} %get-tuple-element.37.own_ref, bf16[60,16,128]{2,1,0:T(8,128)(2,1)S(1)} %collective-permute-done.6.near_ref, bf16[61,16,128]{2,1,0:T(8,128)(2,1)S(1)} %collective-permute-done.7.far_ref, ...), custom_call_target="tpu_custom_call", output_to_operand_aliasing={{}: (7, {})} | custom-call | flops 4194304 | bytes 4194304 | tf_op jit(solution)/shard_map/pallas_call | solution.py:694
  (12 shorter events, 0.1 us)
Async XLA Ops:
  0.6 19.6 %copy-start = (f32[8,60,8,128]{3,2,1,0:T(8,128)S(1)}, f32[8,60,8,128]{3,2,1,0:T(8,128)}, u32[]{:S(2)}) copy-start(f32[8,60,8,128]{3,2,1,0:T(8,128)} %state_ref.1) | copy-start | bytes 5898244
  0.6 19.6 %copy-start.8 = (bf16[640,368]{0,1:T(8,128)(2,1)S(1)}, bf16[640,368]{0,1:T(8,128)(2,1)}, u32[]{:S(2)}) copy-start(bf16[640,368]{0,1:T(8,128)(2,1)} %param.15) | copy-start | bytes 1413124
  0.7 19.6 %copy-start.3 = (s32[1,1,1024]{2,1,0:T(1,128)S(1)}, s32[1,1,1024]{2,1,0:T(1,128)}, u32[]{:S(2)}) copy-start(s32[1,1,1024]{2,1,0:T(1,128)} %param.16) | copy-start | bytes 12292
  0.7 19.6 %copy-start.1 = (bf16[76,8,128]{2,1,0:T(8,128)(2,1)S(1)}, bf16[76,8,128]{2,1,0:T(8,128)(2,1)}, u32[]{:S(2)}) copy-start(bf16[76,8,128]{2,1,0:T(8,128)(2,1)} %surface_ref.1) | copy-start | bytes 466948
  2.3 18.9 %collective-permute-start = (bf16[45,16,128]{2,1,0:T(8,128)(2,1)S(1)}, bf16[45,16,128]{2,1,0:T(8,128)(2,1)S(1)}, u32[]{:S(2)}, u32[]{:S(2)}) collective-permute-start(bf16[45,16,128]{2,1,0:T(8,128)(2,1)S(1)} %get-tuple-element.27), channel_id=1, source_target_pairs={{8,0},{16,8},{24,16},{9,1},{17,9},{25,17},{10,2},{18,10},{26,18},{... | collective-permute-start | bytes 552968 | tf_op jit(solution)/shard_map/ppermute | solution.py:716
  3.6 17.6 %collective-permute-start.1 = (bf16[45,16,128]{2,1,0:T(8,128)(2,1)S(1)}, bf16[45,16,128]{2,1,0:T(8,128)(2,1)S(1)}, u32[]{:S(2)}, u32[]{:S(2)}) collective-permute-start(bf16[45,16,128]{2,1,0:T(8,128)(2,1)S(1)} %get-tuple-element.28), channel_id=1, source_target_pairs={{0,8},{8,16},{16,24},{24,0},{1,9},{9,17},{17,25},{25,1},{2,10},{10... | collective-permute-start | bytes 552968 | tf_op jit(solution)/shard_map/ppermute | solution.py:711
  7.2 5.0 %collective-permute-start.2 = (bf16[18,16,128]{2,1,0:T(8,128)(2,1)S(1)}, bf16[18,16,128]{2,1,0:T(8,128)(2,1)S(1)}, u32[]{:S(2)}, u32[]{:S(2)}) collective-permute-start(bf16[18,16,128]{2,1,0:T(8,128)(2,1)S(1)} %get-tuple-element.29.own_west_ref), channel_id=1, source_target_pairs={{0,7},{1,0},{2,1},{3,2},{4,3},{5,4},{6,5},{7,6},{8,15},{9,8},{10,9... | collective-permute-start | bytes 221192 | tf_op jit(solution)/shard_map/ppermute | solution.py:711
  10.2 5.6 %collective-permute-start.3 = (bf16[18,16,128]{2,1,0:T(8,128)(2,1)S(1)}, bf16[18,16,128]{2,1,0:T(8,128)(2,1)S(1)}, u32[]{:S(2)}, u32[]{:S(2)}) collective-permute-start(bf16[18,16,128]{2,1,0:T(8,128)(2,1)S(1)} %get-tuple-element.30.own_east_ref), channel_id=1, source_target_pairs={{0,1},{1,2},{2,3},{3,4},{4,5},{5,6},{6,7},{7,0},{8,9},{9,10},{10,1... | collective-permute-start | bytes 221192 | tf_op jit(solution)/shard_map/ppermute | solution.py:711
  15.8 6.4 %collective-permute-start.4 = (bf16[9,16,128]{2,1,0:T(8,128)(2,1)S(1)}, bf16[9,16,128]{2,1,0:T(8,128)(2,1)S(1)}, u32[]{:S(2)}, u32[]{:S(2)}) collective-permute-start(bf16[9,16,128]{2,1,0:T(8,128)(2,1)S(1)} %get-tuple-element.32), channel_id=1, source_target_pairs={{8,0},{16,8},{24,16},{9,1},{17,9},{25,17},{10,2},{18,10},{26,18},{... | collective-permute-start | bytes 110600 | tf_op jit(solution)/shard_map/ppermute | solution.py:716
  17.1 5.9 %collective-permute-start.5 = (bf16[9,16,128]{2,1,0:T(8,128)(2,1)S(1)}, bf16[9,16,128]{2,1,0:T(8,128)(2,1)S(1)}, u32[]{:S(2)}, u32[]{:S(2)}) collective-permute-start(bf16[9,16,128]{2,1,0:T(8,128)(2,1)S(1)} %get-tuple-element.33), channel_id=1, source_target_pairs={{0,8},{8,16},{16,24},{24,0},{1,9},{9,17},{17,25},{25,1},{2,10},{10... | collective-permute-start | bytes 110600 | tf_op jit(solution)/shard_map/ppermute | solution.py:711
  20.3 2.8 %copy-start.4 = (bf16[768,640]{1,0:T(8,128)(2,1)S(1)}, bf16[768,640]{1,0:T(8,128)(2,1)}, u32[]{:S(2)}) copy-start(bf16[768,640]{1,0:T(8,128)(2,1)} %two_ref.3) | copy-start | bytes 2949124
  20.3 2.8 %copy-start.5 = (bf16[556,768]{1,0:T(8,128)(2,1)S(1)}, bf16[556,768]{1,0:T(8,128)(2,1)}, u32[]{:S(2)}) copy-start(bf16[556,768]{1,0:T(8,128)(2,1)} %one_ref.3) | copy-start | bytes 2562052
  20.3 2.8 %copy-start.6 = (bf16[640,512]{1,0:T(8,128)(2,1)S(1)}, bf16[640,512]{1,0:T(8,128)(2,1)}, u32[]{:S(2)}) copy-start(bf16[640,512]{1,0:T(8,128)(2,1)} %three_ref.3) | copy-start | bytes 1966084
  20.3 2.8 %copy-start.7 = (bf16[512,640]{1,0:T(8,128)(2,1)S(1)}, bf16[512,640]{1,0:T(8,128)(2,1)}, u32[]{:S(2)}) copy-start(bf16[512,640]{1,0:T(8,128)(2,1)} %four_ref.3) | copy-start | bytes 1966084
  27.0 7.5 %collective-permute-start.8 = (bf16[60,16,128]{2,1,0:T(8,128)(2,1)S(1)}, bf16[60,16,128]{2,1,0:T(8,128)(2,1)S(1)}, u32[]{:S(2)}, u32[]{:S(2)}) collective-permute-start(bf16[60,16,128]{2,1,0:T(8,128)(2,1)S(1)} %get-tuple-element.44.own_ref), channel_id=1, source_target_pairs={{0,1},{1,2},{2,3},{3,4},{4,5},{5,6},{6,7},{7,0},{8,9},{9,10},{10,1... | collective-permute-start | bytes 737288 | tf_op jit(solution)/shard_map/ppermute | solution.py:711
  27.1 7.4 %copy-start.2 = (s32[8]{0:T(128)S(1)}, s32[8]{0:T(128)}, u32[]{:S(2)}) copy-start(s32[8]{0:T(128)} %offset_ref.11) | copy-start | bytes 100
  30.0 7.5 %collective-permute-start.6 = (bf16[60,16,128]{2,1,0:T(8,128)(2,1)S(1)}, bf16[60,16,128]{2,1,0:T(8,128)(2,1)S(1)}, u32[]{:S(2)}, u32[]{:S(2)}) collective-permute-start(bf16[60,16,128]{2,1,0:T(8,128)(2,1)S(1)} %get-tuple-element.37.own_ref), channel_id=1, source_target_pairs={{0,1},{1,2},{2,3},{3,4},{4,5},{5,6},{6,7},{7,0},{8,9},{9,10},{10,1... | collective-permute-start | bytes 737288 | tf_op jit(solution)/shard_map/ppermute | solution.py:711
  30.1 8.7 %collective-permute-start.10 = (bf16[30,16,128]{2,1,0:T(8,128)(2,1)S(1)}, bf16[30,16,128]{2,1,0:T(8,128)(2,1)S(1)}, u32[]{:S(2)}, u32[]{:S(2)}) collective-permute-start(bf16[30,16,128]{2,1,0:T(8,128)(2,1)S(1)} %get-tuple-element.47.own_ref), channel_id=1, source_target_pairs={{0,1},{1,2},{2,3},{3,4},{4,5},{5,6},{6,7},{7,0},{8,9},{9,10},{10,1... | collective-permute-start | bytes 368648 | tf_op jit(solution)/shard_map/ppermute | solution.py:711
  35.3 19.1 %collective-permute-start.9 = (bf16[61,16,128]{2,1,0:T(8,128)(2,1)S(1)}, bf16[61,16,128]{2,1,0:T(8,128)(2,1)S(1)}, u32[]{:S(2)}, u32[]{:S(2)}) collective-permute-start(bf16[61,16,128]{2,1,0:T(8,128)(2,1)S(1)} %shard_map.112), channel_id=1, source_target_pairs={{0,2},{1,3},{2,4},{3,5},{4,6},{5,7},{6,0},{7,1},{8,10},{9,11},{10,... | collective-permute-start | bytes 749576 | tf_op jit(solution)/shard_map/ppermute | solution.py:711
  38.3 17.5 %collective-permute-start.7 = (bf16[61,16,128]{2,1,0:T(8,128)(2,1)S(1)}, bf16[61,16,128]{2,1,0:T(8,128)(2,1)S(1)}, u32[]{:S(2)}, u32[]{:S(2)}) collective-permute-start(bf16[61,16,128]{2,1,0:T(8,128)(2,1)S(1)} %shard_map.110), channel_id=1, source_target_pairs={{0,2},{1,3},{2,4},{3,5},{4,6},{5,7},{6,0},{7,1},{8,10},{9,11},{10,... | collective-permute-start | bytes 749576 | tf_op jit(solution)/shard_map/ppermute | solution.py:711
  39.5 12.8 %collective-permute-start.11 = (bf16[31,16,128]{2,1,0:T(8,128)(2,1)S(1)}, bf16[31,16,128]{2,1,0:T(8,128)(2,1)S(1)}, u32[]{:S(2)}, u32[]{:S(2)}) collective-permute-start(bf16[31,16,128]{2,1,0:T(8,128)(2,1)S(1)} %shard_map.114), channel_id=1, source_target_pairs={{0,2},{1,3},{2,4},{3,5},{4,6},{5,7},{6,0},{7,1},{8,10},{9,11},{10,... | collective-permute-start | bytes 380936 | tf_op jit(solution)/shard_map/ppermute | solution.py:711

commit v5 on v4

--- a/solution.py
+++ b/solution.py
@@ -711,13 +711,6 @@
     return lax.ppermute(value, axis, [(i, (i + steps) % count) for i in range(count)])
 
 
-def passed_along(block, axis, distance):
-    devices = range(lax.axis_size(axis))
-    return lax.ppermute(
-        block, axis, [(i, i + distance) for i in devices if i + distance in devices]
-    )
-
-
 def on_device(
     state,
     surface,
@@ -750,11 +743,11 @@
     from_east = shifted(to_west, "lon", -1)
     from_west = shifted(to_east, "lon", 1)
     from_south = shifted(to_north, "lat", 1)
-    from_north = passed_along(to_south, "lat", -1)
+    from_north = shifted(to_south, "lat", -1)
     ozone_near = shifted(ozone, "lon", 1)
     strips, strips_south, strips_north = strips_of(to_west, to_east, from_east, from_west)
     strips_from_south = shifted(strips_north, "lat", 1)
-    strips_from_north = passed_along(strips_south, "lat", -1)
+    strips_from_north = shifted(strips_south, "lat", -1)
 
     five = layer_five.T
     five_tracers = five[2 * levels : 6 * levels]

time: 58.7 us -> 57.3 us (0.976)
  starting transfers between devices: 12.7 us -> 9.79 us
  waiting for transfers between devices: 23.7 us -> 25.8 us
    ppermute x2 -> x0, starting transfers between devices: 2.58 us -> none  [passed_along(): lax.ppermute(block, axis, [(i, i + distance) for i in devices if i + dist...]
    ppermute x10 -> x12, waiting for transfers between devices: 23.7 us -> 25.8 us  [shifted(): lax.ppermute(value, axis, [(i, (i + steps) % count) for i in range(count)])]
    ppermute x10 -> x12, starting transfers between devices: 10.1 us -> 9.79 us  [shifted(): lax.ppermute(value, axis, [(i, (i + steps) % count) for i in range(count)])]
where the time goes in v5:
time: 57.3 us; the launch traced here: 57.2 us
  waiting for transfers between devices  25.8 us (45%)
  Pallas kernels  19.3 us (34%)
  starting transfers between devices  9.79 us (17%)
  local copies, waits for them, and re-layouts  1.42 us (2%)
  between operations  0.92 us (2%)
    ppermute x12, waiting for transfers between devices, shifted(): lax.ppermute(value, axis, [(i, (i + steps) % count) for i in range(count)])  25.8 us
    ppermute x12, starting transfers between devices, shifted(): lax.ppermute(value, axis, [(i, (i + steps) % count) for i in range(count)])  9.79 us
    pallas_call x1, Pallas kernels, network(): pl.pallas_call(network_kernel, out_shape=(jax.ShapeDtypeStruct((3 * level...  3.94 us
    pallas_call x1, Pallas kernels, second(): pl.pallas_call(functools.partial(second_kernel, first), out_shape=(jax.Sh...  2.93 us
    pallas_call x1, Pallas kernels, winds_out(): pl.pallas_call(winds_kernel, out_shape=(jax.ShapeDtypeStruct((fields * le...  2.22 us
    pallas_call x3, Pallas kernels, relay(): pl.pallas_call(functools.partial(relay_kernel, base, span), out_shape=jax...  2.21 us
    pallas_call x1, Pallas kernels, advect_north(): pl.pallas_call(functools.partial(advect_north_kernel, first), out_shape=j...  2.2 us
    pallas_call x1, Pallas kernels, advect_ozone(): pl.pallas_call(functools.partial(advect_ozone_kernel, first), out_shape=j...  2.07 us
  transfers between devices with their start and end apart: 12, of which 7 were waited for; matrix products, arithmetic and copies ran while one was open for 0% of the time, Pallas kernels for 22%

profile of v5, /device:TPU:0, one launch (start us, length us, event | category | flops | bytes accessed | tf_op | source)
XLA Modules:
  0.0 57.2 jit_solution(14404332601965666196)
XLA Ops:
  0.6 0.0 copy-start
  0.6 0.0 copy-start.8
  0.7 0.0 copy-start.3
  0.7 1.3 %slice.12.winds_ref.state_ref = f32[3,60,8,128]{3,2,1,0:T(8,128)S(1)} slice(f32[8,60,8,128]{3,2,1,0:T(8,128)} %state_ref.1), slice={[0:3], [0:60], [0:8], [0:128]} | slice | bytes 1474560 | tf_op jit(solution)/shard_map/slice | solution.py:740
  2.0 0.3 shard_map.104
  2.3 4.0 %collective-permute-start = (bf16[45,16,128]{2,1,0:T(8,128)(2,1)S(1)}, bf16[45,16,128]{2,1,0:T(8,128)(2,1)S(1)}, u32[]{:S(2)}, u32[]{:S(2)}) collective-permute-start(bf16[45,16,128]{2,1,0:T(8,128)(2,1)S(1)} %get-tuple-element.27), channel_id=1, source_target_pairs={{0,24},{8,0},{16,8},{24,16},{1,25},{9,1},{17,9},{25,17},{2,26},{10... | collective-permute-start | bytes 552968 | tf_op jit(solution)/shard_map/ppermute | solution.py:711
  6.2 0.0 collective-permute-start.1
  6.2 2.8 %collective-permute-start.2 = (bf16[18,16,128]{2,1,0:T(8,128)(2,1)S(1)}, bf16[18,16,128]{2,1,0:T(8,128)(2,1)S(1)}, u32[]{:S(2)}, u32[]{:S(2)}) collective-permute-start(bf16[18,16,128]{2,1,0:T(8,128)(2,1)S(1)} %get-tuple-element.29.own_west_ref), channel_id=1, source_target_pairs={{0,7},{1,0},{2,1},{3,2},{4,3},{5,4},{6,5},{7,6},{8,15},{9,8},{10,9... | collective-permute-start | bytes 221192 | tf_op jit(solution)/shard_map/ppermute | solution.py:711
  9.0 0.0 collective-permute-start.3
  9.0 2.0 %collective-permute-done.2.from_east_ref = bf16[18,16,128]{2,1,0:T(8,128)(2,1)S(1)} collective-permute-done((bf16[18,16,128]{2,1,0:T(8,128)(2,1)S(1)}, bf16[18,16,128]{2,1,0:T(8,128)(2,1)S(1)}, u32[]{:S(2)}, u32[]{:S(2)}) %collective-permute-start.2) | collective-permute-done | bytes 73760 | tf_op jit(solution)/shard_map/ppermute | solution.py:711
  11.0 3.6 %collective-permute-done.3.from_west_ref = bf16[18,16,128]{2,1,0:T(8,128)(2,1)S(1)} collective-permute-done((bf16[18,16,128]{2,1,0:T(8,128)(2,1)S(1)}, bf16[18,16,128]{2,1,0:T(8,128)(2,1)S(1)}, u32[]{:S(2)}, u32[]{:S(2)}) %collective-permute-start.3) | collective-permute-done | bytes 73760 | tf_op jit(solution)/shard_map/ppermute | solution.py:711
  14.6 0.1 shard_map.106
  14.6 2.7 %collective-permute-start.4 = (bf16[9,16,128]{2,1,0:T(8,128)(2,1)S(1)}, bf16[9,16,128]{2,1,0:T(8,128)(2,1)S(1)}, u32[]{:S(2)}, u32[]{:S(2)}) collective-permute-start(bf16[9,16,128]{2,1,0:T(8,128)(2,1)S(1)} %get-tuple-element.32), channel_id=1, source_target_pairs={{0,24},{8,0},{16,8},{24,16},{1,25},{9,1},{17,9},{25,17},{2,26},{10... | collective-permute-start | bytes 110600 | tf_op jit(solution)/shard_map/ppermute | solution.py:711
  17.3 0.0 collective-permute-start.5
  17.4 0.0 copy-start.4
  17.4 0.0 copy-start.5
  17.4 0.0 copy-start.6
  17.4 0.0 copy-start.7
  17.4 0.8 %shard_map.107 = (bf16[556,1024]{1,0:T(8,128)(2,1)S(1)}, f32[8,128]{1,0:T(8,128)S(1)}, bf16[30,16,128]{2,1,0:T(8,128)(2,1)S(1)}) custom-call(f32[8,60,8,128]{3,2,1,0:T(8,128)S(1)} %copy-done, bf16[76,8,128]{2,1,0:T(8,128)(2,1)S(1)} %copy-done.1, s32[1,1024]{1,0:T(1,128)S(1)} %bitcast.6), custom_call_target="tpu_custom_call" | custom-call | flops 16777216 | bytes 4194304 | tf_op jit(solution)/shard_map/pallas_call | solution.py:223
  18.2 0.0 collective-permute-done.from_north_ref
  18.2 0.0 collective-permute-done.1.from_south_ref
  18.3 1.1 %shard_map.105.inner_ref = f32[3,60,8,128]{3,2,1,0:T(8,128)S(1)} custom-call(f32[3,60,8,128]{3,2,1,0:T(8,128)S(1)} %slice.12.winds_ref.state_ref, bf16[45,16,128]{2,1,0:T(8,128)(2,1)S(1)} %collective-permute-done.from_north_ref, bf16[45,16,128]{2,1,0:T(8,128)(2,1)S(1)} %collective-permute-done.1.from_south_ref), custom_call_target="tpu_custom_call" | custom-call | flops 16777216 | bytes 4194304 | tf_op jit(solution)/shard_map/pallas_call | solution.py:187
  19.4 0.0 collective-permute-done.4.north_ref
  19.4 2.8 %collective-permute-done.5.south_ref = bf16[9,16,128]{2,1,0:T(8,128)(2,1)S(1)} collective-permute-done((bf16[9,16,128]{2,1,0:T(8,128)(2,1)S(1)}, bf16[9,16,128]{2,1,0:T(8,128)(2,1)S(1)}, u32[]{:S(2)}, u32[]{:S(2)}) %collective-permute-start.5) | collective-permute-done | bytes 36896 | tf_op jit(solution)/shard_map/ppermute | solution.py:711
  22.2 0.0 copy-done.5
  22.2 3.9 %shard_map.108 = (f32[1440,128]{1,0:T(8,128)S(1)}, f32[60,8,128]{2,1,0:T(8,128)S(1)}, bf16[556,1024]{1,0:T(8,128)(2,1)S(1)}, bf16[512,640]{1,0:T(8,128)(2,1)S(1)}, bf16[60,16,128]{2,1,0:T(8,128)(2,1)S(1)}) custom-call(f32[3,60,8,128]{3,2,1,0:T(8,128)S(1)} %shard_map.105.inner_ref, f32[36,8,128]{2,1,0:T(8,128)S(1)} %get-tuple-element.31.here_ref, ...), custom_call_target="tpu_custom_call" | custom-call | flops 3221225472 | bytes 8388608 | tf_op jit(solution)/shard_map/pallas_call | solution.py:364
  26.2 0.1 collective-permute-start.8
  26.2 0.0 copy-start.2
  26.2 2.9 %shard_map.109 = (bf16[512,640]{1,0:T(8,128)(2,1)S(1)}, bf16[60,16,128]{2,1,0:T(8,128)(2,1)S(1)}) custom-call(bf16[556,1024]{1,0:T(8,128)(2,1)S(1)} %get-tuple-element.36.features_ref, bf16[556,768]{1,0:T(8,128)(2,1)S(1)} %copy-done.5, bf16[768,640]{1,0:T(8,128)(2,1)S(1)} %copy-done.4, bf16[640,512]{1,0:T(8,128)(2,1)S(1)} %copy-done.6, ...), custom_call_target="tpu_custom_call" | custom-call | flops 2147483648 | bytes 6291456 | tf_op jit(solution)/shard_map/pallas_call | solution.py:397
  29.2 0.1 collective-permute-start.6
  29.2 0.1 collective-permute-start.10
  29.3 4.3 %collective-permute-done.8.near_ref = bf16[60,16,128]{2,1,0:T(8,128)(2,1)S(1)} collective-permute-done((bf16[60,16,128]{2,1,0:T(8,128)(2,1)S(1)}, bf16[60,16,128]{2,1,0:T(8,128)(2,1)S(1)}, u32[]{:S(2)}, u32[]{:S(2)}) %collective-permute-start.8) | collective-permute-done | bytes 245792 | tf_op jit(solution)/shard_map/ppermute | solution.py:711
  33.6 0.0 copy-done.2
  33.6 0.8 %shard_map.112 = bf16[61,16,128]{2,1,0:T(8,128)(2,1)S(1)} custom-call(s32[8]{0:T(128)S(1)} %copy-done.2, bf16[60,16,128]{2,1,0:T(8,128)(2,1)S(1)} %get-tuple-element.44.own_ref, bf16[60,16,128]{2,1,0:T(8,128)(2,1)S(1)} %collective-permute-done.8.near_ref), custom_call_target="tpu_custom_call" | custom-call | flops 1048576 | bytes 1048576 | tf_op jit(solution)/shard_map/pallas_call | solution.py:532
  34.4 0.1 collective-permute-start.9
  34.5 2.2 %collective-permute-done.6.near_ref = bf16[60,16,128]{2,1,0:T(8,128)(2,1)S(1)} collective-permute-done((bf16[60,16,128]{2,1,0:T(8,128)(2,1)S(1)}, bf16[60,16,128]{2,1,0:T(8,128)(2,1)S(1)}, u32[]{:S(2)}, u32[]{:S(2)}) %collective-permute-start.6) | collective-permute-done | bytes 245792 | tf_op jit(solution)/shard_map/ppermute | solution.py:711
  36.6 0.8 %shard_map.110 = bf16[61,16,128]{2,1,0:T(8,128)(2,1)S(1)} custom-call(s32[8]{0:T(128)S(1)} %copy-done.2, bf16[60,16,128]{2,1,0:T(8,128)(2,1)S(1)} %get-tuple-element.37.own_ref, bf16[60,16,128]{2,1,0:T(8,128)(2,1)S(1)} %collective-permute-done.6.near_ref), custom_call_target="tpu_custom_call" | custom-call | flops 1048576 | bytes 1048576 | tf_op jit(solution)/shard_map/pallas_call | solution.py:532
  37.4 0.1 collective-permute-start.7
  37.5 0.4 collective-permute-done.10.near_ref
  38.0 0.7 %shard_map.114 = bf16[31,16,128]{2,1,0:T(8,128)(2,1)S(1)} custom-call(s32[8]{0:T(128)S(1)} %copy-done.2, bf16[30,16,128]{2,1,0:T(8,128)(2,1)S(1)} %get-tuple-element.47.own_ref, bf16[30,16,128]{2,1,0:T(8,128)(2,1)S(1)} %collective-permute-done.10.near_ref), custom_call_target="tpu_custom_call" | custom-call | flops 1048576 | bytes 1048576 | tf_op jit(solution)/shard_map/pallas_call | solution.py:532
  38.6 0.1 collective-permute-start.11
  38.7 2.2 %shard_map.111 = (f32[480,8,128]{2,1,0:T(8,128)}, bf16[8,8,128]{2,1,0:T(8,128)(2,1)}, f32[60,8,128]{2,1,0:T(8,128)S(1)}, f32[60,8,128]{2,1,0:T(8,128)S(1)}, f32[...) custom-call(bf16[512,640]{1,0:T(8,128)(2,1)S(1)} %get-tuple-element.38, ...), custom_call_target="tpu_custom_call" | custom-call | flops 268435456 | bytes 4194304 | tf_op jit(solution)/shard_map/pallas_call | solution.py:470
  40.9 10.4 %collective-permute-done.11.far_ref = bf16[31,16,128]{2,1,0:T(8,128)(2,1)S(1)} collective-permute-done((bf16[31,16,128]{2,1,0:T(8,128)(2,1)S(1)}, bf16[31,16,128]{2,1,0:T(8,128)(2,1)S(1)}, u32[]{:S(2)}, u32[]{:S(2)}) %collective-permute-start.11) | collective-permute-done | bytes 127008 | tf_op jit(solution)/shard_map/ppermute | solution.py:711
  51.4 2.1 %shard_map.115.whole_ref = f32[480,8,128]{2,1,0:T(8,128)} custom-call(s32[8]{0:T(128)S(1)} %copy-done.2, bf16[30,16,128]{2,1,0:T(8,128)(2,1)S(1)} %get-tuple-element.47.own_ref, bf16[30,16,128]{2,1,0:T(8,128)(2,1)S(1)} %collective-permute-done.10.near_ref, bf16[31,16,128]{2,1,0:T(8,128)(2,1)S(1)} %collective-permute-done.11.far_ref, ...), custom_call_target="tpu_custom_call", output_to_operand_aliasing={{}: (6, {})} | custom-call | flops 4194304 | bytes 2097152 | tf_op jit(solution)/shard_map/pallas_call | solution.py:606
  53.5 0.0 collective-permute-done.9.far_ref
  53.5 1.5 %shard_map.113.south_ref = f32[120,8,128]{2,1,0:T(8,128)S(1)} custom-call(s32[8]{0:T(128)S(1)} %copy-done.2, bf16[60,16,128]{2,1,0:T(8,128)(2,1)S(1)} %get-tuple-element.44.own_ref, bf16[60,16,128]{2,1,0:T(8,128)(2,1)S(1)} %collective-permute-done.8.near_ref, bf16[61,16,128]{2,1,0:T(8,128)(2,1)S(1)} %collective-permute-done.9.far_ref, ...), custom_call_target="tpu_custom_call" | custom-call | flops 4194304 | bytes 2097152 | tf_op jit(solution)/shard_map/pallas_call | solution.py:641
  54.9 0.0 collective-permute-done.7.far_ref
  55.0 2.2 %shard_map.116 = f32[480,8,128]{2,1,0:T(8,128)} custom-call(s32[8]{0:T(128)S(1)} %copy-done.2, bf16[60,16,128]{2,1,0:T(8,128)(2,1)S(1)} %get-tuple-element.37.own_ref, bf16[60,16,128]{2,1,0:T(8,128)(2,1)S(1)} %collective-permute-done.6.near_ref, bf16[61,16,128]{2,1,0:T(8,128)(2,1)S(1)} %collective-permute-done.7.far_ref, ...), custom_call_target="tpu_custom_call", output_to_operand_aliasing={{}: (7, {})} | custom-call | flops 4194304 | bytes 4194304 | tf_op jit(solution)/shard_map/pallas_call | solution.py:694
  (12 shorter events, 0.1 us)
Async XLA Ops:
  0.6 16.7 %copy-start = (f32[8,60,8,128]{3,2,1,0:T(8,128)S(1)}, f32[8,60,8,128]{3,2,1,0:T(8,128)}, u32[]{:S(2)}) copy-start(f32[8,60,8,128]{3,2,1,0:T(8,128)} %state_ref.1) | copy-start | bytes 5898244
  0.6 16.7 %copy-start.8 = (bf16[640,368]{0,1:T(8,128)(2,1)S(1)}, bf16[640,368]{0,1:T(8,128)(2,1)}, u32[]{:S(2)}) copy-start(bf16[640,368]{0,1:T(8,128)(2,1)} %param.15) | copy-start | bytes 1413124
  0.7 16.7 %copy-start.3 = (s32[1,1,1024]{2,1,0:T(1,128)S(1)}, s32[1,1,1024]{2,1,0:T(1,128)}, u32[]{:S(2)}) copy-start(s32[1,1,1024]{2,1,0:T(1,128)} %param.16) | copy-start | bytes 12292
  0.7 16.7 %copy-start.1 = (bf16[76,8,128]{2,1,0:T(8,128)(2,1)S(1)}, bf16[76,8,128]{2,1,0:T(8,128)(2,1)}, u32[]{:S(2)}) copy-start(bf16[76,8,128]{2,1,0:T(8,128)(2,1)} %surface_ref.1) | copy-start | bytes 466948
  2.3 16.0 %collective-permute-start = (bf16[45,16,128]{2,1,0:T(8,128)(2,1)S(1)}, bf16[45,16,128]{2,1,0:T(8,128)(2,1)S(1)}, u32[]{:S(2)}, u32[]{:S(2)}) collective-permute-start(bf16[45,16,128]{2,1,0:T(8,128)(2,1)S(1)} %get-tuple-element.27), channel_id=1, source_target_pairs={{0,24},{8,0},{16,8},{24,16},{1,25},{9,1},{17,9},{25,17},{2,26},{10... | collective-permute-start | bytes 552968 | tf_op jit(solution)/shard_map/ppermute | solution.py:711
  6.2 12.0 %collective-permute-start.1 = (bf16[45,16,128]{2,1,0:T(8,128)(2,1)S(1)}, bf16[45,16,128]{2,1,0:T(8,128)(2,1)S(1)}, u32[]{:S(2)}, u32[]{:S(2)}) collective-permute-start(bf16[45,16,128]{2,1,0:T(8,128)(2,1)S(1)} %get-tuple-element.28), channel_id=1, source_target_pairs={{0,8},{8,16},{16,24},{24,0},{1,9},{9,17},{17,25},{25,1},{2,10},{10... | collective-permute-start | bytes 552968 | tf_op jit(solution)/shard_map/ppermute | solution.py:711
  6.2 4.7 %collective-permute-start.2 = (bf16[18,16,128]{2,1,0:T(8,128)(2,1)S(1)}, bf16[18,16,128]{2,1,0:T(8,128)(2,1)S(1)}, u32[]{:S(2)}, u32[]{:S(2)}) collective-permute-start(bf16[18,16,128]{2,1,0:T(8,128)(2,1)S(1)} %get-tuple-element.29.own_west_ref), channel_id=1, source_target_pairs={{0,7},{1,0},{2,1},{3,2},{4,3},{5,4},{6,5},{7,6},{8,15},{9,8},{10,9... | collective-permute-start | bytes 221192 | tf_op jit(solution)/shard_map/ppermute | solution.py:711
  9.0 5.6 %collective-permute-start.3 = (bf16[18,16,128]{2,1,0:T(8,128)(2,1)S(1)}, bf16[18,16,128]{2,1,0:T(8,128)(2,1)S(1)}, u32[]{:S(2)}, u32[]{:S(2)}) collective-permute-start(bf16[18,16,128]{2,1,0:T(8,128)(2,1)S(1)} %get-tuple-element.30.own_east_ref), channel_id=1, source_target_pairs={{0,1},{1,2},{2,3},{3,4},{4,5},{5,6},{6,7},{7,0},{8,9},{9,10},{10,1... | collective-permute-start | bytes 221192 | tf_op jit(solution)/shard_map/ppermute | solution.py:711
  14.6 4.8 %collective-permute-start.4 = (bf16[9,16,128]{2,1,0:T(8,128)(2,1)S(1)}, bf16[9,16,128]{2,1,0:T(8,128)(2,1)S(1)}, u32[]{:S(2)}, u32[]{:S(2)}) collective-permute-start(bf16[9,16,128]{2,1,0:T(8,128)(2,1)S(1)} %get-tuple-element.32), channel_id=1, source_target_pairs={{0,24},{8,0},{16,8},{24,16},{1,25},{9,1},{17,9},{25,17},{2,26},{10... | collective-permute-start | bytes 110600 | tf_op jit(solution)/shard_map/ppermute | solution.py:711
  17.3 4.9 %collective-permute-start.5 = (bf16[9,16,128]{2,1,0:T(8,128)(2,1)S(1)}, bf16[9,16,128]{2,1,0:T(8,128)(2,1)S(1)}, u32[]{:S(2)}, u32[]{:S(2)}) collective-permute-start(bf16[9,16,128]{2,1,0:T(8,128)(2,1)S(1)} %get-tuple-element.33), channel_id=1, source_target_pairs={{0,8},{8,16},{16,24},{24,0},{1,9},{9,17},{17,25},{25,1},{2,10},{10... | collective-permute-start | bytes 110600 | tf_op jit(solution)/shard_map/ppermute | solution.py:711
  17.4 4.8 %copy-start.4 = (bf16[768,640]{1,0:T(8,128)(2,1)S(1)}, bf16[768,640]{1,0:T(8,128)(2,1)}, u32[]{:S(2)}) copy-start(bf16[768,640]{1,0:T(8,128)(2,1)} %two_ref.3) | copy-start | bytes 2949124
  17.4 4.8 %copy-start.5 = (bf16[556,768]{1,0:T(8,128)(2,1)S(1)}, bf16[556,768]{1,0:T(8,128)(2,1)}, u32[]{:S(2)}) copy-start(bf16[556,768]{1,0:T(8,128)(2,1)} %one_ref.3) | copy-start | bytes 2562052
  17.4 4.8 %copy-start.6 = (bf16[640,512]{1,0:T(8,128)(2,1)S(1)}, bf16[640,512]{1,0:T(8,128)(2,1)}, u32[]{:S(2)}) copy-start(bf16[640,512]{1,0:T(8,128)(2,1)} %three_ref.3) | copy-start | bytes 1966084
  17.4 4.8 %copy-start.7 = (bf16[512,640]{1,0:T(8,128)(2,1)S(1)}, bf16[512,640]{1,0:T(8,128)(2,1)}, u32[]{:S(2)}) copy-start(bf16[512,640]{1,0:T(8,128)(2,1)} %four_ref.3) | copy-start | bytes 1966084
  26.2 7.5 %collective-permute-start.8 = (bf16[60,16,128]{2,1,0:T(8,128)(2,1)S(1)}, bf16[60,16,128]{2,1,0:T(8,128)(2,1)S(1)}, u32[]{:S(2)}, u32[]{:S(2)}) collective-permute-start(bf16[60,16,128]{2,1,0:T(8,128)(2,1)S(1)} %get-tuple-element.44.own_ref), channel_id=1, source_target_pairs={{0,1},{1,2},{2,3},{3,4},{4,5},{5,6},{6,7},{7,0},{8,9},{9,10},{10,1... | collective-permute-start | bytes 737288 | tf_op jit(solution)/shard_map/ppermute | solution.py:711
  26.2 7.4 %copy-start.2 = (s32[8]{0:T(128)S(1)}, s32[8]{0:T(128)}, u32[]{:S(2)}) copy-start(s32[8]{0:T(128)} %offset_ref.11) | copy-start | bytes 100
  29.2 7.5 %collective-permute-start.6 = (bf16[60,16,128]{2,1,0:T(8,128)(2,1)S(1)}, bf16[60,16,128]{2,1,0:T(8,128)(2,1)S(1)}, u32[]{:S(2)}, u32[]{:S(2)}) collective-permute-start(bf16[60,16,128]{2,1,0:T(8,128)(2,1)S(1)} %get-tuple-element.37.own_ref), channel_id=1, source_target_pairs={{0,1},{1,2},{2,3},{3,4},{4,5},{5,6},{6,7},{7,0},{8,9},{9,10},{10,1... | collective-permute-start | bytes 737288 | tf_op jit(solution)/shard_map/ppermute | solution.py:711
  29.2 8.7 %collective-permute-start.10 = (bf16[30,16,128]{2,1,0:T(8,128)(2,1)S(1)}, bf16[30,16,128]{2,1,0:T(8,128)(2,1)S(1)}, u32[]{:S(2)}, u32[]{:S(2)}) collective-permute-start(bf16[30,16,128]{2,1,0:T(8,128)(2,1)S(1)} %get-tuple-element.47.own_ref), channel_id=1, source_target_pairs={{0,1},{1,2},{2,3},{3,4},{4,5},{5,6},{6,7},{7,0},{8,9},{9,10},{10,1... | collective-permute-start | bytes 368648 | tf_op jit(solution)/shard_map/ppermute | solution.py:711
  34.4 19.1 %collective-permute-start.9 = (bf16[61,16,128]{2,1,0:T(8,128)(2,1)S(1)}, bf16[61,16,128]{2,1,0:T(8,128)(2,1)S(1)}, u32[]{:S(2)}, u32[]{:S(2)}) collective-permute-start(bf16[61,16,128]{2,1,0:T(8,128)(2,1)S(1)} %shard_map.112), channel_id=1, source_target_pairs={{0,2},{1,3},{2,4},{3,5},{4,6},{5,7},{6,0},{7,1},{8,10},{9,11},{10,... | collective-permute-start | bytes 749576 | tf_op jit(solution)/shard_map/ppermute | solution.py:711
  37.4 17.5 %collective-permute-start.7 = (bf16[61,16,128]{2,1,0:T(8,128)(2,1)S(1)}, bf16[61,16,128]{2,1,0:T(8,128)(2,1)S(1)}, u32[]{:S(2)}, u32[]{:S(2)}) collective-permute-start(bf16[61,16,128]{2,1,0:T(8,128)(2,1)S(1)} %shard_map.110), channel_id=1, source_target_pairs={{0,2},{1,3},{2,4},{3,5},{4,6},{5,7},{6,0},{7,1},{8,10},{9,11},{10,... | collective-permute-start | bytes 749576 | tf_op jit(solution)/shard_map/ppermute | solution.py:711
  38.6 12.8 %collective-permute-start.11 = (bf16[31,16,128]{2,1,0:T(8,128)(2,1)S(1)}, bf16[31,16,128]{2,1,0:T(8,128)(2,1)S(1)}, u32[]{:S(2)}, u32[]{:S(2)}) collective-permute-start(bf16[31,16,128]{2,1,0:T(8,128)(2,1)S(1)} %shard_map.114), channel_id=1, source_target_pairs={{0,2},{1,3},{2,4},{3,5},{4,6},{5,7},{6,0},{7,1},{8,10},{9,11},{10,... | collective-permute-start | bytes 380936 | tf_op jit(solution)/shard_map/ppermute | solution.py:711

commit v6 on v5

--- a/solution.py
+++ b/solution.py
@@ -42,17 +42,15 @@
     return (size - shift) % size
 
 
-def paired(tiles, rows, low):
-    tiles = tiles.reshape((tiles.shape[0] // 2, 2) + tiles.shape[1:])
-    even = tiles[:, 0]
-    odd = pltpu.roll(tiles[:, 1], rows // 2, 1)
-    return jnp.where(low, even, odd), jnp.where(low, odd, even)
-
-
-def halo_rows(north_pair, south_pair, low):
-    even = jnp.where(low, north_pair, south_pair)
-    odd = pltpu.roll(jnp.where(low, south_pair, north_pair), north_pair.shape[-2] // 2, 1)
-    return jnp.stack([even, odd], axis=1).reshape((-1,) + even.shape[1:])
+def halo_messages(zonal, merid, press):
+    rows, cols = zonal.shape[1:]
+    place = iota((rows, cols), 0)
+    above = pltpu.roll(merid, 1, 1)
+    spread = zonal - pltpu.roll(zonal, 1, 2) + merid - jnp.where(place == 0, 0.0, above)
+    turned = pltpu.roll(spread, rows // 2, 1)
+    south = jnp.where(place < rows // 2, press, turned)
+    north = jnp.where(place == 0, above, jnp.where(place < rows // 2, turned, press))
+    return south, north
 
 
 def side_packs(tiles, lane):
@@ -79,22 +77,17 @@
 
 def messages_kernel(winds_ref, south_ref, north_ref, west_ref, east_ref):
     fields, levels, rows, cols = winds_ref.shape
-    low = iota((rows, cols), 0) < rows // 2
     lane = iota((rows, cols), 1)
-    held = winds_ref.reshape(fields * levels, rows, cols)
-
-    def body(step, carry):
-        tiles = held[pl.ds(step * 20, 20)]
-        south, north = paired(tiles, rows, low)
-        south_ref[pl.ds(step * 5, 5)] = tall(south)
-        north_ref[pl.ds(step * 5, 5)] = tall(north)
-        west, east = side_packs(tiles, lane)
-        west_ref[pl.ds(step * 2, 2)] = tall(west)
-        east_ref[pl.ds(step * 2, 2)] = tall(east)
-        return carry
-
-    steps = fields * levels // 20
-    lax.fori_loop(0, steps, body, 0, unroll=steps)
+    free = open_rows(rows, cols)[:rows]
+    packs = levels // (cols // STRIP)
+    for field in range(fields):
+        west, east = side_packs(winds_ref[field], lane)
+        at = pl.ds(field * packs // 2, packs // 2)
+        west_ref[at] = tall(west)
+        east_ref[at] = tall(east)
+    south, north = halo_messages(winds_ref[0], winds_ref[1] * free, winds_ref[2])
+    south_ref[...] = tall(south)
+    north_ref[...] = tall(north)
 
 
 def messages(winds):
@@ -106,7 +99,7 @@
     packs = fields * levels // (cols // STRIP)
     return pl.pallas_call(
         messages_kernel,
-        out_shape=(shape(fields * levels // 2),) * 2 + (shape(packs),) * 2,
+        out_shape=(shape(levels),) * 2 + (shape(packs),) * 2,
         in_specs=[vmem()],
         out_specs=(vmem(),) * 4,
         compiler_params=params(4),
@@ -123,20 +116,21 @@
     count = 2 * own_west_ref.shape[0]
     rows, cols = own_west_ref.shape[1] // 2, own_west_ref.shape[2]
     place = iota((rows, cols), 1) % STRIP
-    low = iota((rows, cols), 0) < rows // 2
     value = short(own_east_ref, 0, count)
     value = jnp.where(place < 4 * SUBSTEPS, short(from_west_ref, 0, count), value)
     value = jnp.where(place < 3 * SUBSTEPS, short(from_east_ref, 0, count), value)
     value = jnp.where(place < 2 * SUBSTEPS, short(own_west_ref, 0, count), value)
     out_ref[...] = value
-    south, north = paired(value, rows, low)
+    free = open_rows(rows, cols)[:rows]
+    packs = count // 3
+    south, north = halo_messages(value[:packs], value[packs : 2 * packs] * free, value[2 * packs :])
     south_ref[...] = tall(south)
     north_ref[...] = tall(north)
 
 
 def strips_of(own_west, own_east, from_east, from_west):
     count, height, cols = own_west.shape
-    half = jax.ShapeDtypeStruct((count // 2, height, cols), BF16)
+    half = jax.ShapeDtypeStruct((count // 3, height, cols), BF16)
     return pl.pallas_call(
         strips_kernel,
         out_shape=(jax.ShapeDtypeStruct((2 * count, height // 2, cols), F32), half, half),
@@ -155,31 +149,41 @@
     return jnp.where((row >= 0) & (row < last), 1.0, 0.0).astype(F32)
 
 
-def substeps(zonal, merid, press, free):
-    rows, cols = zonal.shape[-2:]
+def substeps(zonal, merid, press, from_north, from_south, free):
+    rows, cols = zonal.shape[1:]
+    place = iota((rows, cols), 0)
+    low = place < rows // 2
+    merid = merid * free[:rows]
+    above = pltpu.roll(merid, 1, 1)
+    south_free = pltpu.roll(free[rows:], 1, 0)
+    spread = zonal - pltpu.roll(zonal, 1, 2) + merid
+    spread = spread - jnp.where(place == 0, from_south * south_free, above)
+    side = pltpu.roll(jnp.where(low, from_south, from_north), rows // 2, 1)
+    side = jnp.where(place == 0, side - above, side)
+    spread = jnp.concatenate([spread, side], axis=1)
+    press = jnp.concatenate([press, jnp.where(low, from_north, from_south)], axis=1)
+    total = None
     for _ in range(SUBSTEPS):
-        zonal = zonal - SOUND_COURANT * (pltpu.roll(press, cols - 1, 2) - press)
-        merid = (merid - SOUND_COURANT * (pltpu.roll(press, rows - 1, 1) - press)) * free
-        press = press - SOUND_COURANT * (
-            zonal - pltpu.roll(zonal, 1, 2) + merid - pltpu.roll(merid, 1, 1)
-        )
-    return zonal, merid, press
+        total = press if total is None else total + press
+        east = pltpu.roll(press, cols - 1, 2) - press
+        north = (pltpu.roll(press, 2 * rows - 1, 1) - press) * free
+        bend = east - pltpu.roll(east, 1, 2) + north - pltpu.roll(north, 1, 1)
+        spread = spread - SOUND_COURANT * bend
+        press = press - SOUND_COURANT * spread
+    east = pltpu.roll(total, cols - 1, 2) - total
+    north = (pltpu.roll(total, 2 * rows - 1, 1) - total) * free
+    zonal = zonal - SOUND_COURANT * east[:, :rows]
+    merid = merid - SOUND_COURANT * north[:, :rows]
+    return zonal, merid, press[:, :rows]
 
 
 def inner_kernel(state_ref, from_north_ref, from_south_ref, out_ref):
     levels = state_ref.shape[1]
     rows, cols = state_ref.shape[2:]
-    low = iota((rows, cols), 0) < rows // 2
-    free = open_rows(rows, cols)
-    parts = []
-    for field in range(3):
-        at = pl.ds(field * (levels // 4), levels // 4)
-        north = from_north_ref[at].astype(F32).reshape(levels // 2, rows, cols)
-        south = from_south_ref[at].astype(F32).reshape(levels // 2, rows, cols)
-        side = halo_rows(north, south, low)
-        parts.append(jnp.concatenate([state_ref[field], side], axis=1))
-    for field, value in enumerate(substeps(*parts, free)):
-        out_ref[field] = value[:, :rows]
+    parts = [state_ref[field] for field in range(3)]
+    parts += [short(ref, 0, levels) for ref in (from_north_ref, from_south_ref)]
+    for field, value in enumerate(substeps(*parts, open_rows(rows, cols))):
+        out_ref[field] = value
 
 
 def inner(state, from_north, from_south):
@@ -311,15 +315,10 @@
     _, levels, rows, cols = inner_ref.shape
     per = cols // STRIP
     packs = levels // per
-    low = iota((rows, cols), 0) < rows // 2
-    free = open_rows(rows, cols)
-    parts = []
-    for field in range(3):
-        half = [short(ref, field * packs // 2, packs // 2) for ref in (north_ref, south_ref)]
-        here = here_ref[pl.ds(field * packs, packs)]
-        parts.append(jnp.concatenate([here, halo_rows(*half, low)], axis=1))
-    for field, value in enumerate(substeps(*parts, free)):
-        strips[field] = value[:, :rows]
+    parts = [here_ref[pl.ds(field * packs, packs)] for field in range(3)]
+    parts += [short(ref, 0, packs) for ref in (north_ref, south_ref)]
+    for field, value in enumerate(substeps(*parts, open_rows(rows, cols))):
+        strips[field] = value
     lane = iota((rows, cols), 1)
 
     def merge(step, carry):
@@ -504,7 +503,7 @@
     return jnp.take_along_axis(value, index, axis=1, mode="promise_in_bounds")
 
 
-def relay_kernel(base, span, offset_ref, own_ref, near_ref, out_ref):
+def relay_kernel(base, span, offset_ref, own_ref, near_ref, out_ref, column_ref):
     rows = own_ref.shape[1] // 2
     cols = own_ref.shape[2]
     pairs = own_ref.shape[0]
@@ -518,46 +517,52 @@
         own = own_ref[at].astype(F32).reshape(20, rows, cols)
         near = near_ref[at].astype(F32).reshape(20, rows, cols)
         out_ref[at] = tall(jnp.where(take_near, near, own))
+        source = jnp.where(blocks == 1, own, near)
         for level in range(20):
-            column = jnp.where(lane == step * 20 + level, along(near[level], edge), column)
+            column = jnp.where(lane == step * 20 + level, along(source[level], edge), column)
         return column
 
     steps = pairs // 10
     column = lax.fori_loop(0, steps, body, jnp.zeros((rows, cols), F32), unroll=3)
     out_ref[pairs] = jnp.concatenate([column, column], axis=0).astype(BF16)
+    column_ref[...] = column
 
 
 def relay(offset, own, near, base, span):
     pairs, height, cols = own.shape
     return pl.pallas_call(
         functools.partial(relay_kernel, base, span),
-        out_shape=jax.ShapeDtypeStruct((pairs + 1, height, cols), BF16),
+        out_shape=(
+            jax.ShapeDtypeStruct((pairs + 1, height, cols), BF16),
+            jax.ShapeDtypeStruct((height // 2, cols), F32),
+        ),
         in_specs=[pl.BlockSpec(memory_space=pltpu.SMEM), vmem(), vmem()],
-        out_specs=vmem(),
+        out_specs=(vmem(), vmem()),
         compiler_params=params(8),
         cost_estimate=cost(1 << 20, 1 << 20),
     )(offset, own, near)
 
 
-def blend(offset_ref, shape, base, span):
+def blend(offset_ref, far_ref, column_ref, shape, base, span):
     rows, cols = shape
     blocks, cells = spread_offsets(offset_ref, shape, base, span)
     lane = iota((rows, cols), 1)
     from_right = lane <= cols - 1 - cells
     index = (lane - cells) & (cols - 1)
-    edge_index = cols - 1 - cells
-    is_zero, is_one, is_two = blocks == 0, blocks == 1, blocks >= 2
-
-    def tiles(own, near, far, column, stay, come, first):
+    is_zero, is_one = blocks == 0, blocks == 1
+    sent = far_ref[far_ref.shape[0] - 1].astype(F32)[:rows]
+    column = jnp.where(is_zero, column_ref[...], sent)
+
+    def tiles(own, near, far, stay, come, first):
         right = jnp.where(is_zero, own, jnp.where(is_one, near, far))
         left = jnp.where(is_zero, near, far)
         merged = jnp.where(from_right, right, left)
-        edges = jnp.where(is_two, column, left)
+        turned = pltpu.roll(column, lax.rem(cols - first, cols), 1)
         values = []
         for tile in range(own.shape[0]):
-            which = jnp.where(is_two, first + tile, edge_index)
             here = along(merged[tile], index)
-            behind = jnp.where(lane == 0, along(edges[tile], which), pltpu.roll(here, 1, 1))
+            edge = pltpu.roll(turned, back(tile, cols), 1)
+            behind = jnp.where(lane == 0, edge, pltpu.roll(here, 1, 1))
             values.append(stay[tile] * here + come[tile] * behind)
         return values
 
@@ -569,23 +574,17 @@
     return [ref[at].astype(F32).reshape((group,) + shape) for ref in refs]
 
 
-def last_column(far_ref, pairs, rows):
-    return far_ref[pairs].astype(F32)[:rows]
-
-
 def advect_ozone_kernel(
-    first, offset_ref, own_ref, near_ref, far_ref, stay_ref, come_ref, whole_ref, out_ref, result, sem
+    first, offset_ref, own_ref, near_ref, far_ref, column_ref, stay_ref, come_ref, whole_ref, out_ref, result, sem
 ):
     levels, rows, cols = stay_ref.shape
     group = levels // 2
-    tiles = blend(offset_ref, (rows, cols), 0, rows)
-    column = last_column(far_ref, own_ref.shape[0], rows)
+    tiles = blend(offset_ref, far_ref, column_ref, (rows, cols), 0, rows)
     copies = []
     for step in range(2):
         share = pl.ds(step * group, group)
         values = tiles(
             *read_tiles((own_ref, near_ref, far_ref), step, group, (rows, cols)),
-            column,
             stay_ref[share],
             come_ref[share],
             step * group,
@@ -601,30 +600,28 @@
         copy.wait()
 
 
-def advect_ozone(first, offset, own, near, far, stay, come, whole):
+def advect_ozone(first, offset, own, near, far, column, stay, come, whole):
     levels, rows, cols = stay.shape
     return pl.pallas_call(
         functools.partial(advect_ozone_kernel, first),
         out_shape=jax.ShapeDtypeStruct(whole.shape, F32),
-        in_specs=[pl.BlockSpec(memory_space=pltpu.SMEM)] + [vmem()] * 5 + [any_space()],
+        in_specs=[pl.BlockSpec(memory_space=pltpu.SMEM)] + [vmem()] * 6 + [any_space()],
         out_specs=any_space(),
         scratch_shapes=[pltpu.VMEM((levels, rows, cols), F32), pltpu.SemaphoreType.DMA((2,))],
-        input_output_aliases={6: 0},
+        input_output_aliases={7: 0},
         compiler_params=params(8),
         cost_estimate=cost(1 << 22, 2 << 20),
-    )(offset, own, near, far, stay, come, whole)
-
-
-def advect_south_kernel(offset_ref, own_ref, near_ref, far_ref, stay_ref, come_ref, out_ref):
+    )(offset, own, near, far, column, stay, come, whole)
+
+
+def advect_south_kernel(offset_ref, own_ref, near_ref, far_ref, column_ref, stay_ref, come_ref, out_ref):
     group, rows, cols = stay_ref.shape
     pairs = own_ref.shape[0]
-    tiles = blend(offset_ref, (rows, cols), 0, rows // 2)
-    column = last_column(far_ref, pairs, rows)
+    tiles = blend(offset_ref, far_ref, column_ref, (rows, cols), 0, rows // 2)
 
     def body(step, carry):
         values = tiles(
             *read_tiles((own_ref, near_ref, far_ref), step, group, (rows, cols)),
-            column,
             stay_ref[...],
             come_ref[...],
             step * group,
@@ -636,26 +633,25 @@
     lax.fori_loop(0, 2 * pairs // group, body, 0)
 
 
-def advect_south(offset, own, near, far, stay, come):
+def advect_south(offset, own, near, far, column, stay, come):
     pairs, height, cols = own.shape
     return pl.pallas_call(
         advect_south_kernel,
         out_shape=jax.ShapeDtypeStruct((2 * pairs, height // 2, cols), F32),
-        in_specs=[pl.BlockSpec(memory_space=pltpu.SMEM)] + [vmem()] * 5,
+        in_specs=[pl.BlockSpec(memory_space=pltpu.SMEM)] + [vmem()] * 6,
         out_specs=vmem(),
         compiler_params=params(8),
         cost_estimate=cost(1 << 22, 2 << 20),
-    )(offset, own, near, far, stay, come)
+    )(offset, own, near, far, column, stay, come)
 
 
 def advect_north_kernel(
-    first, offset_ref, own_ref, near_ref, far_ref, stay_ref, come_ref, south_ref, whole_ref, out_ref,
+    first, offset_ref, own_ref, near_ref, far_ref, column_ref, stay_ref, come_ref, south_ref, whole_ref, out_ref,
     result, sem,
 ):
     group, rows, cols = stay_ref.shape
     pairs = own_ref.shape[0]
-    tiles = blend(offset_ref, (rows, cols), rows // 2, rows // 2)
-    column = last_column(far_ref, pairs, rows)
+    tiles = blend(offset_ref, far_ref, column_ref, (rows, cols), rows // 2, rows // 2)
     low = iota((rows, cols), 0) < rows // 2
     count = 2 * pairs // group
 
@@ -670,7 +666,6 @@
     def body(step, carry):
         values = tiles(
             *read_tiles((own_ref, near_ref, far_ref), step, group, (rows, cols)),
-            column,
             stay_ref[...],
             come_ref[...],
             step * group,
@@ -688,22 +683,22 @@
         copy_of(step).wait()
 
 
-def advect_north(first, offset, own, near, far, stay, come, south, whole):
+def advect_north(first, offset, own, near, far, column, stay, come, south, whole):
     pairs, height, cols = own.shape
     count = 2 * pairs // stay.shape[0]
     return pl.pallas_call(
         functools.partial(advect_north_kernel, first),
         out_shape=jax.ShapeDtypeStruct(whole.shape, F32),
-        in_specs=[pl.BlockSpec(memory_space=pltpu.SMEM)] + [vmem()] * 6 + [any_space()],
+        in_specs=[pl.BlockSpec(memory_space=pltpu.SMEM)] + [vmem()] * 7 + [any_space()],
         out_specs=any_space(),
         scratch_shapes=[
             pltpu.VMEM((4 * pairs, height // 2, cols), F32),
             pltpu.SemaphoreType.DMA((count,)),
         ],
-        input_output_aliases={7: 0},
+        input_output_aliases={8: 0},
         compiler_params=params(16),
         cost_estimate=cost(1 << 22, 4 << 20),
-    )(offset, own, near, far, stay, come, south, whole)
+    )(offset, own, near, far, column, stay, come, south, whole)
 
 
 def shifted(value, axis, steps):
@@ -754,7 +749,7 @@
     five_winds = jnp.concatenate([five[: 2 * levels], five[6 * levels :]], axis=0)
 
     inner_out = inner(start_winds, from_north, from_south)
-    ozone_relay = relay(row_offset, ozone, ozone_near, 0, rows)
+    ozone_relay, ozone_column = relay(row_offset, ozone, ozone_near, 0, rows)
     ozone_far = shifted(ozone_relay, "lon", 2)
     winds, upwind, features, hidden_south, first = network(
         inner_out,
@@ -768,17 +763,19 @@
     first_near = shifted(first, "lon", 1)
     hidden_north, other = second(3 * levels, features, layers, five_tracers, lit, flat)
     other_near = shifted(other, "lon", 1)
-    first_relay = relay(row_offset, first, first_near, 0, rows // 2)
+    first_relay, first_column = relay(row_offset, first, first_near, 0, rows // 2)
     first_far = shifted(first_relay, "lon", 2)
-    other_relay = relay(row_offset, other, other_near, rows // 2, rows // 2)
+    other_relay, other_column = relay(row_offset, other, other_near, rows // 2, rows // 2)
     other_far = shifted(other_relay, "lon", 2)
     whole, flux, stay, come, stay_south, come_south, stay_north, come_north = winds_out(
         hidden_south, hidden_north, five_winds, lit, winds, upwind, fields
     )
-    whole = advect_ozone(fields - 1, row_offset, ozone, ozone_near, ozone_far, stay, come, whole)
-    south = advect_south(row_offset, first, first_near, first_far, stay_south, come_south)
+    whole = advect_ozone(
+        fields - 1, row_offset, ozone, ozone_near, ozone_far, ozone_column, stay, come, whole
+    )
+    south = advect_south(row_offset, first, first_near, first_far, first_column, stay_south, come_south)
     whole = advect_north(
-        3, row_offset, other, other_near, other_far, stay_north, come_north, south, whole
+        3, row_offset, other, other_near, other_far, other_column, stay_north, come_north, south, whole
     )
     return whole.reshape(fields, levels, rows, cols), flux
 

time: 57.3 us -> 56.7 us (0.990)
  no operation moved by 1% of the time
where the time goes in v6:
time: 56.7 us; the launch traced here: 56.5 us
  waiting for transfers between devices  25.4 us (45%)
  Pallas kernels  19 us (34%)
  starting transfers between devices  9.79 us (17%)
  local copies, waits for them, and re-layouts  1.42 us (3%)
  between operations  0.91 us (2%)
    ppermute x12, waiting for transfers between devices, shifted(): lax.ppermute(value, axis, [(i, (i + steps) % count) for i in range(count)])  25.4 us
    ppermute x12, starting transfers between devices, shifted(): lax.ppermute(value, axis, [(i, (i + steps) % count) for i in range(count)])  9.79 us
    pallas_call x1, Pallas kernels, network(): pl.pallas_call(network_kernel, out_shape=(jax.ShapeDtypeStruct((3 * level...  3.97 us
    pallas_call x1, Pallas kernels, second(): pl.pallas_call(functools.partial(second_kernel, first), out_shape=(jax.Sh...  2.94 us
    pallas_call x3, Pallas kernels, relay(): pl.pallas_call(functools.partial(relay_kernel, base, span), out_shape=(ja...  2.24 us
    pallas_call x1, Pallas kernels, winds_out(): pl.pallas_call(winds_kernel, out_shape=(jax.ShapeDtypeStruct((fields * le...  2.22 us
    pallas_call x1, Pallas kernels, advect_north(): pl.pallas_call(functools.partial(advect_north_kernel, first), out_shape=j...  2.15 us
    pallas_call x1, Pallas kernels, advect_ozone(): pl.pallas_call(functools.partial(advect_ozone_kernel, first), out_shape=j...  1.53 us
  transfers between devices with their start and end apart: 12, of which 7 were waited for; matrix products, arithmetic and copies ran while one was open for 0% of the time, Pallas kernels for 22%

profile of v6, /device:TPU:0, one launch (start us, length us, event | category | flops | bytes accessed | tf_op | source)
XLA Modules:
  0.0 56.5 jit_solution(114361985828527881)
XLA Ops:
  0.6 0.0 copy-start
  0.6 0.0 copy-start.8
  0.7 0.0 copy-start.3
  0.7 0.0 copy-start.1
  0.7 1.3 %slice.12.winds_ref.state_ref = f32[3,60,8,128]{3,2,1,0:T(8,128)S(1)} slice(f32[8,60,8,128]{3,2,1,0:T(8,128)} %state_ref.1), slice={[0:3], [0:60], [0:8], [0:128]} | slice | bytes 1474560 | tf_op jit(solution)/shard_map/slice | solution.py:735
  2.0 0.3 shard_map.104
  2.3 4.0 %collective-permute-start = (bf16[30,16,128]{2,1,0:T(8,128)(2,1)S(1)}, bf16[30,16,128]{2,1,0:T(8,128)(2,1)S(1)}, u32[]{:S(2)}, u32[]{:S(2)}) collective-permute-start(bf16[30,16,128]{2,1,0:T(8,128)(2,1)S(1)} %get-tuple-element.33), channel_id=1, source_target_pairs={{0,24},{8,0},{16,8},{24,16},{1,25},{9,1},{17,9},{25,17},{2,26},{10... | collective-permute-start | bytes 368648 | tf_op jit(solution)/shard_map/ppermute | solution.py:706
  6.3 0.0 collective-permute-start.1
  6.3 2.8 %collective-permute-start.2 = (bf16[18,16,128]{2,1,0:T(8,128)(2,1)S(1)}, bf16[18,16,128]{2,1,0:T(8,128)(2,1)S(1)}, u32[]{:S(2)}, u32[]{:S(2)}) collective-permute-start(bf16[18,16,128]{2,1,0:T(8,128)(2,1)S(1)} %get-tuple-element.35.own_west_ref), channel_id=1, source_target_pairs={{0,7},{1,0},{2,1},{3,2},{4,3},{5,4},{6,5},{7,6},{8,15},{9,8},{10,9... | collective-permute-start | bytes 221192 | tf_op jit(solution)/shard_map/ppermute | solution.py:706
  9.1 0.0 collective-permute-start.3
  9.1 2.0 %collective-permute-done.2.from_east_ref = bf16[18,16,128]{2,1,0:T(8,128)(2,1)S(1)} collective-permute-done((bf16[18,16,128]{2,1,0:T(8,128)(2,1)S(1)}, bf16[18,16,128]{2,1,0:T(8,128)(2,1)S(1)}, u32[]{:S(2)}, u32[]{:S(2)}) %collective-permute-start.2) | collective-permute-done | bytes 73760 | tf_op jit(solution)/shard_map/ppermute | solution.py:706
  11.1 3.6 %collective-permute-done.3.from_west_ref = bf16[18,16,128]{2,1,0:T(8,128)(2,1)S(1)} collective-permute-done((bf16[18,16,128]{2,1,0:T(8,128)(2,1)S(1)}, bf16[18,16,128]{2,1,0:T(8,128)(2,1)S(1)}, u32[]{:S(2)}, u32[]{:S(2)}) %collective-permute-start.3) | collective-permute-done | bytes 73760 | tf_op jit(solution)/shard_map/ppermute | solution.py:706
  14.7 0.1 shard_map.106
  14.8 2.7 %collective-permute-start.4 = (bf16[6,16,128]{2,1,0:T(8,128)(2,1)S(1)}, bf16[6,16,128]{2,1,0:T(8,128)(2,1)S(1)}, u32[]{:S(2)}, u32[]{:S(2)}) collective-permute-start(bf16[6,16,128]{2,1,0:T(8,128)(2,1)S(1)} %get-tuple-element.38), channel_id=1, source_target_pairs={{0,24},{8,0},{16,8},{24,16},{1,25},{9,1},{17,9},{25,17},{2,26},{10... | collective-permute-start | bytes 73736 | tf_op jit(solution)/shard_map/ppermute | solution.py:706
  17.5 0.0 collective-permute-start.5
  17.5 0.0 copy-start.4
  17.5 0.0 copy-start.5
  17.5 0.0 copy-start.6
  17.5 0.0 copy-start.7
  17.6 0.8 %shard_map.107 = (bf16[556,1024]{1,0:T(8,128)(2,1)S(1)}, f32[8,128]{1,0:T(8,128)S(1)}, bf16[30,16,128]{2,1,0:T(8,128)(2,1)S(1)}) custom-call(f32[8,60,8,128]{3,2,1,0:T(8,128)S(1)} %copy-done, bf16[76,8,128]{2,1,0:T(8,128)(2,1)S(1)} %copy-done.1, s32[1,1024]{1,0:T(1,128)S(1)} %bitcast.6), custom_call_target="tpu_custom_call" | custom-call | flops 16777216 | bytes 4194304 | tf_op jit(solution)/shard_map/pallas_call | solution.py:227
  18.4 0.0 collective-permute-done.from_north_ref
  18.4 0.0 collective-permute-done.1.from_south_ref
  18.4 1.4 %shard_map.105.inner_ref = f32[3,60,8,128]{3,2,1,0:T(8,128)S(1)} custom-call(f32[3,60,8,128]{3,2,1,0:T(8,128)S(1)} %slice.12.winds_ref.state_ref, bf16[30,16,128]{2,1,0:T(8,128)(2,1)S(1)} %collective-permute-done.from_north_ref, bf16[30,16,128]{2,1,0:T(8,128)(2,1)S(1)} %collective-permute-done.1.from_south_ref), custom_call_target="tpu_custom_call" | custom-call | flops 16777216 | bytes 4194304 | tf_op jit(solution)/shard_map/pallas_call | solution.py:191
  19.8 0.0 collective-permute-done.4.north_ref
  19.8 2.4 %collective-permute-done.5.south_ref = bf16[6,16,128]{2,1,0:T(8,128)(2,1)S(1)} collective-permute-done((bf16[6,16,128]{2,1,0:T(8,128)(2,1)S(1)}, bf16[6,16,128]{2,1,0:T(8,128)(2,1)S(1)}, u32[]{:S(2)}, u32[]{:S(2)}) %collective-permute-start.5) | collective-permute-done | bytes 24608 | tf_op jit(solution)/shard_map/ppermute | solution.py:706
  22.2 0.0 copy-done.7
  22.2 4.0 %shard_map.108 = (f32[1440,128]{1,0:T(8,128)S(1)}, f32[60,8,128]{2,1,0:T(8,128)S(1)}, bf16[556,1024]{1,0:T(8,128)(2,1)S(1)}, bf16[512,640]{1,0:T(8,128)(2,1)S(1)}, bf16[60,16,128]{2,1,0:T(8,128)(2,1)S(1)}) custom-call(f32[3,60,8,128]{3,2,1,0:T(8,128)S(1)} %shard_map.105.inner_ref, f32[36,8,128]{2,1,0:T(8,128)S(1)} %get-tuple-element.37.here_ref, ...), custom_call_target="tpu_custom_call" | custom-call | flops 3221225472 | bytes 8388608 | tf_op jit(solution)/shard_map/pallas_call | solution.py:363
  26.2 0.1 collective-permute-start.8
  26.2 0.0 copy-start.2
  26.3 2.9 %shard_map.109 = (bf16[512,640]{1,0:T(8,128)(2,1)S(1)}, bf16[60,16,128]{2,1,0:T(8,128)(2,1)S(1)}) custom-call(bf16[556,1024]{1,0:T(8,128)(2,1)S(1)} %get-tuple-element.42.features_ref, bf16[556,768]{1,0:T(8,128)(2,1)S(1)} %copy-done.5, bf16[768,640]{1,0:T(8,128)(2,1)S(1)} %copy-done.4, bf16[640,512]{1,0:T(8,128)(2,1)S(1)} %copy-done.6, ...), custom_call_target="tpu_custom_call" | custom-call | flops 2147483648 | bytes 6291456 | tf_op jit(solution)/shard_map/pallas_call | solution.py:396
  29.2 0.1 collective-permute-start.6
  29.3 0.1 collective-permute-start.10
  29.3 4.3 %collective-permute-done.8.near_ref = bf16[60,16,128]{2,1,0:T(8,128)(2,1)S(1)} collective-permute-done((bf16[60,16,128]{2,1,0:T(8,128)(2,1)S(1)}, bf16[60,16,128]{2,1,0:T(8,128)(2,1)S(1)}, u32[]{:S(2)}, u32[]{:S(2)}) %collective-permute-start.8) | collective-permute-done | bytes 245792 | tf_op jit(solution)/shard_map/ppermute | solution.py:706
  33.7 0.8 %shard_map.112 = (bf16[61,16,128]{2,1,0:T(8,128)(2,1)S(1)}, f32[8,128]{1,0:T(8,128)S(1)}) custom-call(s32[8]{0:T(128)S(1)} %copy-done.2, bf16[60,16,128]{2,1,0:T(8,128)(2,1)S(1)} %get-tuple-element.52.own_ref, bf16[60,16,128]{2,1,0:T(8,128)(2,1)S(1)} %collective-permute-done.8.near_ref), custom_call_target="tpu_custom_call" | custom-call | flops 1048576 | bytes 1048576 | tf_op jit(solution)/shard_map/pallas_call | solution.py:533
  34.4 0.1 collective-permute-start.9
  34.5 2.2 %collective-permute-done.6.near_ref = bf16[60,16,128]{2,1,0:T(8,128)(2,1)S(1)} collective-permute-done((bf16[60,16,128]{2,1,0:T(8,128)(2,1)S(1)}, bf16[60,16,128]{2,1,0:T(8,128)(2,1)S(1)}, u32[]{:S(2)}, u32[]{:S(2)}) %collective-permute-start.6) | collective-permute-done | bytes 245792 | tf_op jit(solution)/shard_map/ppermute | solution.py:706
  36.7 0.8 %shard_map.110 = (bf16[61,16,128]{2,1,0:T(8,128)(2,1)S(1)}, f32[8,128]{1,0:T(8,128)S(1)}) custom-call(s32[8]{0:T(128)S(1)} %copy-done.2, bf16[60,16,128]{2,1,0:T(8,128)(2,1)S(1)} %get-tuple-element.43.own_ref, bf16[60,16,128]{2,1,0:T(8,128)(2,1)S(1)} %collective-permute-done.6.near_ref), custom_call_target="tpu_custom_call" | custom-call | flops 1048576 | bytes 1048576 | tf_op jit(solution)/shard_map/pallas_call | solution.py:533
  37.5 0.1 collective-permute-start.7
  37.6 0.4 collective-permute-done.10.near_ref
  38.0 0.7 %shard_map.114 = (bf16[31,16,128]{2,1,0:T(8,128)(2,1)S(1)}, f32[8,128]{1,0:T(8,128)S(1)}) custom-call(s32[8]{0:T(128)S(1)} %copy-done.2, bf16[30,16,128]{2,1,0:T(8,128)(2,1)S(1)} %get-tuple-element.57.own_ref, bf16[30,16,128]{2,1,0:T(8,128)(2,1)S(1)} %collective-permute-done.10.near_ref), custom_call_target="tpu_custom_call" | custom-call | flops 1048576 | bytes 1048576 | tf_op jit(solution)/shard_map/pallas_call | solution.py:533
  38.7 0.1 collective-permute-start.11
  38.8 2.2 %shard_map.111 = (f32[480,8,128]{2,1,0:T(8,128)}, bf16[8,8,128]{2,1,0:T(8,128)(2,1)}, f32[60,8,128]{2,1,0:T(8,128)S(1)}, f32[60,8,128]{2,1,0:T(8,128)S(1)}, f32[...) custom-call(bf16[512,640]{1,0:T(8,128)(2,1)S(1)} %get-tuple-element.46, ...), custom_call_target="tpu_custom_call" | custom-call | flops 268435456 | bytes 4194304 | tf_op jit(solution)/shard_map/pallas_call | solution.py:469
  41.0 10.4 %collective-permute-done.11.far_ref = bf16[31,16,128]{2,1,0:T(8,128)(2,1)S(1)} collective-permute-done((bf16[31,16,128]{2,1,0:T(8,128)(2,1)S(1)}, bf16[31,16,128]{2,1,0:T(8,128)(2,1)S(1)}, u32[]{:S(2)}, u32[]{:S(2)}) %collective-permute-start.11) | collective-permute-done | bytes 127008 | tf_op jit(solution)/shard_map/ppermute | solution.py:706
  51.4 1.5 %shard_map.115.whole_ref = f32[480,8,128]{2,1,0:T(8,128)} custom-call(s32[8]{0:T(128)S(1)} %copy-done.2, bf16[30,16,128]{2,1,0:T(8,128)(2,1)S(1)} %get-tuple-element.57.own_ref, bf16[30,16,128]{2,1,0:T(8,128)(2,1)S(1)} %collective-permute-done.10.near_ref, bf16[31,16,128]{2,1,0:T(8,128)(2,1)S(1)} %collective-permute-done.11.far_ref, ...), custom_call_target="tpu_custom_call", output_to_operand_aliasing={{}: (7, {})} | custom-call | flops 4194304 | bytes 2097152 | tf_op jit(solution)/shard_map/pallas_call | solution.py:605
  53.0 0.0 collective-permute-done.9.far_ref
  53.0 1.4 %shard_map.113.south_ref = f32[120,8,128]{2,1,0:T(8,128)S(1)} custom-call(s32[8]{0:T(128)S(1)} %copy-done.2, bf16[60,16,128]{2,1,0:T(8,128)(2,1)S(1)} %get-tuple-element.52.own_ref, bf16[60,16,128]{2,1,0:T(8,128)(2,1)S(1)} %collective-permute-done.8.near_ref, bf16[61,16,128]{2,1,0:T(8,128)(2,1)S(1)} %collective-permute-done.9.far_ref, ...), custom_call_target="tpu_custom_call" | custom-call | flops 4194304 | bytes 2097152 | tf_op jit(solution)/shard_map/pallas_call | solution.py:638
  54.4 0.0 collective-permute-done.7.far_ref
  54.4 2.1 %shard_map.116 = f32[480,8,128]{2,1,0:T(8,128)} custom-call(s32[8]{0:T(128)S(1)} %copy-done.2, bf16[60,16,128]{2,1,0:T(8,128)(2,1)S(1)} %get-tuple-element.43.own_ref, bf16[60,16,128]{2,1,0:T(8,128)(2,1)S(1)} %collective-permute-done.6.near_ref, bf16[61,16,128]{2,1,0:T(8,128)(2,1)S(1)} %collective-permute-done.7.far_ref, ...), custom_call_target="tpu_custom_call", output_to_operand_aliasing={{}: (8, {})} | custom-call | flops 4194304 | bytes 4194304 | tf_op jit(solution)/shard_map/pallas_call | solution.py:689
  (12 shorter events, 0.1 us)
Async XLA Ops:
  0.6 16.9 %copy-start = (f32[8,60,8,128]{3,2,1,0:T(8,128)S(1)}, f32[8,60,8,128]{3,2,1,0:T(8,128)}, u32[]{:S(2)}) copy-start(f32[8,60,8,128]{3,2,1,0:T(8,128)} %state_ref.1) | copy-start | bytes 5898244
  0.6 16.8 %copy-start.8 = (bf16[640,368]{0,1:T(8,128)(2,1)S(1)}, bf16[640,368]{0,1:T(8,128)(2,1)}, u32[]{:S(2)}) copy-start(bf16[640,368]{0,1:T(8,128)(2,1)} %param.15) | copy-start | bytes 1413124
  0.7 16.9 %copy-start.3 = (s32[1,1,1024]{2,1,0:T(1,128)S(1)}, s32[1,1,1024]{2,1,0:T(1,128)}, u32[]{:S(2)}) copy-start(s32[1,1,1024]{2,1,0:T(1,128)} %param.16) | copy-start | bytes 12292
  0.7 16.9 %copy-start.1 = (bf16[76,8,128]{2,1,0:T(8,128)(2,1)S(1)}, bf16[76,8,128]{2,1,0:T(8,128)(2,1)}, u32[]{:S(2)}) copy-start(bf16[76,8,128]{2,1,0:T(8,128)(2,1)} %surface_ref.1) | copy-start | bytes 466948
  2.3 16.0 %collective-permute-start = (bf16[30,16,128]{2,1,0:T(8,128)(2,1)S(1)}, bf16[30,16,128]{2,1,0:T(8,128)(2,1)S(1)}, u32[]{:S(2)}, u32[]{:S(2)}) collective-permute-start(bf16[30,16,128]{2,1,0:T(8,128)(2,1)S(1)} %get-tuple-element.33), channel_id=1, source_target_pairs={{0,24},{8,0},{16,8},{24,16},{1,25},{9,1},{17,9},{25,17},{2,26},{10... | collective-permute-start | bytes 368648 | tf_op jit(solution)/shard_map/ppermute | solution.py:706
  6.3 12.1 %collective-permute-start.1 = (bf16[30,16,128]{2,1,0:T(8,128)(2,1)S(1)}, bf16[30,16,128]{2,1,0:T(8,128)(2,1)S(1)}, u32[]{:S(2)}, u32[]{:S(2)}) collective-permute-start(bf16[30,16,128]{2,1,0:T(8,128)(2,1)S(1)} %get-tuple-element.34), channel_id=1, source_target_pairs={{0,8},{8,16},{16,24},{24,0},{1,9},{9,17},{17,25},{25,1},{2,10},{10... | collective-permute-start | bytes 368648 | tf_op jit(solution)/shard_map/ppermute | solution.py:706
  6.3 4.7 %collective-permute-start.2 = (bf16[18,16,128]{2,1,0:T(8,128)(2,1)S(1)}, bf16[18,16,128]{2,1,0:T(8,128)(2,1)S(1)}, u32[]{:S(2)}, u32[]{:S(2)}) collective-permute-start(bf16[18,16,128]{2,1,0:T(8,128)(2,1)S(1)} %get-tuple-element.35.own_west_ref), channel_id=1, source_target_pairs={{0,7},{1,0},{2,1},{3,2},{4,3},{5,4},{6,5},{7,6},{8,15},{9,8},{10,9... | collective-permute-start | bytes 221192 | tf_op jit(solution)/shard_map/ppermute | solution.py:706
  9.1 5.6 %collective-permute-start.3 = (bf16[18,16,128]{2,1,0:T(8,128)(2,1)S(1)}, bf16[18,16,128]{2,1,0:T(8,128)(2,1)S(1)}, u32[]{:S(2)}, u32[]{:S(2)}) collective-permute-start(bf16[18,16,128]{2,1,0:T(8,128)(2,1)S(1)} %get-tuple-element.36.own_east_ref), channel_id=1, source_target_pairs={{0,1},{1,2},{2,3},{3,4},{4,5},{5,6},{6,7},{7,0},{8,9},{9,10},{10,1... | collective-permute-start | bytes 221192 | tf_op jit(solution)/shard_map/ppermute | solution.py:706
  14.8 5.0 %collective-permute-start.4 = (bf16[6,16,128]{2,1,0:T(8,128)(2,1)S(1)}, bf16[6,16,128]{2,1,0:T(8,128)(2,1)S(1)}, u32[]{:S(2)}, u32[]{:S(2)}) collective-permute-start(bf16[6,16,128]{2,1,0:T(8,128)(2,1)S(1)} %get-tuple-element.38), channel_id=1, source_target_pairs={{0,24},{8,0},{16,8},{24,16},{1,25},{9,1},{17,9},{25,17},{2,26},{10... | collective-permute-start | bytes 73736 | tf_op jit(solution)/shard_map/ppermute | solution.py:706
  17.5 4.7 %collective-permute-start.5 = (bf16[6,16,128]{2,1,0:T(8,128)(2,1)S(1)}, bf16[6,16,128]{2,1,0:T(8,128)(2,1)S(1)}, u32[]{:S(2)}, u32[]{:S(2)}) collective-permute-start(bf16[6,16,128]{2,1,0:T(8,128)(2,1)S(1)} %get-tuple-element.39), channel_id=1, source_target_pairs={{0,8},{8,16},{16,24},{24,0},{1,9},{9,17},{17,25},{25,1},{2,10},{10... | collective-permute-start | bytes 73736 | tf_op jit(solution)/shard_map/ppermute | solution.py:706
  17.5 4.7 %copy-start.4 = (bf16[768,640]{1,0:T(8,128)(2,1)S(1)}, bf16[768,640]{1,0:T(8,128)(2,1)}, u32[]{:S(2)}) copy-start(bf16[768,640]{1,0:T(8,128)(2,1)} %two_ref.3) | copy-start | bytes 2949124
  17.5 4.7 %copy-start.5 = (bf16[556,768]{1,0:T(8,128)(2,1)S(1)}, bf16[556,768]{1,0:T(8,128)(2,1)}, u32[]{:S(2)}) copy-start(bf16[556,768]{1,0:T(8,128)(2,1)} %one_ref.3) | copy-start | bytes 2562052
  17.5 4.7 %copy-start.6 = (bf16[640,512]{1,0:T(8,128)(2,1)S(1)}, bf16[640,512]{1,0:T(8,128)(2,1)}, u32[]{:S(2)}) copy-start(bf16[640,512]{1,0:T(8,128)(2,1)} %three_ref.3) | copy-start | bytes 1966084
  17.5 4.7 %copy-start.7 = (bf16[512,640]{1,0:T(8,128)(2,1)S(1)}, bf16[512,640]{1,0:T(8,128)(2,1)}, u32[]{:S(2)}) copy-start(bf16[512,640]{1,0:T(8,128)(2,1)} %four_ref.3) | copy-start | bytes 1966084
  26.2 7.5 %collective-permute-start.8 = (bf16[60,16,128]{2,1,0:T(8,128)(2,1)S(1)}, bf16[60,16,128]{2,1,0:T(8,128)(2,1)S(1)}, u32[]{:S(2)}, u32[]{:S(2)}) collective-permute-start(bf16[60,16,128]{2,1,0:T(8,128)(2,1)S(1)} %get-tuple-element.52.own_ref), channel_id=1, source_target_pairs={{0,1},{1,2},{2,3},{3,4},{4,5},{5,6},{6,7},{7,0},{8,9},{9,10},{10,1... | collective-permute-start | bytes 737288 | tf_op jit(solution)/shard_map/ppermute | solution.py:706
  26.2 7.4 %copy-start.2 = (s32[8]{0:T(128)S(1)}, s32[8]{0:T(128)}, u32[]{:S(2)}) copy-start(s32[8]{0:T(128)} %offset_ref.11) | copy-start | bytes 100
  29.2 7.5 %collective-permute-start.6 = (bf16[60,16,128]{2,1,0:T(8,128)(2,1)S(1)}, bf16[60,16,128]{2,1,0:T(8,128)(2,1)S(1)}, u32[]{:S(2)}, u32[]{:S(2)}) collective-permute-start(bf16[60,16,128]{2,1,0:T(8,128)(2,1)S(1)} %get-tuple-element.43.own_ref), channel_id=1, source_target_pairs={{0,1},{1,2},{2,3},{3,4},{4,5},{5,6},{6,7},{7,0},{8,9},{9,10},{10,1... | collective-permute-start | bytes 737288 | tf_op jit(solution)/shard_map/ppermute | solution.py:706
  29.3 8.7 %collective-permute-start.10 = (bf16[30,16,128]{2,1,0:T(8,128)(2,1)S(1)}, bf16[30,16,128]{2,1,0:T(8,128)(2,1)S(1)}, u32[]{:S(2)}, u32[]{:S(2)}) collective-permute-start(bf16[30,16,128]{2,1,0:T(8,128)(2,1)S(1)} %get-tuple-element.57.own_ref), channel_id=1, source_target_pairs={{0,1},{1,2},{2,3},{3,4},{4,5},{5,6},{6,7},{7,0},{8,9},{9,10},{10,1... | collective-permute-start | bytes 368648 | tf_op jit(solution)/shard_map/ppermute | solution.py:706
  34.4 18.5 %collective-permute-start.9 = (bf16[61,16,128]{2,1,0:T(8,128)(2,1)S(1)}, bf16[61,16,128]{2,1,0:T(8,128)(2,1)S(1)}, u32[]{:S(2)}, u32[]{:S(2)}) collective-permute-start(bf16[61,16,128]{2,1,0:T(8,128)(2,1)S(1)} %get-tuple-element.53), channel_id=1, source_target_pairs={{0,2},{1,3},{2,4},{3,5},{4,6},{5,7},{6,0},{7,1},{8,10},{9,11},{10,... | collective-permute-start | bytes 749576 | tf_op jit(solution)/shard_map/ppermute | solution.py:706
  37.5 16.9 %collective-permute-start.7 = (bf16[61,16,128]{2,1,0:T(8,128)(2,1)S(1)}, bf16[61,16,128]{2,1,0:T(8,128)(2,1)S(1)}, u32[]{:S(2)}, u32[]{:S(2)}) collective-permute-start(bf16[61,16,128]{2,1,0:T(8,128)(2,1)S(1)} %get-tuple-element.44), channel_id=1, source_target_pairs={{0,2},{1,3},{2,4},{3,5},{4,6},{5,7},{6,0},{7,1},{8,10},{9,11},{10,... | collective-permute-start | bytes 749576 | tf_op jit(solution)/shard_map/ppermute | solution.py:706
  38.7 12.8 %collective-permute-start.11 = (bf16[31,16,128]{2,1,0:T(8,128)(2,1)S(1)}, bf16[31,16,128]{2,1,0:T(8,128)(2,1)S(1)}, u32[]{:S(2)}, u32[]{:S(2)}) collective-permute-start(bf16[31,16,128]{2,1,0:T(8,128)(2,1)S(1)} %get-tuple-element.58), channel_id=1, source_target_pairs={{0,2},{1,3},{2,4},{3,5},{4,6},{5,7},{6,0},{7,1},{8,10},{9,11},{10,... | collective-permute-start | bytes 380936 | tf_op jit(solution)/shard_map/ppermute | solution.py:706
